TPU v7x, 128 devices: a whole 4x4x4 slice. The times are simulated.
128 devices in a mesh: slab: 8 (over y, core), sub: 16 (over z, x).
Axes of the slice: x: 4, y: 4, z: 4, core: 2. Of those that a mesh axis runs over, the one named last changes fastest.
Arguments:
- positions: float32 [3, 8388608], P(None, ('slab', 'sub')), may hold values from 0 to 64, as said below
- masses: float32 [8388608], P(('slab', 'sub')), may hold values from 0.001 to 0.01
- leaf_counts: int32 [32768], P(('slab', 'sub')), may hold values from 64 to 256, as said below
- send_leaves: int32 [128, 256], P(('slab', 'sub')), may hold values from 0 to 255, as said below
- send_parents: int32 [128, 64], P(('slab', 'sub')), may hold values from 0 to 31, as said below
- near_pairs: int32 [128, 3, 256], P(('slab', 'sub')), may hold values from -1 to 511, as said below
- far_pairs: int32 [128, 3, 1024], P(('slab', 'sub')), may hold values from -1 to 511, as said below
- parent_pairs: int32 [128, 3, 64], P(('slab', 'sub')), may hold values from -1 to 95, as said below
Outputs:
- field: float32 [4, 8388608], P(None, ('slab', 'sub'))
Inputs may be any that keep to these rules, and one draw needn't show every extreme that they name: `positions`: the coordinates of a body of leaf c on device (s, u) lie within one unit above that leaf's integer coordinates along each dimension. `leaf_counts`: every device has a leaf whose 256 slots are all used. `send_leaves`: within one direction of a row, the 64 leaves are different. `send_parents`: within one direction of a row, the 16 parent cells are different. `near_pairs`: row 0 is an own leaf, row 1 a leaf table entry or -1 for an unused entry (unused entries come last), row 2 the z image -1, 0 or 1 (0 where unused). Own pairs have a < b; no pair repeats; pairs are leaves at most one leaf apart along each dimension after the image. `far_pairs`: as near_pairs, for leaves whose squared separation after the image is 4 to 12 leaf units. `parent_pairs`: as near_pairs, for parent cells whose squared separation after the image is 2 parent units or more, with the parent table.
All inputs are finite; a program needn't handle non-finite values.
Results may differ from a plain program's by a relative error of at most 0.0003.
Values sent between devices are 32-bit elements; how exact they have to be, the bound alone decides.
A program may use at most 320 MiB of HBM per device.

v0:
```python
import jax
import jax.numpy as jnp
from jax import lax
from jax.sharding import PartitionSpec as P

CX = 2
CY = 4
CZ = 32


tensor_offsets = (0, 1, 4, 13, 40, 121)
factorials = (1.0, 1.0, 2.0, 6.0, 24.0)
soft_square = 0.0025
slab_steps = (1, 0, 1, 1)
sub_steps = (0, 1, 1, -1)


def from_behind(value, axis, steps):
    count = lax.axis_size(axis)
    pairs = [(source, (source + steps) % count) for source in range(count)]
    return lax.ppermute(value, axis, pairs)


def outer_powers(offset):
    tail = offset.shape[1:]
    powers = [jnp.ones((1,) + tail, offset.dtype)]
    for degree in range(4):
        before = powers[-1]
        grown = before[:, None] * offset[None, :]
        powers.append(grown.reshape((before.shape[0] * 3,) + tail))
    return powers


def inverse_distance(vector):
    return 1.0 / jnp.sqrt(jnp.sum(vector * vector))


def jacobian_of(inner):

    def result(vector):
        values, pullback = jax.vjp(inner, vector)
        unit_rows = jnp.eye(values.shape[0], dtype=values.dtype)
        stacked = jax.vmap(pullback)(unit_rows)[0]
        return stacked.reshape(-1)

    return result


def derivative_tensors(separation):
    first_grad = jax.grad(inverse_distance)
    second_grad = jacobian_of(first_grad)
    third_grad = jacobian_of(second_grad)

    def single(vector):
        return (
            inverse_distance(vector).reshape(1),
            first_grad(vector),
            second_grad(vector),
            third_grad(vector),
            jacobian_of(third_grad)(vector),
        )

    return jax.vmap(single)(separation)


def mutual_locals(moments_a, moments_b, separation):
    tensors = derivative_tensors(separation)
    pair_count = separation.shape[0]
    locals_a = []
    locals_b = []
    for degree in range(5):
        summed_a = jnp.zeros((pair_count, 3**degree), jnp.float32)
        summed_b = jnp.zeros((pair_count, 3**degree), jnp.float32)
        for source in range(5 - degree):
            tensor_block = tensors[source + degree].reshape(pair_count, 3**source, 3**degree)
            piece_b = moments_b[:, tensor_offsets[source] : tensor_offsets[source + 1]]
            piece_a = moments_a[:, tensor_offsets[source] : tensor_offsets[source + 1]]
            summed_a = summed_a + (-1.0) ** source / factorials[source] * jnp.einsum(
                "pa,pab->pb", piece_b, tensor_block, precision=lax.Precision.HIGHEST
            )
            summed_b = summed_b + 1.0 / factorials[source] * jnp.einsum(
                "pa,pab->pb", piece_a, tensor_block, precision=lax.Precision.HIGHEST
            )
        locals_a.append(-summed_a)
        locals_b.append(-((-1.0) ** degree) * summed_b)
    return (jnp.concatenate(locals_a, 1), jnp.concatenate(locals_b, 1))


def shift_locals(parent_terms, offset):
    powers = outer_powers(offset)
    result = []
    for degree in range(5):
        summed = jnp.zeros((3**degree,) + offset.shape[1:], jnp.float32)
        for source in range(degree, 5):
            spacing = source - degree
            tensor_block = parent_terms[
                tensor_offsets[source] : tensor_offsets[source + 1]
            ].reshape((3**spacing, 3**degree) + offset.shape[1:])
            summed = (
                summed + jnp.sum(tensor_block * powers[spacing][:, None], 0) / factorials[spacing]
            )
        result.append(summed)
    return jnp.concatenate(result, 0)


def evaluate_locals(leaf_terms, powers):
    cell_count = leaf_terms.shape[1]
    potential = jnp.zeros(powers[0].shape[1:], jnp.float32)
    accel = jnp.zeros((3,) + powers[0].shape[1:], jnp.float32)
    for degree in range(5):
        tensor_block = leaf_terms[tensor_offsets[degree] : tensor_offsets[degree + 1]]
        potential = (
            potential + jnp.sum(tensor_block[:, :, None] * powers[degree], 0) / factorials[degree]
        )
        if degree < 4:
            upper = leaf_terms[tensor_offsets[degree + 1] : tensor_offsets[degree + 2]].reshape(
                3**degree, 3, cell_count
            )
            accel = (
                accel
                - jnp.sum(upper[:, :, :, None] * powers[degree][:, None], 0) / factorials[degree]
            )
    return jnp.concatenate([potential[None], accel], 0)


def pair_block(place_a, weight_a, place_b, weight_b):
    spacing = place_a[:, :, None] - place_b[:, None, :]
    inverse = lax.rsqrt(jnp.sum(spacing * spacing, 0) + soft_square)
    cubed = inverse * inverse * inverse
    potential_a = -jnp.sum(weight_b[None, :] * inverse, 1)
    potential_b = -jnp.sum(weight_a[:, None] * inverse, 0)
    accel_a = -jnp.sum(spacing * (weight_b[None, :] * cubed)[None], 2)
    accel_b = jnp.sum(spacing * (weight_a[:, None] * cubed)[None], 1)
    return (
        jnp.concatenate([potential_a[None], accel_a], 0),
        jnp.concatenate([potential_b[None], accel_b], 0),
    )


def self_block(places, weight_row):
    slot_count = weight_row.shape[0]
    spacing = places[:, :, None] - places[:, None, :]
    apart = lax.broadcasted_iota(jnp.int32, (slot_count, slot_count), 0) != lax.broadcasted_iota(
        jnp.int32, (slot_count, slot_count), 1
    )
    inverse = jnp.where(apart, lax.rsqrt(jnp.sum(spacing * spacing, 0) + soft_square), 0.0)
    cubed = inverse * inverse * inverse
    potential = -jnp.sum(weight_row[None, :] * inverse, 1)
    accel = -jnp.sum(spacing * (weight_row[None, :] * cubed)[None], 2)
    return jnp.concatenate([potential[None], accel], 0)


def self_work(body_rows):
    leaf_total = body_rows.shape[0]
    leaf_size = body_rows.shape[2]
    grouped = body_rows.reshape(leaf_total // 8, 8, 4, leaf_size)

    def self_one_group(bundle):
        return jax.vmap(self_block)(bundle[:, :3], bundle[:, 3])

    fields = lax.map(self_one_group, grouped)
    return fields.reshape(leaf_total, 4, leaf_size)


def near_work(table_bodies, pair_list):
    owned_ids = pair_list[0]
    partner_ids = jnp.maximum(pair_list[1], 0)
    active = pair_list[1] >= 0
    z_lift = pair_list[2].astype(jnp.float32) * CZ
    pair_count = owned_ids.shape[0]
    leaf_size = table_bodies.shape[2]

    def near_one_group(bundle):
        ids_a, ids_b, lifts, actives = bundle
        rows_a = jnp.take(table_bodies, ids_a, axis=0)
        rows_b = jnp.take(table_bodies, ids_b, axis=0)
        rows_b = rows_b.at[:, 2].add(lifts[:, None])
        part_a, part_b = jax.vmap(pair_block)(
            rows_a[:, :3], rows_a[:, 3], rows_b[:, :3], rows_b[:, 3]
        )
        keeper = actives[:, None, None]
        return (jnp.where(keeper, part_a, 0.0), jnp.where(keeper, part_b, 0.0))

    def shaped(values):
        return values.reshape(pair_count // 16, 16)

    part_a, part_b = lax.map(
        near_one_group, (shaped(owned_ids), shaped(partner_ids), shaped(z_lift), shaped(active))
    )
    part_a = part_a.reshape(pair_count, 4, leaf_size)
    part_b = part_b.reshape(pair_count, 4, leaf_size)
    summed = jnp.zeros(table_bodies.shape, jnp.float32)
    return summed.at[owned_ids].add(part_a).at[partner_ids].add(part_b)


def far_work(table_cells, pair_list):
    owned_ids = pair_list[0]
    partner_ids = jnp.maximum(pair_list[1], 0)
    active = pair_list[1] >= 0
    z_lift = pair_list[2].astype(jnp.float32) * CZ
    centre_a = jnp.take(table_cells[:, 121:], owned_ids, axis=0)
    centre_b = jnp.take(table_cells[:, 121:], partner_ids, axis=0)
    centre_b = centre_b.at[:, 2].add(z_lift)
    separation = jnp.where(active[:, None], centre_a - centre_b, 3.0)
    moments_a = jnp.take(table_cells[:, :121], owned_ids, axis=0)
    moments_b = jnp.take(table_cells[:, :121], partner_ids, axis=0)
    locals_a, locals_b = mutual_locals(moments_a, moments_b, separation)
    locals_a = jnp.where(active[:, None], locals_a, 0.0)
    locals_b = jnp.where(active[:, None], locals_b, 0.0)
    summed = jnp.zeros((table_cells.shape[0], 121), jnp.float32)
    return summed.at[owned_ids].add(locals_a).at[partner_ids].add(locals_b)


def geometry(slab_at, sub_at):
    leaf_ids = jnp.arange(CX * CY * CZ, dtype=jnp.int32)
    cell_x = leaf_ids // (CY * CZ)
    cell_y = leaf_ids // CZ % CY
    cell_z = leaf_ids % CZ
    base_x = slab_at * CX
    base_y = sub_at * CY
    centres = jnp.stack([base_x + cell_x, base_y + cell_y, cell_z]).astype(jnp.float32) + 0.5
    half_y = CY // 2
    half_z = CZ // 2
    parent_of = (cell_x // 2 * half_y + cell_y // 2) * half_z + cell_z // 2
    parent_ids = jnp.arange(CX // 2 * half_y * half_z, dtype=jnp.int32)
    parent_x = parent_ids // (half_y * half_z)
    parent_y = parent_ids // half_z % half_y
    parent_z = parent_ids % half_z
    parent_centres = (
        jnp.stack([base_x + 2 * parent_x, base_y + 2 * parent_y, 2 * parent_z]).astype(jnp.float32)
        + 1.0
    )
    return (centres, parent_centres, parent_of)


def image_shift(slab_at, sub_at, slab_count, sub_count):
    rows_out = []
    for direction in range(4):
        reach_x = slab_at + slab_steps[direction]
        reach_y = sub_at + sub_steps[direction]
        jump_x = (reach_x - reach_x % slab_count) * CX
        jump_y = (reach_y - reach_y % sub_count) * CY
        rows_out.append(jnp.stack([jump_x, jump_y, jnp.zeros_like(jump_x)]))
    return jnp.stack(rows_out).astype(jnp.float32)


def device_front(positions, masses, leaf_counts, send_leaves, send_parents, slab_at, sub_at):
    leaf_total = leaf_counts.shape[0]
    leaf_size = masses.shape[0] // leaf_total
    places = positions.reshape(3, leaf_total, leaf_size)
    filled = lax.broadcasted_iota(jnp.int32, (leaf_total, leaf_size), 1) < leaf_counts[:, None]
    weights = jnp.where(filled, masses.reshape(leaf_total, leaf_size), 0.0)
    centres, parent_centres, parent_of = geometry(slab_at, sub_at)
    parent_total = parent_centres.shape[1]
    leaf_powers = outer_powers(places - centres[:, :, None])
    moments = jnp.sum(jnp.concatenate(leaf_powers, 0) * weights[None], 2)
    parent_powers = jnp.concatenate(
        outer_powers(places - jnp.take(parent_centres, parent_of, axis=1)[:, :, None]), 0
    )
    per_leaf = jnp.sum(parent_powers * weights[None], 2)
    belongs = (parent_of[:, None] == jnp.arange(parent_total, dtype=jnp.int32)[None, :]).astype(
        jnp.float32
    )
    parent_moments = jnp.dot(per_leaf, belongs, precision=lax.Precision.HIGHEST)
    body_rows = jnp.concatenate([places, weights[None]], 0).transpose(1, 0, 2)
    leaf_rows = jnp.concatenate([moments, centres], 0).T
    parent_rows = jnp.concatenate([parent_moments, parent_centres], 0).T
    out_bodies = jnp.take(body_rows, send_leaves, axis=0).reshape(4, -1)
    out_leaf = jnp.take(leaf_rows, send_leaves, axis=0).reshape(4, -1)
    out_parent = jnp.take(parent_rows, send_parents, axis=0).reshape(4, -1)
    outgoing = jnp.concatenate([out_bodies, out_leaf, out_parent], 1)
    return (
        filled,
        leaf_powers,
        body_rows,
        leaf_rows,
        parent_rows,
        centres,
        parent_centres,
        parent_of,
        send_leaves,
        send_parents,
        outgoing,
    )


def device_middle(
    body_rows, leaf_rows, parent_rows, incoming, image, near_list, far_list, parent_list
):
    leaf_total = body_rows.shape[0]
    leaf_size = body_rows.shape[2]
    parent_total = parent_rows.shape[0]
    slots = leaf_total // 4
    parent_slots = parent_total // 2
    cut_a = 4 * slots * leaf_size
    cut_b = cut_a + 124 * slots
    body_lift = jnp.concatenate([image, jnp.zeros((4, 1), jnp.float32)], 1)
    cell_lift = jnp.concatenate([jnp.zeros((4, 121), jnp.float32), image], 1)
    in_bodies = incoming[:, :cut_a].reshape(4, slots, 4, leaf_size) + body_lift[:, None, :, None]
    in_leaf = incoming[:, cut_a:cut_b].reshape(4, slots, 124) + cell_lift[:, None, :]
    in_parent = incoming[:, cut_b:].reshape(4, parent_slots, 124) + cell_lift[:, None, :]
    table_bodies = jnp.concatenate([body_rows, in_bodies.reshape(4 * slots, 4, leaf_size)], 0)
    table_leaf = jnp.concatenate([leaf_rows, in_leaf.reshape(4 * slots, 124)], 0)
    table_parent = jnp.concatenate([parent_rows, in_parent.reshape(4 * parent_slots, 124)], 0)
    near_table = near_work(table_bodies, near_list)
    local_near = near_table[:leaf_total] + self_work(body_rows)
    leaf_table = far_work(table_leaf, far_list)
    parent_table = far_work(table_parent, parent_list)
    back_bodies = near_table[leaf_total:].reshape(4, -1)
    back_leaf = leaf_table[leaf_total:].reshape(4, -1)
    back_parent = parent_table[parent_total:].reshape(4, -1)
    returning = jnp.concatenate([back_bodies, back_leaf, back_parent], 1)
    return (returning, local_near, leaf_table[:leaf_total], parent_table[:parent_total])


def device_back(
    local_near,
    leaf_terms,
    parent_terms,
    arrived,
    flat_leaf,
    flat_parent,
    leaf_powers,
    centres,
    parent_centres,
    parent_of,
    filled,
):
    leaf_size = local_near.shape[2]
    slots = flat_leaf.shape[0] // 4
    cut_a = 4 * slots * leaf_size
    cut_b = cut_a + 121 * slots
    got_bodies = arrived[:, :cut_a].reshape(4 * slots, 4, leaf_size)
    got_leaf = arrived[:, cut_a:cut_b].reshape(4 * slots, 121)
    got_parent = arrived[:, cut_b:].reshape(-1, 121)
    local_near = local_near.at[flat_leaf].add(got_bodies)
    leaf_terms = leaf_terms.at[flat_leaf].add(got_leaf)
    parent_terms = parent_terms.at[flat_parent].add(got_parent)
    leaf_columns = leaf_terms.T + shift_locals(
        jnp.take(parent_terms, parent_of, axis=0).T,
        centres - jnp.take(parent_centres, parent_of, axis=1),
    )
    result = evaluate_locals(leaf_columns, leaf_powers) + local_near.transpose(1, 0, 2)
    result = jnp.where(filled[None], result, 0.0)
    return result.reshape(4, -1)


def on_device(
    positions, masses, leaf_counts, send_leaves, send_parents, near_pairs, far_pairs, parent_pairs
):
    slab_count = lax.axis_size("slab")
    sub_count = lax.axis_size("sub")
    slab_at = lax.axis_index("slab")
    sub_at = lax.axis_index("sub")
    parts = device_front(
        positions, masses, leaf_counts, send_leaves[0], send_parents[0], slab_at, sub_at
    )
    outgoing = parts[10]
    image = image_shift(slab_at, sub_at, slab_count, sub_count)
    slab_moved = from_behind(jnp.stack([outgoing[0], outgoing[2], outgoing[3]]), "slab", -1)
    rising = from_behind(jnp.stack([outgoing[1], slab_moved[1]]), "sub", -1)
    falling = from_behind(slab_moved[2], "sub", 1)
    incoming = jnp.stack([slab_moved[0], rising[0], rising[1], falling])
    returning, local_near, leaf_terms, parent_terms = device_middle(
        parts[2], parts[3], parts[4], incoming, image, near_pairs[0], far_pairs[0], parent_pairs[0]
    )
    back_rise = from_behind(jnp.stack([returning[1], returning[2]]), "sub", 1)
    back_fall = from_behind(returning[3], "sub", -1)
    back_slab = from_behind(jnp.stack([returning[0], back_rise[1], back_fall]), "slab", 1)
    arrived = jnp.stack([back_slab[0], back_rise[0], back_slab[1], back_slab[2]])
    return device_back(
        local_near,
        leaf_terms,
        parent_terms,
        arrived,
        parts[8],
        parts[9],
        parts[1],
        parts[5],
        parts[6],
        parts[7],
        parts[0],
    )


def solution(mesh):
    return jax.shard_map(
        on_device,
        mesh=mesh,
        in_specs=(
            P(None, ("slab", "sub")),
            P(("slab", "sub")),
            P(("slab", "sub")),
            P(("slab", "sub"), None),
            P(("slab", "sub"), None),
            P(("slab", "sub"), None, None),
            P(("slab", "sub"), None, None),
            P(("slab", "sub"), None, None),
        ),
        out_specs=P(None, ("slab", "sub")),
        check_vma=False,
    )
```

profile of v0, /device:TPU:1, one launch (start us, length us, event | category | flops | bytes accessed | tf_op | source)
XLA Modules:
  0.0 844.8 jit_solution(3706671722894200506)
XLA Ops:
  17.7 2.7 broadcast_multiply_fusion.1
  20.4 3.4 constant_dynamic-update-slice_fusion.1
  25.5 3.9 broadcast_multiply_fusion.2
  31.1 10.3 %broadcast_multiply_fusion = f32[27,3,256,256]{3,2,1,0:T(8,128)} fusion(f32[3,256,256]{2,1,0:T(8,128)S(1)} %copy-done.5, f32[27,256,256]{2,1,0:T(8,128)} %bitcast.24), kind=kLoop, calls=%fused_computation.79 | loop fusion | flops 5308416 | bytes 29097984 | tf_op jit(solution)/shard_map/mul | solution.py:29
  41.4 6.7 constant_dynamic-update-slice_fusion.5
  48.1 10.6 %constant_dynamic-update-slice_fusion = f32[121,256,256]{2,1,0:T(8,128)} fusion(f32[121,256,256]{2,1,0:T(8,128)} %constant_dynamic-update-slice_fusion.1, f32[81,256,256]{2,1,0:T(8,128)S(1)} %bitcast.277), kind=kLoop, calls=%fused_computation.354 | loop fusion | bytes 42467328 | tf_op jit(solution)/shard_map/concatenate | solution.py:256
  61.2 7.3 constant_dynamic-update-slice_fusion.4
  68.6 21.9 %multiply_reduce_fusion.4 = (f32[121,256]{1,0:T(8,128)S(1)}, f32[121,256]{1,0:T(8,128)S(1)}) fusion(f32[121,256,256]{2,1,0:T(8,128)} %constant_dynamic-update-slice_fusion, f32[256,256]{1,0:T(8,128)S(1)} %broadcast_select_fusion.7, f32[121,256,256]{2,1,0:T(8,128)} %constant_dynamic-update-slice_fusion.4), kind=kLoop, calls=%fused_computation.75 | loop fusion | flops 31657472 | bytes 63948800 | tf_op jit(solution)/shard_map/reduce_sum | solution.py:256
  111.2 167.1 %while.28 = (s32[]{:T(128)}, f32[32,8,4,256]{3,2,1,0:T(4,128)}, f32[32,8,4,256]{3,1,0,2:T(8,128)}, s32[]{:T(128)}) while((s32[]{:T(128)}, f32[32,8,4,256]{3,2,1,0:T(4,128)}, f32[32,8,4,256]{3,1,0,2:T(8,128)}, s32[]{:T(128)}) %tuple.289), condition=%wide.region_117.124_spmd, body=%wide.region_113.123_spmd.sunk | while | flops 12656642 | bytes 8938041 | solution.py:161
  279.8 4.7 fusion.90
  286.1 6.0 collective-permute-start.1
  297.9 7.9 collective-permute-done.2
  308.1 4.0 gather_fusion.9
  312.1 4.0 gather_fusion.8
  316.1 2.8 gather_fusion.7
  318.9 2.8 gather_fusion.10
  344.5 5.9 multiply_reduce_fusion.17
  428.2 6.2 scatter_custom_fusion
  434.5 6.9 scatter_fusion
  443.8 2.7 copy.853
  446.5 272.0 %while.27 = (s32[]{:T(128)}, f32[16,16,4,256]{3,2,1,0:T(4,128)S(1)}, f32[16,16,4,256]{3,2,1,0:T(4,128)S(1)}, pred[16,16]{1,0:T(8,128)(4,1)}, s32[16,16]{1,0:T(8,...) while((s32[]{:T(128)}, ...), condition=%wide.region_52.57_spmd, body=%wide.region_46.56_spmd.sunk | while | flops 33646784 | bytes 26781088 | solution.py:187
  457.2 5.5 fusion.112
  474.2 5.5 fusion.112
  491.2 5.5 fusion.112
  508.2 5.5 fusion.112
  525.2 5.5 fusion.112
  542.1 5.5 fusion.112
  559.1 5.5 fusion.112
  576.1 5.5 fusion.112
  593.1 5.5 fusion.112
  610.1 5.5 fusion.112
  627.1 5.5 fusion.112
  644.1 5.5 fusion.112
  661.1 5.5 fusion.112
  678.1 5.5 fusion.112
  695.1 5.5 fusion.112
  712.0 5.5 fusion.112
  719.7 8.8 %scatter_fusion.1 = f32[512,4,256]{2,1,0:T(4,128)S(1)} fusion(f32[512,4,256]{2,1,0:T(4,128)S(1)} %broadcast_in_dim.316, s32[256]{0:T(256)S(1)} %bitcast.314, f32[256,4,256]{2,1,0:T(4,128)S(1)} %bitcast.296), kind=kCustom, calls=%fused_computation.17 | custom fusion | flops 262144 | bytes 3146752 | tf_op jit(solution)/shard_map/scatter-add | solution.py:193
  728.6 19.5 %scatter_fusion.2 = f32[512,4,256]{2,1,0:T(4,128)S(1)} fusion(f32[512,4,256]{2,1,0:T(4,128)S(1)} %scatter_fusion.1, s32[256]{0:T(256)S(1)} %bitcast.313, f32[256,4,256]{2,1,0:T(4,128)} %bitcast.297), kind=kCustom, calls=%fused_computation.18 | custom fusion | flops 262144 | bytes 3146752 | tf_op jit(solution)/shard_map/scatter-add | solution.py:193
  748.2 2.7 slice_add_fusion.1
  767.3 5.1 collective-permute-start.4
  772.4 3.8 collective-permute-done.4
  776.3 4.6 collective-permute-done.3
  782.2 8.8 %collective-permute-start.5 = (f32[3,75216]{1,0:T(4,128)S(1)}, f32[3,75216]{1,0:T(4,128)S(1)}, u32[]{:S(2)}, u32[]{:S(2)}) collective-permute-start(f32[3,75216]{1,0:T(4,128)S(1)} %pad_maximum_fusion.3), channel_id=1, source_target_pairs={{0,16},{16,32},{32,48},{48,64},{64,80},{80,96},{96,112},{112,0},{1... | collective-permute-start | bytes 2707784 | tf_op jit(solution)/shard_map/ppermute | solution.py:21
  793.3 11.1 %collective-permute-done.5 = f32[3,75216]{1,0:T(4,128)S(1)} collective-permute-done((f32[3,75216]{1,0:T(4,128)S(1)}, f32[3,75216]{1,0:T(4,128)S(1)}, u32[]{:S(2)}, u32[]{:S(2)}) %collective-permute-start.5) | collective-permute-done | bytes 902624 | tf_op jit(solution)/shard_map/ppermute | solution.py:21
  820.9 2.7 multiply_reduce_fusion.9
  823.6 7.0 multiply_reduce_fusion.6
  830.7 8.8 %scatter_fusion.5 = f32[256,4,256]{2,1,0:T(4,128)S(1)} fusion(f32[256,4,256]{2,1,0:T(4,128)S(1)} %copy-done.6, s32[256]{0:T(256)S(1)} %bitcast.310, f32[256,4,256]{2,1,0:T(4,128)S(1)} %copy-done.14), kind=kCustom, calls=%fused_computation.23 | custom fusion | flops 262144 | bytes 3146752 | tf_op jit(solution)/shard_map/scatter-add | solution.py:336
  (1480 shorter events, 544.4 us)
Async XLA Ops:
  0.0 14.0 %copy-start.135 = (pred[256]{0:T(512)(128)(4,1)}, pred[256]{0:T(512)(128)(4,1)S(1)}, u32[]{:S(2)}) copy-start(pred[256]{0:T(512)(128)(4,1)S(1)} %compare_and_fusion.6) | copy-start | bytes 772
  0.8 13.2 %copy-start.130 = (s32[1,256]{1,0:T(1,128)}, s32[1,256]{1,0:T(1,128)S(1)}, u32[]{:S(2)}) copy-start(s32[1,256]{1,0:T(1,128)S(1)} %get-tuple-element.527) | copy-start | bytes 3076
  0.8 13.2 %copy-start.132 = (s32[1,256]{1,0:T(1,128)}, s32[1,256]{1,0:T(1,128)S(1)}, u32[]{:S(2)}) copy-start(s32[1,256]{1,0:T(1,128)S(1)} %get-tuple-element.528) | copy-start | bytes 3076
  0.9 13.1 %copy-start.149 = (s32[1,256]{1,0:T(1,128)}, s32[1,256]{1,0:T(1,128)S(1)}, u32[]{:S(2)}) copy-start(s32[1,256]{1,0:T(1,128)S(1)} %fusion.58) | copy-start | bytes 3076
  4.8 88.2 %copy-start.153 = (s32[64]{0:T(128)}, s32[64]{0:T(128)S(1)}, u32[]{:S(2)}) copy-start(s32[64]{0:T(128)S(1)} %fusion.78) | copy-start | bytes 772
  41.4 17.3 %slice-start = ((s8[21233664]{0:T(1024)(128)(4,1)}), s8[262144]{0:T(1024)(128)(4,1)S(1)}, s32[]{:S(2)}) async-start(s8[21233664]{0:T(1024)(128)(4,1)} %bitcast.278), calls=%async_computation | async-start | bytes 524288
  41.4 17.3 %slice-start.1 = ((s8[21233664]{0:T(1024)(128)(4,1)}), s8[4194304]{0:T(1024)(128)(4,1)S(1)}, s32[]{:S(2)}) async-start(s8[21233664]{0:T(1024)(128)(4,1)} %bitcast.278), calls=%async_computation.1 | async-start | bytes 8388608
  48.1 10.6 %slice-start.2 = ((s8[21233664]{0:T(1024)(128)(4,1)}), s8[4194304]{0:T(1024)(128)(4,1)S(1)}, s32[]{:S(2)}) async-start(s8[21233664]{0:T(1024)(128)(4,1)} %bitcast.278), calls=%async_computation.2 | async-start | bytes 8388608
  48.1 10.6 %slice-start.3 = ((s8[21233664]{0:T(1024)(128)(4,1)}), s8[4194304]{0:T(1024)(128)(4,1)S(1)}, s32[]{:S(2)}) async-start(s8[21233664]{0:T(1024)(128)(4,1)} %bitcast.278), calls=%async_computation.3 | async-start | bytes 8388608
  48.1 11.9 %slice-start.4 = ((s8[21233664]{0:T(1024)(128)(4,1)}), s8[4194304]{0:T(1024)(128)(4,1)S(1)}, s32[]{:S(2)}) async-start(s8[21233664]{0:T(1024)(128)(4,1)} %bitcast.278), calls=%async_computation.4 | async-start | bytes 8388608
  48.1 13.1 %slice-start.5 = ((s8[21233664]{0:T(1024)(128)(4,1)}), s8[4194304]{0:T(1024)(128)(4,1)S(1)}, s32[]{:S(2)}) async-start(s8[21233664]{0:T(1024)(128)(4,1)} %bitcast.278), calls=%async_computation.5 | async-start | bytes 8388608
  68.6 22.0 %copy-start.40 = (f32[3,256]{0,1:T(8,128)S(1)}, f32[3,256]{0,1:T(8,128)}, u32[]{:S(2)}) copy-start(f32[3,256]{0,1:T(8,128)} %copy.826) | copy-start | bytes 9220
  68.6 23.8 %copy-start.157 = (s32[1,3,64]{2,0,1:T(1,128)S(1)}, s32[1,3,64]{2,0,1:T(1,128)}, u32[]{:S(2)}) copy-start(s32[1,3,64]{2,0,1:T(1,128)} %param.37) | copy-start | bytes 2308
  105.8 174.1 %collective-permute-start = (f32[3,75456]{1,0:T(4,128)}, f32[3,75456]{1,0:T(4,128)}, u32[]{:S(2)}, u32[]{:S(2)}) collective-permute-start(f32[3,75456]{1,0:T(4,128)} %fusion.14), channel_id=1, source_target_pairs={{0,112},{16,0},{32,16},{48,32},{64,48},{80,64},{96,80},{112,96},{1... | collective-permute-start | bytes 2716424 | tf_op jit(solution)/shard_map/ppermute | solution.py:21
  107.2 189.3 %copy-start.88 = (s32[1,1,1024]{2,0,1:T(1,128)}, s32[1,1,1024]{2,0,1:T(1,128)S(1)}, u32[]{:S(2)}) copy-start(s32[1,1,1024]{2,0,1:T(1,128)S(1)} %get-tuple-element.474) | copy-start | bytes 12292
  107.2 224.3 %copy-start.128 = (pred[1024]{0:T(1024)(128)(4,1)}, pred[1024]{0:T(1024)(128)(4,1)S(1)}, u32[]{:S(2)}) copy-start(pred[1024]{0:T(1024)(128)(4,1)S(1)} %compare_reduce_fusion) | copy-start | bytes 3076
  107.3 224.9 %copy-start.104 = (f32[3,3]{1,0:T(4,128)}, f32[3,3]{1,0:T(4,128)S(1)}, u32[]{:S(2)}) copy-start(f32[3,3]{1,0:T(4,128)S(1)} %fusion.65) | copy-start | bytes 112
  107.3 288.9 %copy-start.62 = (f32[3,3]{1,0:T(4,128)}, f32[3,3]{1,0:T(4,128)S(1)}, u32[]{:S(2)}) copy-start(f32[3,3]{1,0:T(4,128)S(1)} %fusion.52) | copy-start | bytes 112
  110.6 233.8 %copy-start.64 = (f32[27,9,3]{0,2,1:T(4,128)}, f32[27,9,3]{0,2,1:T(4,128)S(1)}, u32[]{:S(2)}) copy-start(f32[27,9,3]{0,2,1:T(4,128)S(1)} %get-tuple-element.293) | copy-start | bytes 8752
  286.1 19.9 %collective-permute-start.1 = (f32[2,75456]{1,0:T(2,128)}, f32[2,75456]{1,0:T(2,128)S(1)}, u32[]{:S(2)}, u32[]{:S(2)}) collective-permute-start(f32[2,75456]{1,0:T(2,128)} %fusion.19), channel_id=1, source_target_pairs={{0,15},{1,0},{2,1},{3,2},{4,3},{5,4},{6,5},{7,6},{8,7},{9,8},{10,9... | collective-permute-start | bytes 1810952 | tf_op jit(solution)/shard_map/ppermute | solution.py:21
  293.0 19.1 %copy-start.110 = (f32[4,124]{1,0:T(4,128)}, f32[4,124]{1,0:T(4,128)S(1)}, u32[]{:S(2)}) copy-start(f32[4,124]{1,0:T(4,128)S(1)} %concatenate.109) | copy-start | bytes 5956
  296.6 9.3 %collective-permute-start.2 = (f32[75456]{0:T(1024)}, f32[75456]{0:T(1024)S(1)}, u32[]{:S(2)}, u32[]{:S(2)}) collective-permute-start(f32[75456]{0:T(1024)} %get-tuple-element.406), channel_id=1, source_target_pairs={{0,1},{1,2},{2,3},{3,4},{4,5},{5,6},{6,7},{7,8},{8,9},{9,10},{10,1... | collective-permute-start | bytes 905480 | tf_op jit(solution)/shard_map/ppermute | solution.py:21
  331.6 10.6 %copy-start.100 = (f32[1024]{0:T(1024)}, f32[1024]{0:T(1024)S(1)}, u32[]{:S(2)}) copy-start(f32[1024]{0:T(1024)S(1)} %get-tuple-element.359) | copy-start | bytes 12292
  332.2 10.0 %copy-start.84 = (f32[1024]{0:T(1024)}, f32[1024]{0:T(1024)S(1)}, u32[]{:S(2)}) copy-start(f32[1024]{0:T(1024)S(1)} %get-tuple-element.494) | copy-start | bytes 12292
  332.2 10.0 %copy-start.95 = (f32[1024]{0:T(1024)}, f32[1024]{0:T(1024)S(1)}, u32[]{:S(2)}) copy-start(f32[1024]{0:T(1024)S(1)} %get-tuple-element.492) | copy-start | bytes 12292
  332.2 10.0 %copy-start.86 = (f32[1024]{0:T(1024)}, f32[1024]{0:T(1024)S(1)}, u32[]{:S(2)}) copy-start(f32[1024]{0:T(1024)S(1)} %get-tuple-element.488) | copy-start | bytes 12292
  369.5 10.6 %copy-start.138 = (pred[64]{0:T(512)(128)(4,1)S(1)}, pred[64]{0:T(512)(128)(4,1)}, u32[]{:S(2)}) copy-start(pred[64]{0:T(512)(128)(4,1)} %get-tuple-element.501) | copy-start | bytes 196
  369.5 10.6 %copy-start.142 = (pred[64]{0:T(512)(128)(4,1)S(1)}, pred[64]{0:T(512)(128)(4,1)}, u32[]{:S(2)}) copy-start(pred[64]{0:T(512)(128)(4,1)} %compare_bitcast_fusion) | copy-start | bytes 196
  369.5 10.7 %copy-start.105 = (f32[3,3]{1,0:T(4,128)S(1)}, f32[3,3]{1,0:T(4,128)}, u32[]{:S(2)}) copy-start(f32[3,3]{1,0:T(4,128)} %copy-done.104) | copy-start | bytes 112
  371.5 10.4 %copy-start.70 = (f32[27,9,3]{0,2,1:T(4,128)S(1)}, f32[27,9,3]{0,2,1:T(4,128)}, u32[]{:S(2)}) copy-start(f32[27,9,3]{0,2,1:T(4,128)} %fusion.66) | copy-start | bytes 8752
  374.3 13.9 %copy-start.125 = (f32[9]{0:T(128)S(1)}, f32[9]{0:T(128)}, u32[]{:S(2)}) copy-start(f32[9]{0:T(128)} %add_reduce_fusion.1) | copy-start | bytes 112
  375.2 18.4 %copy-start.65 = (f32[27,9,3]{0,2,1:T(4,128)S(1)}, f32[27,9,3]{0,2,1:T(4,128)}, u32[]{:S(2)}) copy-start(f32[27,9,3]{0,2,1:T(4,128)} %copy-done.64) | copy-start | bytes 8752
  380.2 20.0 %copy-start.78 = (f32[64,3]{0,1:T(4,128)}, f32[64,3]{0,1:T(4,128)S(1)}, u32[]{:S(2)}) copy-start(f32[64,3]{0,1:T(4,128)S(1)} %get-tuple-element.384) | copy-start | bytes 2308
  393.4 16.2 %copy-start.21 = (f32[1024,27]{1,0:T(8,128)S(1)}, f32[1024,27]{1,0:T(8,128)}, u32[]{:S(2)}) copy-start(f32[1024,27]{1,0:T(8,128)} %slice.488) | copy-start | bytes 331780
  393.6 16.2 %copy-start.22 = (f32[1024,27]{1,0:T(8,128)S(1)}, f32[1024,27]{1,0:T(8,128)}, u32[]{:S(2)}) copy-start(f32[1024,27]{1,0:T(8,128)} %slice.493) | copy-start | bytes 331780
  396.5 18.3 %copy-start.23 = (f32[1024,81]{1,0:T(8,128)S(1)}, f32[1024,81]{1,0:T(8,128)}, u32[]{:S(2)}) copy-start(f32[1024,81]{1,0:T(8,128)} %slice.494) | copy-start | bytes 995332
  446.5 273.2 %copy-start.148 = (s32[256,1]{0,1:T(1,128)S(1)}, s32[256,1]{0,1:T(1,128)}, u32[]{:S(2)}) copy-start(s32[256,1]{0,1:T(1,128)} %compare_select_fusion.6) | copy-start | bytes 3076
  718.5 10.1 %copy-start.147 = (s32[1,1,256]{2,0,1:T(1,128)S(1)}, s32[1,1,256]{2,0,1:T(1,128)}, u32[]{:S(2)}) copy-start(s32[1,1,256]{2,0,1:T(1,128)} %get-tuple-element.496) | copy-start | bytes 3076
  762.8 28.2 %copy-start.15 = (f32[1,3,256,256]{3,2,1,0:T(8,128)S(1)}, f32[1,3,256,256]{3,2,1,0:T(8,128)}, u32[]{:S(2)}) copy-start(f32[1,3,256,256]{3,2,1,0:T(8,128)} %get-tuple-element.482) | copy-start | bytes 2359300
  766.2 26.4 %copy-start.127 = (s32[256]{0:T(256)S(1)}, s32[256]{0:T(256)}, u32[]{:S(2)}) copy-start(s32[256]{0:T(256)} %param.32) | copy-start | bytes 3076
  766.2 14.7 %collective-permute-start.3 = (f32[2,75216]{1,0:T(2,128)S(1)}, f32[2,75216]{1,0:T(2,128)S(1)}, u32[]{:S(2)}, u32[]{:S(2)}) collective-permute-start(f32[2,75216]{1,0:T(2,128)S(1)} %stack.108), channel_id=1, source_target_pairs={{0,1},{1,2},{2,3},{3,4},{4,5},{5,6},{6,7},{7,8},{8,9},{9,10},{10,1... | collective-permute-start | bytes 1805192 | tf_op jit(solution)/shard_map/ppermute | solution.py:21
  767.3 8.8 %collective-permute-start.4 = (f32[75216]{0:T(1024)S(1)}, f32[75216]{0:T(1024)S(1)}, u32[]{:S(2)}, u32[]{:S(2)}) collective-permute-start(f32[75216]{0:T(1024)S(1)} %get-tuple-element.409), channel_id=1, source_target_pairs={{0,15},{1,0},{2,1},{3,2},{4,3},{5,4},{6,5},{7,6},{8,7},{9,8},{10,9... | collective-permute-start | bytes 902600 | tf_op jit(solution)/shard_map/ppermute | solution.py:21
  782.2 22.2 %collective-permute-start.5 = (f32[3,75216]{1,0:T(4,128)S(1)}, f32[3,75216]{1,0:T(4,128)S(1)}, u32[]{:S(2)}, u32[]{:S(2)}) collective-permute-start(f32[3,75216]{1,0:T(4,128)S(1)} %pad_maximum_fusion.3), channel_id=1, source_target_pairs={{0,16},{16,32},{32,48},{48,64},{64,80},{80,96},{96,112},{112,0},{1... | collective-permute-start | bytes 2707784 | tf_op jit(solution)/shard_map/ppermute | solution.py:21
  792.6 13.5 %copy-start.154 = (s32[64]{0:T(128)S(1)}, s32[64]{0:T(128)}, u32[]{:S(2)}) copy-start(s32[64]{0:T(128)} %copy-done.153) | copy-start | bytes 772
  823.6 15.9 %copy-start.117 = (f32[3,256]{1,0:T(4,128)S(1)}, f32[3,256]{1,0:T(4,128)}, u32[]{:S(2)}) copy-start(f32[3,256]{1,0:T(4,128)} %get-tuple-element.442) | copy-start | bytes 9220
  830.7 10.6 %copy-start.35 = (f32[256,256]{1,0:T(8,128)S(1)}, f32[256,256]{1,0:T(8,128)}, u32[]{:S(2)}) copy-start(f32[256,256]{1,0:T(8,128)} %get-tuple-element.212) | copy-start | bytes 786436
  830.7 10.6 %slice-start.7 = ((f32[121,256]{1,0:T(8,128)}), f32[1,256]{1,0:T(1,128)S(1)}, s32[]{:S(2)}) async-start(f32[121,256]{1,0:T(8,128)} %copy-done.39), calls=%async_computation.7 | async-start | bytes 2048 | tf_op jit(solution)/shard_map/slice | solution.py:111
  830.7 11.7 %copy-start.50 = (pred[256,256]{1,0:T(8,128)(4,1)S(1)}, pred[256,256]{1,0:T(8,128)(4,1)}, u32[]{:S(2)}) copy-start(pred[256,256]{1,0:T(8,128)(4,1)} %iota_compare_fusion.3) | copy-start | bytes 196612
  (124 other events, 600.1 us)
where the time goes:
time: 861 us; the launch traced here: 845 us
  other arithmetic  503 us (58%)
  local copies, waits for them, and re-layouts  283 us (33%)
  waiting for transfers between devices  27.3 us (3%)
  starting transfers between devices  21.5 us (2%)
    reduce_sum x16, other arithmetic, pair_block(): accel_b = jnp.sum(spacing * (weight_a[:, None] * cubed)[None], 1)  88.4 us
    reduce_sum x32, other arithmetic, self_block(): accel = -jnp.sum(spacing * (weight_row[None, :] * cubed)[None], 2)  59.8 us
    reduce_sum x32, other arithmetic, self_block(): jnp.sum(spacing * spacing, 0) + soft_square  35.4 us
    reduce_sum x16, other arithmetic, pair_block(): inverse = lax.rsqrt(jnp.sum(spacing * spacing, 0) + soft_square)  35.2 us
    unnamed x356, local copies, waits for them, and re-layouts  34.9 us
    gather x16, local copies, waits for them, and re-layouts, near_one_group(): rows_a = jnp.take(table_bodies, ids_a, axis=0)  34.9 us
    gather x16, local copies, waits for them, and re-layouts, near_one_group(): rows_b = jnp.take(table_bodies, ids_b, axis=0)  34.9 us
    reduce_sum x16, other arithmetic, pair_block(): potential_b = -jnp.sum(weight_a[:, None] * inverse, 0)  33.7 us
  transfers between devices with their start and end apart: 6, of which 4 were waited for; matrix products, arithmetic and copies ran while one was open for 21% of the time, Pallas kernels for 0%

commit v1 on v0

v1 whole, which is shorter than its diff:
```python
import jax
import jax.numpy as jnp
from jax import lax
from jax.experimental import pallas as pl
from jax.experimental.pallas import tpu as pltpu
from jax.sharding import PartitionSpec as P

CX = 2
CY = 4
CZ = 32
LEAVES = 256
LEAF = 256
PARENTS = 32
SLOTS = 64
PSLOTS = 16
NEAR = 256
FAR = 1024
PFAR = 64
PAY = SLOTS + 5
SOFT = 0.0025
slab_steps = (1, 0, 1, 1)
sub_steps = (0, 1, 1, -1)
f32 = jnp.float32
bf16 = jnp.bfloat16

ALPHAS = [
    (i, j, d - i - j) for d in range(5) for i in range(d, -1, -1) for j in range(d - i, -1, -1)
]
AT = {a: n for n, a in enumerate(ALPHAS)}
FACT = (1.0, 1.0, 2.0, 6.0, 24.0)
TABLE = LEAVES + 4 * 128 + 128


def afact(alpha):
    return FACT[alpha[0]] * FACT[alpha[1]] * FACT[alpha[2]]


def add(a, b):
    return (a[0] + b[0], a[1] + b[1], a[2] + b[2])


def unit(axis):
    return tuple(1 if k == axis else 0 for k in range(3))


def split3(value):
    one = value.astype(bf16)
    rest = value - one.astype(f32)
    two = rest.astype(bf16)
    three = (rest - two.astype(f32)).astype(bf16)
    return one, two, three


def dot_nn(a, b):
    return lax.dot_general(a, b, (((1,), (0,)), ((), ())), preferred_element_type=f32)


def dot_nt(a, b):
    return lax.dot_general(a, b, (((1,), (1,)), ((), ())), preferred_element_type=f32)


def dot_tn(a, b):
    return lax.dot_general(a, b, (((0,), (0,)), ((), ())), preferred_element_type=f32)


def pick(values, onehot, transposed=False):
    parts = jnp.concatenate([part.astype(f32) for part in split3(values)], 0).astype(bf16)
    out = dot_nt(parts, onehot) if transposed else dot_nn(parts, onehot)
    rows = values.shape[0]
    return out[:rows] + out[rows : 2 * rows] + out[2 * rows :]


def iota(shape, dim):
    return lax.broadcasted_iota(jnp.int32, shape, dim)


def onehot_rows(count, ids):
    hit = iota((count, ids.shape[1]), 0) == ids
    return jnp.where(hit, 1.0, 0.0).astype(bf16)


def put_slab(slab_ref, c, slab):
    wide = jnp.concatenate([slab, jnp.zeros((4, LEAF), f32)], 0)
    for half in range(2):
        rows = pl.ds(pl.multiple_of(half * LEAVES * 8 + c * 8, 8), 8)
        slab_ref[rows, :] = wide[:, half * 128 : half * 128 + 128]


def get_rows(slab_ref, comp):
    return jnp.concatenate(
        [slab_ref[pl.ds(half * LEAVES * 8 + comp, LEAVES, stride=8), :] for half in range(2)], 1
    )


def monomials(x, y, z, w):
    made = {(0, 0, 0): w}
    for alpha in ALPHAS[1:]:
        for axis, value in ((2, z), (1, y), (0, x)):
            if alpha[axis]:
                lower = tuple(alpha[k] - (k == axis) for k in range(3))
                made[alpha] = made[lower] * value
                break
    return made


def shift_moments(moments, offsets):
    choose = ((1,), (1, 1), (1, 2, 1), (1, 3, 3, 1), (1, 4, 6, 4, 1))
    for axis in range(3):
        powers = [None, offsets[axis]]
        for _ in range(3):
            powers.append(powers[-1] * offsets[axis])
        moved = {}
        for alpha in ALPHAS:
            total = moments[alpha]
            for k in range(alpha[axis]):
                lower = tuple(k if q == axis else alpha[q] for q in range(3))
                total = total + moments[lower] * powers[alpha[axis] - k] * float(
                    choose[alpha[axis]][k]
                )
            moved[alpha] = total
        moments = moved
    return moments


def leaf_lanes():
    lane = iota((1, LEAVES), 1)
    return lane // (CY * CZ), lane // CZ % CY, lane % CZ


def parent_offsets():
    cell_x, cell_y, cell_z = leaf_lanes()
    return [(cell % 2).astype(f32) - 0.5 for cell in (cell_x, cell_y, cell_z)]


def front_kernel(
    at_ref, counts_ref, send_ref, ids_ref, pos_ref, mass_ref,
    own_ref, cells_ref, pcells_ref, pay0, pay1, pay2, pay3, slab_ref, turned_ref,
):
    pays = (pay0, pay1, pay2, pay3)
    base_x = at_ref[0] * CX
    base_y = at_ref[1] * CY
    row4 = iota((4, LEAF), 0)
    lane = iota((1, LEAF), 1)

    def one_leaf(c, _):
        start = pl.multiple_of(c * LEAF, LEAF)
        place = pos_ref[:, pl.ds(start, LEAF)]
        mass = jnp.concatenate(
            [mass_ref[pl.ds(2 * c, 1), :], mass_ref[pl.ds(2 * c + 1, 1), :]], 1
        )
        weight = jnp.where(lane < counts_ref[c], mass, 0.0)
        centre_x = (base_x + c // (CY * CZ)).astype(f32) + 0.5
        centre_y = (base_y + c // CZ % CY).astype(f32) + 0.5
        centre_z = (c % CZ).astype(f32) + 0.5
        centre = jnp.where(row4 == 1, centre_x, jnp.where(row4 == 2, centre_y, centre_z))
        centre = jnp.where(row4 == 0, 0.0, centre)
        slab = jnp.concatenate([weight, place], 0) - centre
        own_ref[c] = slab
        put_slab(slab_ref, c, slab)
        return 0

    lax.fori_loop(0, LEAVES, one_leaf, 0, unroll=8)

    for comp in range(4):
        turned_ref[comp] = get_rows(slab_ref, comp).T

    for half in range(2):
        lanes = slice(half * 128, half * 128 + 128)

        def chunk(step, totals):
            rows = pl.ds(pl.multiple_of(step * 8, 8), 8)
            w, x, y, z = [turned_ref[comp, rows, lanes] for comp in range(4)]
            made = monomials(x, y, z, w)
            return tuple(total + made[alpha] for total, alpha in zip(totals, ALPHAS))

        totals = lax.fori_loop(
            0, LEAF // 8, chunk, tuple(jnp.zeros((8, 128), f32) for _ in ALPHAS)
        )
        for n, total in enumerate(totals):
            cells_ref[n : n + 1, lanes] = jnp.sum(total, 0, keepdims=True)

    cell_x, cell_y, cell_z = leaf_lanes()
    cells_ref[35:36, :] = (base_x + cell_x).astype(f32) + 0.5
    cells_ref[36:37, :] = (base_y + cell_y).astype(f32) + 0.5
    cells_ref[37:38, :] = cell_z.astype(f32) + 0.5
    cells_ref[38:40, :] = jnp.zeros((2, LEAVES), f32)

    moments = {alpha: cells_ref[n : n + 1, :] for n, alpha in enumerate(ALPHAS)}
    moved = shift_moments(moments, parent_offsets())
    moved = jnp.concatenate(
        [moved[alpha] for alpha in ALPHAS] + [jnp.zeros((5, LEAVES), f32)], 0
    )
    parent_of = (iota((LEAVES, 128), 0) // CZ % CY // 2) * (CZ // 2) + iota(
        (LEAVES, 128), 0
    ) % CZ // 2
    belongs = jnp.where(parent_of == iota((LEAVES, 128), 1), 1.0, 0.0).astype(bf16)
    pcells = pick(moved, belongs)
    plane = iota((40, 128), 1)
    prow = iota((40, 128), 0)
    pcells = jnp.where(prow == 35, (base_x + 1).astype(f32), pcells)
    pcells = jnp.where(
        prow == 36, (base_y + 2 * (plane // (CZ // 2))).astype(f32) + 1.0, pcells
    )
    pcells = jnp.where(prow == 37, (2 * (plane % (CZ // 2))).astype(f32) + 1.0, pcells)
    pcells_ref[...] = pcells

    lane128 = iota((1, 128), 1)
    for q in range(4):
        pay = pays[q]

        def copy_leaf(k, _, pay=pay, q=q):
            pay[k] = own_ref[send_ref[q * SLOTS + k]]
            return 0

        lax.fori_loop(0, SLOTS, copy_leaf, 0, unroll=8)
        ids = ids_ref[q : q + 1, :]
        leaf_hot = onehot_rows(LEAVES, jnp.where(lane128 < SLOTS, ids, -1))
        parent_hot = onehot_rows(128, jnp.where(lane128 >= SLOTS, ids, -1))
        block = pick(cells_ref[...], leaf_hot) + pick(pcells, parent_hot)
        put_block(pay, block)


def put_block(pay, block):
    for s in range(5):
        pay[SLOTS + s, :, 0:128] = block[4 * s : 4 * s + 4]
        pay[SLOTS + s, :, 128:256] = block[20 + 4 * s : 24 + 4 * s]


def get_block(tail):
    return jnp.concatenate(
        [tail(s)[:, 0:128] for s in range(5)] + [tail(s)[:, 128:256] for s in range(5)], 0
    )


VM = pl.BlockSpec(memory_space=pltpu.VMEM)
SM = pl.BlockSpec(memory_space=pltpu.SMEM)
HB = pl.BlockSpec(memory_space=pl.ANY)
PARAMS = dict(vmem_limit_bytes=48 * 1024 * 1024)


def shaped(*shape):
    return jax.ShapeDtypeStruct(shape, f32)


def front(at, counts, send, ids, positions, masses):
    return pl.pallas_call(
        front_kernel,
        name="front",
        out_shape=[
            shaped(LEAVES, 4, LEAF), shaped(40, LEAVES), shaped(40, 128),
        ] + [shaped(PAY, 4, LEAF)] * 4,
        in_specs=[SM, SM, SM, VM, VM, VM],
        out_specs=[VM] * 7,
        scratch_shapes=[
            pltpu.VMEM((LEAVES * 16, 128), f32),
            pltpu.VMEM((4, LEAF, LEAVES), f32),
        ],
        compiler_params=pltpu.CompilerParams(**PARAMS),
    )(at, counts, send, ids, positions, masses)


def slab8(slab):
    return jnp.concatenate([slab, jnp.zeros((4, LEAF), f32)], 0)


def b_form(points):
    row = iota(points.shape, 0)
    square = jnp.sum(jnp.where(row == 0, 0.0, points * points), 0, keepdims=True)
    return jnp.where(row == 4, square, points)


def a_form(points):
    row = iota(points.shape, 0)
    square = jnp.sum(jnp.where(row == 0, 0.0, points * points), 0, keepdims=True)
    value = jnp.where(row == 0, square + SOFT, -2.0 * points)
    return jnp.where(row == 4, 1.0, value)


def widen(value):
    one = value.astype(bf16).astype(f32)
    rest = value - one
    two = rest.astype(bf16).astype(f32)
    return one, two, rest - two


def squares(a_points, b_points):
    a1, a2, a3 = widen(a_form(a_points))
    b1, b2, b3 = widen(b_form(b_points))
    left = jnp.concatenate([a1, a1, a2, a2, a1, a3], 0).astype(bf16)
    right = jnp.concatenate([b1, b2, b1, b2, b3, b1], 0).astype(bf16)
    return dot_tn(left, right)


def sources(points, weight):
    row = iota(points.shape, 0)
    loaded = points * weight
    one, two, _ = widen(loaded)
    third = jnp.concatenate([one, two], 0).astype(bf16)
    one, two, _ = widen(jnp.where(row == 4, weight, 0.0))
    first = jnp.concatenate([one, two], 0).astype(bf16)
    return third, first


def summed(sides, third, first, dot):
    out = dot(sides[0], third) + dot(sides[1], first)
    return out[0:8] + out[8:16]


def finish(total, points):
    row = iota((8, LEAF), 0)
    value = jnp.where(row == 0, -total[4:5], total - points * total[0:1])
    return value[0:4]


def load_points(slab):
    wide = slab8(slab)
    row = iota((8, LEAF), 0)
    return jnp.where(row == 0, 1.0, wide), slab[0:1]


def self_kernel(own_ref, out_ref):
    apart = jnp.where(iota((LEAF, LEAF), 0) == iota((LEAF, LEAF), 1), 0.0, 1.0)

    def one_leaf(c, _):
        points, weight = load_points(own_ref[c])
        inverse = lax.rsqrt(squares(points, points)) * apart
        cubed = inverse * inverse * inverse
        total = summed(
            sources(points, weight), cubed.astype(bf16), inverse.astype(bf16), dot_nn
        )
        out_ref[c] = finish(total, points)
        return 0

    lax.fori_loop(0, own_ref.shape[0], one_leaf, 0, unroll=4)


def self_part(own, first, count):
    block = 16
    return pl.pallas_call(
        self_kernel,
        name="self_part",
        grid=(count // block,),
        out_shape=shaped(count, 4, LEAF),
        in_specs=[pl.BlockSpec((block, 4, LEAF), lambda i: (i + first // block, 0, 0))],
        out_specs=pl.BlockSpec((block, 4, LEAF), lambda i: (i, 0, 0)),
        cost_estimate=pl.CostEstimate(
            flops=count * 40_000_000, bytes_accessed=count * 8192, transcendentals=0
        ),
        compiler_params=pltpu.CompilerParams(**PARAMS),
    )(own)


def near_kernel(
    pairs_ref, moved_ref, own_ref, in0, in1, in2, in3, backs_ref,
    out_ref, pay0, pay1, pay2, pay3, table, total, sem,
):
    pays = (pay0, pay1, pay2, pay3)
    copies = [pltpu.make_async_copy(own_ref, table.at[pl.ds(0, LEAVES)], sem.at[0])]
    for q, part in enumerate((in0, in1, in2, in3)):
        copies.append(
            pltpu.make_async_copy(
                part.at[pl.ds(0, SLOTS)],
                table.at[pl.ds(LEAVES + q * SLOTS, SLOTS)],
                sem.at[1 + q],
            )
        )
    for copy in copies:
        copy.start()

    def clear(c, _):
        total[c] = jnp.zeros((8, LEAF), f32)
        return 0

    lax.fori_loop(0, 2 * LEAVES, clear, 0, unroll=8)
    for copy in copies:
        copy.wait()

    row = iota((8, LEAF), 0)

    def one_pair(p):
        a = pairs_ref[0, p]
        listed = pairs_ref[1, p]
        b = jnp.maximum(listed, 0)
        used = jnp.where(listed >= 0, 1.0, 0.0)
        points_a, weight_a = load_points(table[a])
        points_b, weight_b = load_points(table[b])
        shift = jnp.where(
            row == 1,
            moved_ref[0, p],
            jnp.where(row == 2, moved_ref[1, p], jnp.where(row == 3, moved_ref[2, p], 0.0)),
        )
        from_b = points_a + shift
        from_a = points_b - shift
        inverse = lax.rsqrt(squares(from_b, points_b))
        cubed = (inverse * inverse * inverse).astype(bf16)
        inverse = inverse.astype(bf16)
        to_b = summed(sources(from_b, weight_a * used), cubed, inverse, dot_nn)
        to_a = summed(sources(from_a, weight_b * used), cubed, inverse, dot_nt)
        return a, b, to_a, to_b

    width = 4

    def some_pairs(step, _):
        done = [one_pair(step * width + k) for k in range(width)]
        for a, b, to_a, to_b in done:
            total[a] = total[a] + to_a
            total[b] = total[b] + to_b
        return 0

    def count_used(p, n):
        return n + jnp.where(pairs_ref[1, p] >= 0, 1, 0)

    used_pairs = lax.fori_loop(0, NEAR, count_used, 0)
    lax.fori_loop(0, (used_pairs + width - 1) // width, some_pairs, 0)

    def finish_own(c, _):
        points, _ = load_points(table[c])
        out_ref[c] = finish(total[c], points)
        return 0

    lax.fori_loop(0, LEAVES, finish_own, 0, unroll=8)
    for q in range(4):

        def finish_other(k, _, q=q):
            points, _ = load_points(table[LEAVES + q * SLOTS + k])
            pays[q][k] = finish(total[LEAVES + q * SLOTS + k], points)
            return 0

        lax.fori_loop(0, SLOTS, finish_other, 0, unroll=8)
        put_block(pays[q], backs_ref[q])


def near_part(pairs, moved, own, incoming, backs):
    return pl.pallas_call(
        near_kernel,
        name="near_part",
        out_shape=[shaped(LEAVES, 4, LEAF)] + [shaped(PAY, 4, LEAF)] * 4,
        in_specs=[SM, SM, HB, HB, HB, HB, HB, VM],
        out_specs=[VM] * 5,
        scratch_shapes=[
            pltpu.VMEM((2 * LEAVES, 4, LEAF), f32),
            pltpu.VMEM((2 * LEAVES, 8, LEAF), f32),
            pltpu.SemaphoreType.DMA((5,)),
        ],
        cost_estimate=pl.CostEstimate(
            flops=NEAR * 80_000_000, bytes_accessed=4_000_000, transcendentals=0
        ),
        compiler_params=pltpu.CompilerParams(**PARAMS),
    )(pairs, moved, own, *incoming, backs)


def derivatives(x, y, z):
    square = x * x + y * y + z * z
    inverse = 1.0 / jnp.sqrt(square)
    inverse2 = inverse * inverse
    table = {(0, (0, 0, 0)): inverse}
    for m in range(1, 5):
        table[(m, (0, 0, 0))] = table[(m - 1, (0, 0, 0))] * inverse2 * float(-(2 * m - 1))
    place = (x, y, z)

    def entry(m, alpha):
        key = (m, alpha)
        if key not in table:
            axis = [k for k in range(3) if alpha[k]][0]
            lower = tuple(alpha[k] - (k == axis) for k in range(3))
            value = place[axis] * entry(m + 1, lower)
            if lower[axis]:
                lowest = tuple(lower[k] - (k == axis) for k in range(3))
                value = value + float(lower[axis]) * entry(m + 1, lowest)
            table[key] = value
        return table[key]

    return {alpha: entry(0, alpha) for alpha in ALPHAS}


def mutual(a_ref, b_ref, to_a, to_b):
    def rows(n):
        return pl.ds(n * 8, 8)

    lift = a_ref[rows(38), :]
    live = a_ref[rows(39), :] > 0.5
    gap = [
        jnp.where(live, a_ref[rows(35 + k), :] - b_ref[rows(35 + k), :] - (lift if k == 2 else 0.0), 3.0)
        for k in range(3)
    ]
    made = derivatives(*gap)
    for beta in ALPHAS:
        sum_a = None
        sum_b = None
        for alpha in ALPHAS:
            if sum(alpha) + sum(beta) > 4:
                continue
            tensor = made[add(alpha, beta)]
            scale = 1.0 / afact(alpha)
            sign_a = -((-1.0) ** sum(alpha)) * scale
            sign_b = -((-1.0) ** sum(beta)) * scale
            term_a = b_ref[rows(AT[alpha]), :] * sign_a * tensor
            term_b = a_ref[rows(AT[alpha]), :] * sign_b * tensor
            sum_a = term_a if sum_a is None else sum_a + term_a
            sum_b = term_b if sum_b is None else sum_b + term_b
        to_a[rows(AT[beta]), :] = jnp.where(live, sum_a, 0.0)
        to_b[rows(AT[beta]), :] = jnp.where(live, sum_b, 0.0)


def far_kernel(
    image_ref, far_ref, parent_ref, near_ref, cells_ref, pcells_ref, in0, in1, in2, in3,
    leaf_ref, par_ref, backs_ref, moved_ref, tails, table, left, right, to_a, to_b, total, sem,
):
    copies = []
    for q, part in enumerate((in0, in1, in2, in3)):
        copies.append(
            pltpu.make_async_copy(part.at[pl.ds(SLOTS, 5)], tails.at[q], sem.at[q])
        )
    for copy in copies:
        copy.start()
    table[:, 0:LEAVES] = cells_ref[...]
    table[:, LEAVES + 512 :] = pcells_ref[...]
    row = iota((40, 128), 0)
    to_a[...] = jnp.zeros_like(to_a)
    to_b[...] = jnp.zeros_like(to_b)
    left[...] = jnp.zeros_like(left)
    right[...] = jnp.zeros_like(right)
    for copy in copies:
        copy.wait()
    for q in range(4):
        block = get_block(lambda s, q=q: tails[q, s])
        block = block + jnp.where(
            row == 35, image_ref[q, 0], jnp.where(row == 36, image_ref[q, 1], 0.0)
        )
        table[:, LEAVES + q * 128 : LEAVES + q * 128 + 128] = block
    parts = jnp.concatenate([part.astype(f32) for part in split3(table[...])], 0).astype(bf16)
    total[...] = jnp.zeros_like(total)

    def gathered(hot, first, count):
        out = dot_nn(parts[:, first : first + count], hot)
        return out[0:40] + out[40:80] + out[80:120]

    def leaf_entry(ids):
        other = ids - LEAVES
        return jnp.where(ids < LEAVES, ids, LEAVES + other // SLOTS * 128 + other % SLOTS)

    def parent_entry(ids):
        other = ids - PARENTS
        return jnp.where(
            ids < PARENTS, LEAVES + 512 + ids, LEAVES + other // PSLOTS * 128 + SLOTS + other % PSLOTS
        )

    def hots(ids_a, ids_b, parents):
        if parents:
            return (
                onehot_rows(128, ids_a), LEAVES + 512, 128,
                onehot_rows(640, parent_entry(ids_b) - LEAVES), LEAVES, 640,
            )
        return (
            onehot_rows(LEAVES, ids_a), 0, LEAVES,
            onehot_rows(768, leaf_entry(ids_b)), 0, 768,
        )

    def load(ids_a, ids_b, lifts, g, parents):
        hot_a, first_a, count_a, hot_b, first_b, count_b = hots(ids_a, ids_b, parents)
        from_a = gathered(hot_a, first_a, count_a)
        from_b = gathered(hot_b, first_b, count_b)
        live = jnp.where(ids_b >= 0, 1.0, 0.0)
        from_a = jnp.where(row == 38, lifts.astype(f32) * float(CZ), from_a)
        from_a = jnp.where(row == 39, live, from_a)
        left[pl.ds(g, 40, stride=8), :] = from_a
        right[pl.ds(g, 40, stride=8), :] = from_b

    def store(ids_a, ids_b, g, parents):
        hot_a, first_a, count_a, hot_b, first_b, count_b = hots(ids_a, ids_b, parents)
        sum_a = pick(to_a[pl.ds(g, 40, stride=8), :], hot_a, True)
        sum_b = pick(to_b[pl.ds(g, 40, stride=8), :], hot_b, True)
        total[:, first_a : first_a + count_a] += sum_a
        total[:, first_b : first_b + count_b] += sum_b

    for g in range(FAR // 128):
        lanes = slice(g * 128, g * 128 + 128)
        load(far_ref[0:1, lanes], far_ref[1:2, lanes], far_ref[2:3, lanes], g, False)
    mutual(left, right, to_a, to_b)
    for g in range(FAR // 128):
        lanes = slice(g * 128, g * 128 + 128)
        store(far_ref[0:1, lanes], far_ref[1:2, lanes], g, False)
    load(parent_ref[0:1, :], parent_ref[1:2, :], parent_ref[2:3, :], 0, True)
    mutual(left, right, to_a, to_b)
    store(parent_ref[0:1, :], parent_ref[1:2, :], 0, True)

    for g in range(NEAR // 128):
        lanes = slice(g * 128, g * 128 + 128)
        hot_a, _, _, hot_b, _, _ = hots(near_ref[0:1, lanes], near_ref[1:2, lanes], False)
        apart = gathered(hot_a, 0, LEAVES) - gathered(hot_b, 0, 768)
        apart = jnp.where(row == 37, apart - near_ref[2:3, lanes].astype(f32) * float(CZ), apart)
        for k in range(3):
            moved_ref[k : k + 1, lanes] = apart[35 + k : 36 + k, :]

    leaf_ref[...] = total[:, 0:LEAVES]
    par_ref[...] = total[:, LEAVES + 512 :]
    for q in range(4):
        backs_ref[q] = total[:, LEAVES + q * 128 : LEAVES + q * 128 + 128]


def far_part(image, far, parent, near, cells, pcells, incoming):
    return pl.pallas_call(
        far_kernel,
        name="far_part",
        out_shape=[
            shaped(40, LEAVES), shaped(40, 128), shaped(4, 40, 128), shaped(3, NEAR),
        ],
        in_specs=[SM, VM, VM, VM, VM, VM, HB, HB, HB, HB],
        out_specs=[VM] * 4,
        scratch_shapes=[
            pltpu.VMEM((4, 5, 4, LEAF), f32),
            pltpu.VMEM((40, TABLE), f32),
        ] + [pltpu.VMEM((320, 128), f32)] * 4 + [
            pltpu.VMEM((40, TABLE), f32),
            pltpu.SemaphoreType.DMA((4,)),
        ],
        compiler_params=pltpu.CompilerParams(**PARAMS),
    )(image, far, parent, near, cells, pcells, *incoming)


def shift_terms(terms, offsets):
    for axis in range(3):
        powers = [None, offsets[axis]]
        for _ in range(3):
            powers.append(powers[-1] * offsets[axis])
        moved = {}
        for alpha in ALPHAS:
            total = terms[alpha]
            for k in range(1, 5 - sum(alpha)):
                upper = tuple(alpha[q] + k * (q == axis) for q in range(3))
                total = total + terms[upper] * powers[k] * (1.0 / FACT[k])
            moved[alpha] = total
        terms = moved
    return terms


def horner(get, degree, x, y, z):
    over_x = None
    for i in range(degree, -1, -1):
        over_y = None
        for j in range(degree - i, -1, -1):
            over_z = None
            for k in range(degree - i - j, -1, -1):
                value = get((i, j, k))
                over_z = value if over_z is None else over_z * z + value
            over_y = over_z if over_y is None else over_y * y + over_z
        over_x = over_y if over_x is None else over_x * x + over_y
    return over_x


def last_kernel(
    counts_ref, send_ref, ids_ref, own_ref, near_ref, self0_ref, self1_ref, leaf_ref, par_ref,
    in0, in1, in2, in3, out_ref, slab_ref, turned_ref, terms_ref, field_ref, near_sum,
):
    incoming = (in0, in1, in2, in3)
    lane128 = iota((1, 128), 1)

    def copy_leaf(c, _):
        put_slab(slab_ref, c, own_ref[c])
        return 0

    lax.fori_loop(0, LEAVES, copy_leaf, 0, unroll=8)

    def both(c, _):
        near_sum[c] = near_ref[c] + self0_ref[c]
        near_sum[c + LEAVES // 2] = near_ref[c + LEAVES // 2] + self1_ref[c]
        return 0

    lax.fori_loop(0, LEAVES // 2, both, 0, unroll=8)

    leaf = leaf_ref[...]
    par = par_ref[...]
    for q in range(4):
        block = get_block(lambda s, q=q: incoming[q][SLOTS + s])
        ids = ids_ref[q : q + 1, :]
        leaf_hot = onehot_rows(LEAVES, jnp.where(lane128 < SLOTS, ids, -1))
        parent_hot = onehot_rows(128, jnp.where(lane128 >= SLOTS, ids, -1))
        leaf = leaf + pick(block, leaf_hot, True)
        par = par + pick(block, parent_hot, True)

        def arrive(k, _, q=q):
            c = send_ref[q * SLOTS + k]
            near_sum[c] = near_sum[c] + incoming[q][k]
            return 0

        lax.fori_loop(0, SLOTS, arrive, 0, unroll=4)
    lane_parent = (iota((128, LEAVES), 1) // CZ % CY // 2) * (CZ // 2) + iota(
        (128, LEAVES), 1
    ) % CZ // 2
    above = pick(par, jnp.where(lane_parent == iota((128, LEAVES), 0), 1.0, 0.0).astype(bf16))
    terms = {alpha: above[n : n + 1, :] for n, alpha in enumerate(ALPHAS)}
    terms = shift_terms(terms, parent_offsets())
    for n, alpha in enumerate(ALPHAS):
        terms_ref[n : n + 1, :] = leaf[n : n + 1, :] + terms[alpha]

    for comp in range(1, 4):
        turned_ref[comp] = get_rows(slab_ref, comp).T

    for half in range(2):
        lanes = slice(half * 128, half * 128 + 128)

        def term(alpha):
            return terms_ref[AT[alpha] : AT[alpha] + 1, lanes]

        def potential_at(alpha):
            return term(alpha) * (1.0 / afact(alpha))

        coefs = [{alpha: potential_at(alpha) for alpha in ALPHAS}]
        for axis in range(3):
            coefs.append(
                {
                    alpha: term(add(alpha, unit(axis))) * (-1.0 / afact(alpha))
                    for alpha in ALPHAS
                    if sum(alpha) <= 3
                }
            )

        def chunk(step, _):
            rows = pl.ds(pl.multiple_of(step * 32, 32), 32)
            x, y, z = [turned_ref[comp, rows, lanes] for comp in range(1, 4)]
            for comp in range(4):
                field_ref[comp, rows, lanes] = horner(
                    lambda alpha, comp=comp: coefs[comp][alpha], 3 if comp else 4, x, y, z
                )
            return 0

        lax.fori_loop(0, LEAF // 32, chunk, 0)

    for comp in range(4):
        turned = field_ref[comp].T
        for half in range(2):
            slab_ref[pl.ds(half * LEAVES * 8 + comp, LEAVES, stride=8), :] = turned[
                :, half * 128 : half * 128 + 128
            ]

    lane = iota((4, LEAF), 1)

    def write(c, _):
        value = jnp.concatenate(
            [
                slab_ref[pl.ds(pl.multiple_of(half * LEAVES * 8 + c * 8, 8), 8), :]
                for half in range(2)
            ],
            1,
        )[0:4] + near_sum[c]
        start = pl.multiple_of(c * LEAF, LEAF)
        out_ref[:, pl.ds(start, LEAF)] = jnp.where(lane < counts_ref[c], value, 0.0)
        return 0

    lax.fori_loop(0, LEAVES, write, 0, unroll=8)


def last(counts, send, ids, own, near, self0, self1, leaf, par, arrived):
    return pl.pallas_call(
        last_kernel,
        name="last",
        out_shape=shaped(4, LEAVES * LEAF),
        in_specs=[SM, SM] + [VM] * 11,
        out_specs=VM,
        scratch_shapes=[
            pltpu.VMEM((LEAVES * 16, 128), f32),
            pltpu.VMEM((4, LEAF, LEAVES), f32),
            pltpu.VMEM((40, LEAVES), f32),
            pltpu.VMEM((4, LEAF, LEAVES), f32),
            pltpu.VMEM((LEAVES, 4, LEAF), f32),
        ],
        compiler_params=pltpu.CompilerParams(**PARAMS),
    )(counts, send, ids, own, near, self0, self1, leaf, par, *arrived)


def image_shift(slab_at, sub_at, slab_count, sub_count):
    rows_out = []
    for direction in range(4):
        reach_x = slab_at + slab_steps[direction]
        reach_y = sub_at + sub_steps[direction]
        jump_x = (reach_x - reach_x % slab_count) * CX
        jump_y = (reach_y - reach_y % sub_count) * CY
        rows_out.append(jnp.stack([jump_x, jump_y]))
    return jnp.stack(rows_out).astype(f32)


def moved_by(value, slab_step, sub_step, slab_count, sub_count):
    pairs = []
    for slab_at in range(slab_count):
        for sub_at in range(sub_count):
            target = (slab_at + slab_step) % slab_count * sub_count + (sub_at + sub_step) % sub_count
            pairs.append((slab_at * sub_count + sub_at, target))
    return lax.ppermute(value, ("slab", "sub"), pairs)


def id_table(send_leaves, send_parents):
    return jnp.concatenate(
        [
            send_leaves.reshape(4, SLOTS),
            send_parents.reshape(4, PSLOTS),
            jnp.full((4, 128 - SLOTS - PSLOTS), -1, jnp.int32),
        ],
        1,
    )


def pad_pairs(pairs):
    filler = jnp.broadcast_to(
        jnp.array([[0], [-1], [0]], jnp.int32), (3, 128 - pairs.shape[1])
    )
    return jnp.concatenate([pairs, filler], 1)


def on_device(
    positions, masses, leaf_counts, send_leaves, send_parents, near_pairs, far_pairs, parent_pairs
):
    slab_count = lax.axis_size("slab")
    sub_count = lax.axis_size("sub")
    slab_at = lax.axis_index("slab")
    sub_at = lax.axis_index("sub")
    at = jnp.stack([slab_at, sub_at]).astype(jnp.int32)
    send = send_leaves[0]
    ids = id_table(send, send_parents[0])
    own, cells, pcells, *outgoing = front(
        at, leaf_counts, send, ids, positions, masses.reshape(-1, 128)
    )
    incoming = [
        moved_by(outgoing[q], -slab_steps[q], -sub_steps[q], slab_count, sub_count)
        for q in range(4)
    ]
    image = image_shift(slab_at, sub_at, slab_count, sub_count)
    self0 = self_part(own, 0, LEAVES // 2)
    leaf, par, backs, moved = far_part(
        image, far_pairs[0], pad_pairs(parent_pairs[0]), near_pairs[0], cells, pcells, incoming
    )
    near, *returning = near_part(near_pairs[0], moved, own, incoming, backs)
    arrived = [
        moved_by(returning[q], slab_steps[q], sub_steps[q], slab_count, sub_count)
        for q in range(4)
    ]
    self1 = self_part(own, LEAVES // 2, LEAVES // 2)
    return last(leaf_counts, send, ids, own, near, self0, self1, leaf, par, arrived)


def solution(mesh):
    return jax.shard_map(
        on_device,
        mesh=mesh,
        in_specs=(
            P(None, ("slab", "sub")),
            P(("slab", "sub")),
            P(("slab", "sub")),
            P(("slab", "sub"), None),
            P(("slab", "sub"), None),
            P(("slab", "sub"), None, None),
            P(("slab", "sub"), None, None),
            P(("slab", "sub"), None, None),
        ),
        out_specs=P(None, ("slab", "sub")),
        check_vma=False,
    )
```

time: 861 us -> 159 us (0.18); the launches traced: 845 us -> 156 us
  other arithmetic: 503 us -> 1.73 us
  local copies, waits for them, and re-layouts: 283 us -> 6.46 us
  Pallas kernels: 0 us -> 105 us
  waiting for transfers between devices: 27.3 us -> 0.03 us
  starting transfers between devices: 21.5 us -> 42.4 us
    reduce_sum x188 -> x0, other arithmetic: 331 us -> none  [the longest x16 88.4 us: pair_block(): accel_b = jnp.sum(spacing * (weight_a[:, None] * cubed)[None], 1)]
    pallas_call x0 -> x6, Pallas kernels: none -> 105 us  [the longest x1 47.8 us: near_part(): pl.pallas_call(near_kernel, name='near_part', out_shape=[shaped(LEAVES, 4...]
    gather x53 -> x0, local copies, waits for them, and re-layouts: 93.7 us -> none  [the longest x16 34.9 us: near_one_group(): rows_a = jnp.take(table_bodies, ids_a, axis=0)]
    scatter-add x9 -> x0, other arithmetic: 55.7 us -> none  [the longest x2 28.4 us: near_work(): return summed.at[owned_ids].add(part_a).at[partner_ids].add(part_b)]
    unnamed x356 -> x22, local copies, waits for them, and re-layouts: 34.9 us -> 6.15 us
    ppermute x6 -> x8, waiting for transfers between devices: 27.3 us -> 0.03 us  [moved_by(): return lax.ppermute(value, ('slab', 'sub'), pairs)]
    mul x29 -> x0, other arithmetic: 25.1 us -> none  [the longest x9 19.6 us: outer_powers(): grown = before[:, None] * offset[None, :]]
    squeeze x34 -> x0, local copies, waits for them, and re-layouts: 24.5 us -> none  [the longest x32 24.3 us: self_work(): fields = lax.map(self_one_group, grouped)]
  transfers between devices with their start and end apart: 6 -> 8, of which waited for: 4 -> 0; matrix products, arithmetic and copies ran while one was open for 21% -> 0% of each run, Pallas kernels for 0% -> 26%
where the time goes in v1:
time: 159 us; the launch traced here: 156 us
  Pallas kernels  105 us (66%)
  starting transfers between devices  42.4 us (27%)
  local copies, waits for them, and re-layouts  6.46 us (4%)
  other arithmetic  1.73 us (1%)
    pallas_call x1, Pallas kernels, near_part(): pl.pallas_call(near_kernel, name='near_part', out_shape=[shaped(LEAVES, 4...  47.8 us
    ppermute x8, starting transfers between devices, moved_by(): return lax.ppermute(value, ('slab', 'sub'), pairs)  42.4 us
    pallas_call x2, Pallas kernels, self_part(): pl.pallas_call(self_kernel, name='self_part', grid=(count // block,), out...  40.1 us
    pallas_call x1, Pallas kernels, front(): pl.pallas_call(front_kernel, name='front', out_shape=[shaped(LEAVES, 4, L...  7.59 us
    pallas_call x1, Pallas kernels, last(): pl.pallas_call(last_kernel, name='last', out_shape=shaped(4, LEAVES * LEA...  6.94 us
    unnamed x22, local copies, waits for them, and re-layouts  6.15 us
  transfers between devices with their start and end apart: 8, of which 0 were waited for; matrix products, arithmetic and copies ran while one was open for 0% of the time, Pallas kernels for 26%

profile of v1, /device:TPU:1, one launch (start us, length us, event | category | flops | bytes accessed | tf_op | source)
XLA Modules:
  0.0 156.2 jit_solution(14980962198521417275)
XLA Ops:
  0.0 0.0 copy-start.2
  0.0 0.5 broadcast.13
  0.5 0.2 copy-done.2
  0.7 0.7 reduce.7
  1.4 0.1 reshape_squeeze.6
  1.4 0.6 copy-done.8
  2.0 0.7 reduce.6
  2.7 0.1 reshape_squeeze.7
  2.8 0.1 pad.18.clone
  2.8 0.1 pad_add_fusion.1.at_ref
  2.9 0.1 add_add_fusion.ids_ref
  3.0 0.0 copy-start.3
  3.0 0.7 copy-done.3
  3.7 0.0 copy-start
  3.7 1.2 copy-done
  4.9 0.0 copy-start.1
  4.9 0.9 copy-done.1
  5.8 7.6 %front.1 = (f32[256,4,256]{2,1,0:T(4,128)S(1)}, f32[40,256]{1,0:T(8,128)S(1)}, f32[40,128]{1,0:T(8,128)S(1)}, f32[69,4,256]{2,1,0:T(4,128)S(1)}, f32[69,4,256]{2...) custom-call(s32[2]{0:T(128)S(1)} %pad_add_fusion.1.at_ref, s32[256]{0:T(256)S(1)} %copy-done.3, ...), custom_call_target="tpu_custom_call" | custom-call | tf_op jit(solution)/shard_map/front/pallas_call | solution.py:246
  13.4 1.4 collective-permute-start
  14.9 6.0 %collective-permute-start.1 = (f32[69,4,256]{2,1,0:T(4,128)S(1)}, f32[69,4,256]{2,1,0:T(4,128)S(1)}, u32[]{:S(2)}, u32[]{:S(2)}) collective-permute-start(f32[69,4,256]{2,1,0:T(4,128)S(1)} %get-tuple-element.25), channel_id=1, source_target_pairs={{0,15},{1,0},{2,1},{3,2},{4,3},{5,4},{6,5},{7,6},{8,7},{9,8},{10,9... | collective-permute-start | bytes 847880 | tf_op jit(solution)/shard_map/ppermute | solution.py:788
  20.9 3.2 %collective-permute-start.2 = (f32[69,4,256]{2,1,0:T(4,128)S(1)}, f32[69,4,256]{2,1,0:T(4,128)S(1)}, u32[]{:S(2)}, u32[]{:S(2)}) collective-permute-start(f32[69,4,256]{2,1,0:T(4,128)S(1)} %get-tuple-element.26), channel_id=1, source_target_pairs={{0,127},{1,112},{2,113},{3,114},{4,115},{5,116},{6,117},{7,118},{8... | collective-permute-start | bytes 847880 | tf_op jit(solution)/shard_map/ppermute | solution.py:788
  24.1 1.0 collective-permute-start.3
  25.1 0.0 copy-start.4
  25.1 0.7 copy-done.5
  25.8 0.0 copy-done.4
  25.8 0.7 copy-done.6
  26.5 20.0 %self_part.2.self0_ref = f32[128,4,256]{2,1,0:T(4,128)S(1)} custom-call(f32[256,4,256]{2,1,0:T(4,128)S(1)} %get-tuple-element.21.own_ref), custom_call_target="tpu_custom_call" | custom-call | flops 5120000000 | bytes 1048576 | tf_op jit(solution)/shard_map/self_part/pallas_call | solution.py:339
  46.5 0.1 add_bitcast_fusion
  46.6 0.1 add_bitcast_fusion.1
  46.7 0.7 copy-done.7
  47.4 0.1 broadcast_in_dim.12
  47.4 0.1 pad_add_fusion.parent_ref
  47.5 0.0 collective-permute-done.in0
  47.5 0.0 collective-permute-done.1.in1
  47.5 0.0 collective-permute-done.2.in2
  47.5 0.0 collective-permute-done.3.in3
  47.6 3.0 %far_part.1 = (f32[40,256]{1,0:T(8,128)S(1)}, f32[40,128]{1,0:T(8,128)S(1)}, f32[4,40,128]{2,1,0:T(8,128)S(1)}, f32[3,256]{1,0:T(4,128)S(1)}) custom-call(f32[4,2]{1,0:T(4,128)S(1)} %add_convert_fusion.image_ref, s32[3,1024]{1,0:T(4,128)S(1)} %bitcast.27, s32[3,128]{1,0:T(4,128)S(1)} %pad_add_fusion.parent_ref, s32[3,256]{1,0:T(4,128)S(1)} %bitcast.28, ...), custom_call_target="tpu_custom_call" | custom-call | tf_op jit(solution)/shard_map/far_part/pallas_call | solution.py:602
  50.6 47.8 %near_part.1 = (f32[256,4,256]{2,1,0:T(4,128)S(1)}, f32[69,4,256]{2,1,0:T(4,128)S(1)}, f32[69,4,256]{2,1,0:T(4,128)S(1)}, f32[69,4,256]{2,1,0:T(4,128)S(1)}, f32[69,4,256]{2,1,0:T(4,128)S(1)}) custom-call(s32[3,256]{1,0:T(4,128)S(1)} %bitcast.29, f32[3,256]{1,0:T(4,128)S(1)} %get-tuple-element.28.moved_ref, f32[256,4,256]{2,1,0:T(4,128)S(1)} %get-tuple-element.21.own_ref, ...), custom_call_target="tpu_custom_call" | custom-call | flops 20480000000 | bytes 4000000 | tf_op jit(solution)/shard_map/near_part/pallas_call | solution.py:434
  98.4 15.4 %collective-permute-start.4 = (f32[69,4,256]{2,1,0:T(4,128)S(1)}, f32[69,4,256]{2,1,0:T(4,128)S(1)}, u32[]{:S(2)}, u32[]{:S(2)}) collective-permute-start(f32[69,4,256]{2,1,0:T(4,128)S(1)} %get-tuple-element.33), channel_id=1, source_target_pairs={{0,16},{1,17},{2,18},{3,19},{4,20},{5,21},{6,22},{7,23},{8,24},{9,... | collective-permute-start | bytes 847880 | tf_op jit(solution)/shard_map/ppermute | solution.py:788
  113.8 13.7 %collective-permute-start.5 = (f32[69,4,256]{2,1,0:T(4,128)S(1)}, f32[69,4,256]{2,1,0:T(4,128)S(1)}, u32[]{:S(2)}, u32[]{:S(2)}) collective-permute-start(f32[69,4,256]{2,1,0:T(4,128)S(1)} %get-tuple-element.34), channel_id=1, source_target_pairs={{0,1},{1,2},{2,3},{3,4},{4,5},{5,6},{6,7},{7,8},{8,9},{9,10},{10,1... | collective-permute-start | bytes 847880 | tf_op jit(solution)/shard_map/ppermute | solution.py:788
  127.5 0.0 collective-permute-start.6
  127.5 1.7 %collective-permute-start.7 = (f32[69,4,256]{2,1,0:T(4,128)S(1)}, f32[69,4,256]{2,1,0:T(4,128)S(1)}, u32[]{:S(2)}, u32[]{:S(2)}) collective-permute-start(f32[69,4,256]{2,1,0:T(4,128)S(1)} %get-tuple-element.36), channel_id=1, source_target_pairs={{0,31},{1,16},{2,17},{3,18},{4,19},{5,20},{6,21},{7,22},{8,23},{9,... | collective-permute-start | bytes 847880 | tf_op jit(solution)/shard_map/ppermute | solution.py:788
  129.2 20.0 %self_part.3.self1_ref = f32[128,4,256]{2,1,0:T(4,128)S(1)} custom-call(f32[256,4,256]{2,1,0:T(4,128)S(1)} %get-tuple-element.21.own_ref), custom_call_target="tpu_custom_call" | custom-call | flops 5120000000 | bytes 1048576 | tf_op jit(solution)/shard_map/self_part/pallas_call | solution.py:339
  149.2 0.0 collective-permute-done.4.in0
  149.2 0.0 collective-permute-done.5.in1
  149.3 0.0 collective-permute-done.6.in2
  149.3 0.0 collective-permute-done.7.in3
  149.3 6.9 %last.1 = f32[4,65536]{1,0:T(4,128)} custom-call(s32[256]{0:T(256)S(1)} %copy-done.3, s32[256]{0:T(256)S(1)} %bitcast.31, s32[4,128]{1,0:T(4,128)S(1)} %add_add_fusion.ids_ref, f32[256,4,256]{2,1,0:T(4,128)S(1)} %get-tuple-element.21.own_ref, f32[256,4,256]{2,1,0:T(4,128)S(1)} %get-tuple-element.30.near_ref, f32[128,4,256]{2,1,0:T(4,128)S(1)} %self_part.2.self0_ref, ...), custom_call_target="tpu_custom_call" | custom-call | tf_op jit(solution)/shard_map/last/pallas_call | solution.py:754
  (9 shorter events, 0.0 us)
Async XLA Ops:
  0.0 0.7 copy-start.2
  1.3 0.7 copy-start.8
  3.0 0.7 copy-start.3
  3.7 1.2 copy-start
  4.9 0.9 copy-start.1
  13.4 34.1 %collective-permute-start = (f32[69,4,256]{2,1,0:T(4,128)S(1)}, f32[69,4,256]{2,1,0:T(4,128)S(1)}, u32[]{:S(2)}, u32[]{:S(2)}) collective-permute-start(f32[69,4,256]{2,1,0:T(4,128)S(1)} %get-tuple-element.24), channel_id=1, source_target_pairs={{0,112},{1,113},{2,114},{3,115},{4,116},{5,117},{6,118},{7,119},{8... | collective-permute-start | bytes 847880 | tf_op jit(solution)/shard_map/ppermute | solution.py:788
  14.9 32.7 %collective-permute-start.1 = (f32[69,4,256]{2,1,0:T(4,128)S(1)}, f32[69,4,256]{2,1,0:T(4,128)S(1)}, u32[]{:S(2)}, u32[]{:S(2)}) collective-permute-start(f32[69,4,256]{2,1,0:T(4,128)S(1)} %get-tuple-element.25), channel_id=1, source_target_pairs={{0,15},{1,0},{2,1},{3,2},{4,3},{5,4},{6,5},{7,6},{8,7},{9,8},{10,9... | collective-permute-start | bytes 847880 | tf_op jit(solution)/shard_map/ppermute | solution.py:788
  20.9 26.6 %collective-permute-start.2 = (f32[69,4,256]{2,1,0:T(4,128)S(1)}, f32[69,4,256]{2,1,0:T(4,128)S(1)}, u32[]{:S(2)}, u32[]{:S(2)}) collective-permute-start(f32[69,4,256]{2,1,0:T(4,128)S(1)} %get-tuple-element.26), channel_id=1, source_target_pairs={{0,127},{1,112},{2,113},{3,114},{4,115},{5,116},{6,117},{7,118},{8... | collective-permute-start | bytes 847880 | tf_op jit(solution)/shard_map/ppermute | solution.py:788
  24.1 23.5 %collective-permute-start.3 = (f32[69,4,256]{2,1,0:T(4,128)S(1)}, f32[69,4,256]{2,1,0:T(4,128)S(1)}, u32[]{:S(2)}, u32[]{:S(2)}) collective-permute-start(f32[69,4,256]{2,1,0:T(4,128)S(1)} %get-tuple-element.27), channel_id=1, source_target_pairs={{0,113},{1,114},{2,115},{3,116},{4,117},{5,118},{6,119},{7,120},{8... | collective-permute-start | bytes 847880 | tf_op jit(solution)/shard_map/ppermute | solution.py:788
  25.1 0.7 copy-start.4
  25.1 0.7 copy-start.5
  25.8 0.7 copy-start.6
  46.7 0.7 copy-start.7
  98.4 50.8 %collective-permute-start.4 = (f32[69,4,256]{2,1,0:T(4,128)S(1)}, f32[69,4,256]{2,1,0:T(4,128)S(1)}, u32[]{:S(2)}, u32[]{:S(2)}) collective-permute-start(f32[69,4,256]{2,1,0:T(4,128)S(1)} %get-tuple-element.33), channel_id=1, source_target_pairs={{0,16},{1,17},{2,18},{3,19},{4,20},{5,21},{6,22},{7,23},{8,24},{9,... | collective-permute-start | bytes 847880 | tf_op jit(solution)/shard_map/ppermute | solution.py:788
  113.8 35.4 %collective-permute-start.5 = (f32[69,4,256]{2,1,0:T(4,128)S(1)}, f32[69,4,256]{2,1,0:T(4,128)S(1)}, u32[]{:S(2)}, u32[]{:S(2)}) collective-permute-start(f32[69,4,256]{2,1,0:T(4,128)S(1)} %get-tuple-element.34), channel_id=1, source_target_pairs={{0,1},{1,2},{2,3},{3,4},{4,5},{5,6},{6,7},{7,8},{8,9},{9,10},{10,1... | collective-permute-start | bytes 847880 | tf_op jit(solution)/shard_map/ppermute | solution.py:788
  127.5 21.7 %collective-permute-start.6 = (f32[69,4,256]{2,1,0:T(4,128)S(1)}, f32[69,4,256]{2,1,0:T(4,128)S(1)}, u32[]{:S(2)}, u32[]{:S(2)}) collective-permute-start(f32[69,4,256]{2,1,0:T(4,128)S(1)} %get-tuple-element.35), channel_id=1, source_target_pairs={{0,17},{1,18},{2,19},{3,20},{4,21},{5,22},{6,23},{7,24},{8,25},{9,... | collective-permute-start | bytes 847880 | tf_op jit(solution)/shard_map/ppermute | solution.py:788
  127.5 21.7 %collective-permute-start.7 = (f32[69,4,256]{2,1,0:T(4,128)S(1)}, f32[69,4,256]{2,1,0:T(4,128)S(1)}, u32[]{:S(2)}, u32[]{:S(2)}) collective-permute-start(f32[69,4,256]{2,1,0:T(4,128)S(1)} %get-tuple-element.36), channel_id=1, source_target_pairs={{0,31},{1,16},{2,17},{3,18},{4,19},{5,20},{6,21},{7,22},{8,23},{9,... | collective-permute-start | bytes 847880 | tf_op jit(solution)/shard_map/ppermute | solution.py:788

commit v2 on v1

--- a/solution.py
+++ b/solution.py
@@ -18,6 +18,7 @@
 PFAR = 64
 PAY = SLOTS + 5
 SOFT = 0.0025
+WIDTH = 8
 slab_steps = (1, 0, 1, 1)
 sub_steps = (0, 1, 1, -1)
 f32 = jnp.float32
@@ -292,24 +293,24 @@
 
 
 def sources(points, weight):
+    parts = widen(b_form(points) * weight)
+    return jnp.concatenate(parts + (jnp.zeros_like(parts[0]),), 0).astype(bf16)
+
+
+def fold(out):
+    total = out[0:8]
+    for first in range(8, out.shape[0] // 8 * 8, 8):
+        total = total + out[first : first + 8]
+    return total
+
+
+def finish(total, points):
     row = iota(points.shape, 0)
-    loaded = points * weight
-    one, two, _ = widen(loaded)
-    third = jnp.concatenate([one, two], 0).astype(bf16)
-    one, two, _ = widen(jnp.where(row == 4, weight, 0.0))
-    first = jnp.concatenate([one, two], 0).astype(bf16)
-    return third, first
-
-
-def summed(sides, third, first, dot):
-    out = dot(sides[0], third) + dot(sides[1], first)
-    return out[0:8] + out[8:16]
-
-
-def finish(total, points):
-    row = iota((8, LEAF), 0)
-    value = jnp.where(row == 0, -total[4:5], total - points * total[0:1])
-    return value[0:4]
+    mass = total[0:1]
+    square = b_form(points)[4:5]
+    along = jnp.sum(jnp.where((row >= 1) & (row <= 3), points * total, 0.0), 0, keepdims=True)
+    potential = total[4:5] + (square + SOFT) * mass - 2.0 * along
+    return jnp.where(row == 0, -potential, total - points * mass)[0:4]
 
 
 def load_points(slab):
@@ -321,21 +322,27 @@
 def self_kernel(own_ref, out_ref):
     apart = jnp.where(iota((LEAF, LEAF), 0) == iota((LEAF, LEAF), 1), 0.0, 1.0)
 
-    def one_leaf(c, _):
-        points, weight = load_points(own_ref[c])
-        inverse = lax.rsqrt(squares(points, points)) * apart
-        cubed = inverse * inverse * inverse
-        total = summed(
-            sources(points, weight), cubed.astype(bf16), inverse.astype(bf16), dot_nn
-        )
-        out_ref[c] = finish(total, points)
+    def some_leaves(step, _):
+        first = step * WIDTH
+        loaded = [load_points(own_ref[first + k]) for k in range(WIDTH)]
+        spaced = [squares(points, points) for points, _ in loaded]
+        cubes = []
+        for value in spaced:
+            inverse = lax.rsqrt(value) * apart
+            cubes.append(inverse * inverse * inverse)
+        high = [cube.astype(bf16) for cube in cubes]
+        for k, (points, weight) in enumerate(loaded):
+            low = (cubes[k] - high[k].astype(f32)).astype(bf16)
+            side = sources(points, weight)
+            total = fold(dot_nn(side, high[k])) + fold(dot_nn(side[0:16], low))
+            out_ref[first + k] = finish(total, points)
         return 0
 
-    lax.fori_loop(0, own_ref.shape[0], one_leaf, 0, unroll=4)
+    lax.fori_loop(0, own_ref.shape[0] // WIDTH, some_leaves, 0)
 
 
 def self_part(own, first, count):
-    block = 16
+    block = 32
     return pl.pallas_call(
         self_kernel,
         name="self_part",
@@ -377,32 +384,35 @@
 
     row = iota((8, LEAF), 0)
 
-    def one_pair(p):
-        a = pairs_ref[0, p]
-        listed = pairs_ref[1, p]
-        b = jnp.maximum(listed, 0)
-        used = jnp.where(listed >= 0, 1.0, 0.0)
-        points_a, weight_a = load_points(table[a])
-        points_b, weight_b = load_points(table[b])
-        shift = jnp.where(
-            row == 1,
-            moved_ref[0, p],
-            jnp.where(row == 2, moved_ref[1, p], jnp.where(row == 3, moved_ref[2, p], 0.0)),
-        )
-        from_b = points_a + shift
-        from_a = points_b - shift
-        inverse = lax.rsqrt(squares(from_b, points_b))
-        cubed = (inverse * inverse * inverse).astype(bf16)
-        inverse = inverse.astype(bf16)
-        to_b = summed(sources(from_b, weight_a * used), cubed, inverse, dot_nn)
-        to_a = summed(sources(from_a, weight_b * used), cubed, inverse, dot_nt)
-        return a, b, to_a, to_b
-
-    width = 4
-
     def some_pairs(step, _):
-        done = [one_pair(step * width + k) for k in range(width)]
-        for a, b, to_a, to_b in done:
+        first = step * WIDTH
+        ends, loaded = [], []
+        for k in range(WIDTH):
+            p = first + k
+            a = pairs_ref[0, p]
+            listed = pairs_ref[1, p]
+            b = jnp.maximum(listed, 0)
+            used = jnp.where(listed >= 0, 1.0, 0.0)
+            points_a, weight_a = load_points(table[a])
+            points_b, weight_b = load_points(table[b])
+            shift = jnp.where(
+                row == 1,
+                moved_ref[0, p],
+                jnp.where(row == 2, moved_ref[1, p], jnp.where(row == 3, moved_ref[2, p], 0.0)),
+            )
+            ends.append((a, b))
+            loaded.append((points_a + shift, weight_a * used, points_b, weight_b * used, shift))
+        spaced = [squares(from_b, points_b) for from_b, _, points_b, _, _ in loaded]
+        high = []
+        for value in spaced:
+            inverse = lax.rsqrt(value)
+            high.append((inverse * inverse * inverse).astype(bf16))
+        done = []
+        for (from_b, weight_a, points_b, weight_b, shift), cube in zip(loaded, high):
+            to_b = fold(dot_nn(sources(from_b, weight_a), cube))
+            to_a = fold(dot_nt(sources(points_b - shift, weight_b), cube))
+            done.append((to_a, to_b))
+        for (a, b), (to_a, to_b) in zip(ends, done):
             total[a] = total[a] + to_a
             total[b] = total[b] + to_b
         return 0
@@ -411,7 +421,7 @@
         return n + jnp.where(pairs_ref[1, p] >= 0, 1, 0)
 
     used_pairs = lax.fori_loop(0, NEAR, count_used, 0)
-    lax.fori_loop(0, (used_pairs + width - 1) // width, some_pairs, 0)
+    lax.fori_loop(0, (used_pairs + WIDTH - 1) // WIDTH, some_pairs, 0)
 
     def finish_own(c, _):
         points, _ = load_points(table[c])

time: 159 us -> 107 us (0.67); the launches traced: 156 us -> 107 us
  Pallas kernels: 105 us -> 75.3 us
  starting transfers between devices: 42.4 us -> 23.1 us
    ppermute x8, starting transfers between devices: 42.4 us -> 23.1 us  [moved_by(): return lax.ppermute(value, ('slab', 'sub'), pairs)]
    pallas_call x1, Pallas kernels: 47.8 us -> 30.2 us  [near_part(): pl.pallas_call(near_kernel, name='near_part', out_shape=[shaped(LEAVES, 4...]
    pallas_call x2, Pallas kernels: 40.1 us -> 27.5 us  [self_part(): pl.pallas_call(self_kernel, name='self_part', grid=(count // block,), out...]
where the time goes in v2:
time: 107 us
  Pallas kernels  75.3 us (70%)
  starting transfers between devices  23.1 us (22%)
  local copies, waits for them, and re-layouts  6.46 us (6%)
  other arithmetic  1.72 us (2%)
    pallas_call x1, Pallas kernels, near_part(): pl.pallas_call(near_kernel, name='near_part', out_shape=[shaped(LEAVES, 4...  30.2 us
    pallas_call x2, Pallas kernels, self_part(): pl.pallas_call(self_kernel, name='self_part', grid=(count // block,), out...  27.5 us
    ppermute x8, starting transfers between devices, moved_by(): return lax.ppermute(value, ('slab', 'sub'), pairs)  23.1 us
    pallas_call x1, Pallas kernels, front(): pl.pallas_call(front_kernel, name='front', out_shape=[shaped(LEAVES, 4, L...  7.59 us
    pallas_call x1, Pallas kernels, last(): pl.pallas_call(last_kernel, name='last', out_shape=shaped(4, LEAVES * LEA...  6.94 us
    unnamed x22, local copies, waits for them, and re-layouts  6.14 us
    pallas_call x1, Pallas kernels, far_part(): pl.pallas_call(far_kernel, name='far_part', out_shape=[shaped(40, LEAVES)...  3.02 us
  transfers between devices with their start and end apart: 8, of which 0 were waited for; matrix products, arithmetic and copies ran while one was open for 0% of the time, Pallas kernels for 26%

profile of v2, /device:TPU:1, one launch (start us, length us, event | category | flops | bytes accessed | tf_op | source)
XLA Modules:
  0.0 106.7 jit_solution(10819978214072294045)
XLA Ops:
  0.0 0.0 copy-start.2
  0.0 0.5 broadcast.13
  0.5 0.2 copy-done.2
  0.7 0.7 reduce.7
  1.4 0.1 reshape_squeeze.6
  1.4 0.6 copy-done.8
  2.0 0.7 reduce.6
  2.7 0.1 reshape_squeeze.7
  2.8 0.1 pad.18.clone
  2.8 0.1 pad_add_fusion.1.at_ref
  2.9 0.1 add_add_fusion.ids_ref
  3.0 0.0 copy-start.3
  3.0 0.7 copy-done.3
  3.7 0.0 copy-start
  3.7 1.2 %copy-done = f32[3,65536]{1,0:T(4,128)S(1)} copy-done((f32[3,65536]{1,0:T(4,128)S(1)}, f32[3,65536]{1,0:T(4,128)}, u32[]{:S(2)}) %copy-start) | copy-done | bytes 786456
  4.9 0.0 copy-start.1
  4.9 0.9 copy-done.1
  5.8 7.6 %front.1 = (f32[256,4,256]{2,1,0:T(4,128)S(1)}, f32[40,256]{1,0:T(8,128)S(1)}, f32[40,128]{1,0:T(8,128)S(1)}, f32[69,4,256]{2,1,0:T(4,128)S(1)}, f32[69,4,256]{2...) custom-call(s32[2]{0:T(128)S(1)} %pad_add_fusion.1.at_ref, s32[256]{0:T(256)S(1)} %copy-done.3, ...), custom_call_target="tpu_custom_call" | custom-call | tf_op jit(solution)/shard_map/front/pallas_call | solution.py:247
  13.4 1.4 %collective-permute-start = (f32[69,4,256]{2,1,0:T(4,128)S(1)}, f32[69,4,256]{2,1,0:T(4,128)S(1)}, u32[]{:S(2)}, u32[]{:S(2)}) collective-permute-start(f32[69,4,256]{2,1,0:T(4,128)S(1)} %get-tuple-element.24), channel_id=1, source_target_pairs={{0,112},{1,113},{2,114},{3,115},{4,116},{5,117},{6,118},{7,119},{8... | collective-permute-start | bytes 847880 | tf_op jit(solution)/shard_map/ppermute | solution.py:798
  14.9 6.0 %collective-permute-start.1 = (f32[69,4,256]{2,1,0:T(4,128)S(1)}, f32[69,4,256]{2,1,0:T(4,128)S(1)}, u32[]{:S(2)}, u32[]{:S(2)}) collective-permute-start(f32[69,4,256]{2,1,0:T(4,128)S(1)} %get-tuple-element.25), channel_id=1, source_target_pairs={{0,15},{1,0},{2,1},{3,2},{4,3},{5,4},{6,5},{7,6},{8,7},{9,8},{10,9... | collective-permute-start | bytes 847880 | tf_op jit(solution)/shard_map/ppermute | solution.py:798
  20.9 3.2 %collective-permute-start.2 = (f32[69,4,256]{2,1,0:T(4,128)S(1)}, f32[69,4,256]{2,1,0:T(4,128)S(1)}, u32[]{:S(2)}, u32[]{:S(2)}) collective-permute-start(f32[69,4,256]{2,1,0:T(4,128)S(1)} %get-tuple-element.26), channel_id=1, source_target_pairs={{0,127},{1,112},{2,113},{3,114},{4,115},{5,116},{6,117},{7,118},{8... | collective-permute-start | bytes 847880 | tf_op jit(solution)/shard_map/ppermute | solution.py:798
  24.1 1.0 collective-permute-start.3
  25.1 0.0 copy-start.4
  25.1 0.7 copy-done.5
  25.8 0.0 copy-done.4
  25.8 0.7 copy-done.6
  26.5 13.8 %self_part.2.self0_ref = f32[128,4,256]{2,1,0:T(4,128)S(1)} custom-call(f32[256,4,256]{2,1,0:T(4,128)S(1)} %get-tuple-element.21.own_ref), custom_call_target="tpu_custom_call" | custom-call | flops 5120000000 | bytes 1048576 | tf_op jit(solution)/shard_map/self_part/pallas_call | solution.py:346
  40.3 0.1 add_bitcast_fusion
  40.3 0.1 add_bitcast_fusion.1
  40.4 0.7 copy-done.7
  41.1 0.1 broadcast_in_dim.12
  41.1 0.1 pad_add_fusion.parent_ref
  41.2 0.0 collective-permute-done.in0
  41.2 0.0 collective-permute-done.1.in1
  41.2 0.0 collective-permute-done.2.in2
  41.3 0.0 collective-permute-done.3.in3
  41.3 3.0 %far_part.1 = (f32[40,256]{1,0:T(8,128)S(1)}, f32[40,128]{1,0:T(8,128)S(1)}, f32[4,40,128]{2,1,0:T(8,128)S(1)}, f32[3,256]{1,0:T(4,128)S(1)}) custom-call(f32[4,2]{1,0:T(4,128)S(1)} %add_convert_fusion.image_ref, s32[3,1024]{1,0:T(4,128)S(1)} %bitcast.27, s32[3,128]{1,0:T(4,128)S(1)} %pad_add_fusion.parent_ref, s32[3,256]{1,0:T(4,128)S(1)} %bitcast.28, ...), custom_call_target="tpu_custom_call" | custom-call | tf_op jit(solution)/shard_map/far_part/pallas_call | solution.py:612
  44.3 30.2 %near_part.1 = (f32[256,4,256]{2,1,0:T(4,128)S(1)}, f32[69,4,256]{2,1,0:T(4,128)S(1)}, f32[69,4,256]{2,1,0:T(4,128)S(1)}, f32[69,4,256]{2,1,0:T(4,128)S(1)}, f32[69,4,256]{2,1,0:T(4,128)S(1)}) custom-call(s32[3,256]{1,0:T(4,128)S(1)} %bitcast.29, f32[3,256]{1,0:T(4,128)S(1)} %get-tuple-element.28.moved_ref, f32[256,4,256]{2,1,0:T(4,128)S(1)} %get-tuple-element.21.own_ref, ...), custom_call_target="tpu_custom_call" | custom-call | flops 20480000000 | bytes 4000000 | tf_op jit(solution)/shard_map/near_part/pallas_call | solution.py:444
  74.5 0.0 collective-permute-start.4
  74.6 0.1 collective-permute-start.5
  74.7 3.4 %collective-permute-start.6 = (f32[69,4,256]{2,1,0:T(4,128)S(1)}, f32[69,4,256]{2,1,0:T(4,128)S(1)}, u32[]{:S(2)}, u32[]{:S(2)}) collective-permute-start(f32[69,4,256]{2,1,0:T(4,128)S(1)} %get-tuple-element.35), channel_id=1, source_target_pairs={{0,17},{1,18},{2,19},{3,20},{4,21},{5,22},{6,23},{7,24},{8,25},{9,... | collective-permute-start | bytes 847880 | tf_op jit(solution)/shard_map/ppermute | solution.py:798
  78.1 7.9 %collective-permute-start.7 = (f32[69,4,256]{2,1,0:T(4,128)S(1)}, f32[69,4,256]{2,1,0:T(4,128)S(1)}, u32[]{:S(2)}, u32[]{:S(2)}) collective-permute-start(f32[69,4,256]{2,1,0:T(4,128)S(1)} %get-tuple-element.36), channel_id=1, source_target_pairs={{0,31},{1,16},{2,17},{3,18},{4,19},{5,20},{6,21},{7,22},{8,23},{9,... | collective-permute-start | bytes 847880 | tf_op jit(solution)/shard_map/ppermute | solution.py:798
  86.0 13.7 %self_part.3.self1_ref = f32[128,4,256]{2,1,0:T(4,128)S(1)} custom-call(f32[256,4,256]{2,1,0:T(4,128)S(1)} %get-tuple-element.21.own_ref), custom_call_target="tpu_custom_call" | custom-call | flops 5120000000 | bytes 1048576 | tf_op jit(solution)/shard_map/self_part/pallas_call | solution.py:346
  99.7 0.0 collective-permute-done.4.in0
  99.7 0.0 collective-permute-done.5.in1
  99.8 0.0 collective-permute-done.6.in2
  99.8 0.0 collective-permute-done.7.in3
  99.8 6.9 %last.1 = f32[4,65536]{1,0:T(4,128)} custom-call(s32[256]{0:T(256)S(1)} %copy-done.3, s32[256]{0:T(256)S(1)} %bitcast.31, s32[4,128]{1,0:T(4,128)S(1)} %add_add_fusion.ids_ref, f32[256,4,256]{2,1,0:T(4,128)S(1)} %get-tuple-element.21.own_ref, f32[256,4,256]{2,1,0:T(4,128)S(1)} %get-tuple-element.30.near_ref, f32[128,4,256]{2,1,0:T(4,128)S(1)} %self_part.2.self0_ref, ...), custom_call_target="tpu_custom_call" | custom-call | tf_op jit(solution)/shard_map/last/pallas_call | solution.py:764
  (9 shorter events, 0.0 us)
Async XLA Ops:
  0.0 0.7 copy-start.2
  1.3 0.7 copy-start.8
  3.0 0.7 copy-start.3
  3.7 1.2 %copy-start = (f32[3,65536]{1,0:T(4,128)S(1)}, f32[3,65536]{1,0:T(4,128)}, u32[]{:S(2)}) copy-start(f32[3,65536]{1,0:T(4,128)} %pos_ref.1) | copy-start | bytes 2359300
  4.9 0.9 copy-start.1
  13.4 27.8 %collective-permute-start = (f32[69,4,256]{2,1,0:T(4,128)S(1)}, f32[69,4,256]{2,1,0:T(4,128)S(1)}, u32[]{:S(2)}, u32[]{:S(2)}) collective-permute-start(f32[69,4,256]{2,1,0:T(4,128)S(1)} %get-tuple-element.24), channel_id=1, source_target_pairs={{0,112},{1,113},{2,114},{3,115},{4,116},{5,117},{6,118},{7,119},{8... | collective-permute-start | bytes 847880 | tf_op jit(solution)/shard_map/ppermute | solution.py:798
  14.9 26.4 %collective-permute-start.1 = (f32[69,4,256]{2,1,0:T(4,128)S(1)}, f32[69,4,256]{2,1,0:T(4,128)S(1)}, u32[]{:S(2)}, u32[]{:S(2)}) collective-permute-start(f32[69,4,256]{2,1,0:T(4,128)S(1)} %get-tuple-element.25), channel_id=1, source_target_pairs={{0,15},{1,0},{2,1},{3,2},{4,3},{5,4},{6,5},{7,6},{8,7},{9,8},{10,9... | collective-permute-start | bytes 847880 | tf_op jit(solution)/shard_map/ppermute | solution.py:798
  20.9 20.3 %collective-permute-start.2 = (f32[69,4,256]{2,1,0:T(4,128)S(1)}, f32[69,4,256]{2,1,0:T(4,128)S(1)}, u32[]{:S(2)}, u32[]{:S(2)}) collective-permute-start(f32[69,4,256]{2,1,0:T(4,128)S(1)} %get-tuple-element.26), channel_id=1, source_target_pairs={{0,127},{1,112},{2,113},{3,114},{4,115},{5,116},{6,117},{7,118},{8... | collective-permute-start | bytes 847880 | tf_op jit(solution)/shard_map/ppermute | solution.py:798
  24.1 17.2 %collective-permute-start.3 = (f32[69,4,256]{2,1,0:T(4,128)S(1)}, f32[69,4,256]{2,1,0:T(4,128)S(1)}, u32[]{:S(2)}, u32[]{:S(2)}) collective-permute-start(f32[69,4,256]{2,1,0:T(4,128)S(1)} %get-tuple-element.27), channel_id=1, source_target_pairs={{0,113},{1,114},{2,115},{3,116},{4,117},{5,118},{6,119},{7,120},{8... | collective-permute-start | bytes 847880 | tf_op jit(solution)/shard_map/ppermute | solution.py:798
  25.1 0.7 copy-start.4
  25.1 0.7 copy-start.5
  25.8 0.7 copy-start.6
  40.4 0.7 copy-start.7
  74.5 25.2 %collective-permute-start.4 = (f32[69,4,256]{2,1,0:T(4,128)S(1)}, f32[69,4,256]{2,1,0:T(4,128)S(1)}, u32[]{:S(2)}, u32[]{:S(2)}) collective-permute-start(f32[69,4,256]{2,1,0:T(4,128)S(1)} %get-tuple-element.33), channel_id=1, source_target_pairs={{0,16},{1,17},{2,18},{3,19},{4,20},{5,21},{6,22},{7,23},{8,24},{9,... | collective-permute-start | bytes 847880 | tf_op jit(solution)/shard_map/ppermute | solution.py:798
  74.6 25.2 %collective-permute-start.5 = (f32[69,4,256]{2,1,0:T(4,128)S(1)}, f32[69,4,256]{2,1,0:T(4,128)S(1)}, u32[]{:S(2)}, u32[]{:S(2)}) collective-permute-start(f32[69,4,256]{2,1,0:T(4,128)S(1)} %get-tuple-element.34), channel_id=1, source_target_pairs={{0,1},{1,2},{2,3},{3,4},{4,5},{5,6},{6,7},{7,8},{8,9},{9,10},{10,1... | collective-permute-start | bytes 847880 | tf_op jit(solution)/shard_map/ppermute | solution.py:798
  74.7 25.1 %collective-permute-start.6 = (f32[69,4,256]{2,1,0:T(4,128)S(1)}, f32[69,4,256]{2,1,0:T(4,128)S(1)}, u32[]{:S(2)}, u32[]{:S(2)}) collective-permute-start(f32[69,4,256]{2,1,0:T(4,128)S(1)} %get-tuple-element.35), channel_id=1, source_target_pairs={{0,17},{1,18},{2,19},{3,20},{4,21},{5,22},{6,23},{7,24},{8,25},{9,... | collective-permute-start | bytes 847880 | tf_op jit(solution)/shard_map/ppermute | solution.py:798
  78.1 21.7 %collective-permute-start.7 = (f32[69,4,256]{2,1,0:T(4,128)S(1)}, f32[69,4,256]{2,1,0:T(4,128)S(1)}, u32[]{:S(2)}, u32[]{:S(2)}) collective-permute-start(f32[69,4,256]{2,1,0:T(4,128)S(1)} %get-tuple-element.36), channel_id=1, source_target_pairs={{0,31},{1,16},{2,17},{3,18},{4,19},{5,20},{6,21},{7,22},{8,23},{9,... | collective-permute-start | bytes 847880 | tf_op jit(solution)/shard_map/ppermute | solution.py:798

commit v3 on v2

--- a/solution.py
+++ b/solution.py
@@ -19,6 +19,8 @@
 PAY = SLOTS + 5
 SOFT = 0.0025
 WIDTH = 8
+CLASSES = (128, 192, 256)
+SORTED = 384
 slab_steps = (1, 0, 1, 1)
 sub_steps = (0, 1, 1, -1)
 f32 = jnp.float32
@@ -78,6 +80,28 @@
 def onehot_rows(count, ids):
     hit = iota((count, ids.shape[1]), 0) == ids
     return jnp.where(hit, 1.0, 0.0).astype(bf16)
+
+
+def fetch_all(moves, sem):
+    copies = [
+        pltpu.make_async_copy(source, target, sem.at[n])
+        for n, (source, target) in enumerate(moves)
+    ]
+    for copy in copies:
+        copy.start()
+    for copy in copies:
+        copy.wait()
+
+
+def id_row(sent_leaves, sent_parents, q):
+    return jnp.concatenate(
+        [
+            sent_leaves[:, q * SLOTS : (q + 1) * SLOTS],
+            sent_parents[:, q * PSLOTS : (q + 1) * PSLOTS],
+            jnp.full((1, 128 - SLOTS - PSLOTS), -1, jnp.int32),
+        ],
+        1,
+    )
 
 
 def put_slab(slab_ref, c, slab):
@@ -134,10 +158,15 @@
 
 
 def front_kernel(
-    at_ref, counts_ref, send_ref, ids_ref, pos_ref, mass_ref,
-    own_ref, cells_ref, pcells_ref, pay0, pay1, pay2, pay3, slab_ref, turned_ref,
+    at_ref, counts_row, sent_leaves, sent_parents, counts_hbm, send_hbm, pos_hbm, mass_hbm,
+    own_ref, cells_ref, pcells_ref, pay0, pay1, pay2, pay3,
+    slab_ref, turned_ref, pos_ref, mass_ref, counts_ref, send_ref, sem,
 ):
     pays = (pay0, pay1, pay2, pay3)
+    fetch_all(
+        ((counts_hbm, counts_ref), (send_hbm, send_ref), (pos_hbm, pos_ref), (mass_hbm, mass_ref)),
+        sem,
+    )
     base_x = at_ref[0] * CX
     base_y = at_ref[1] * CY
     row4 = iota((4, LEAF), 0)
@@ -184,7 +213,8 @@
     cells_ref[35:36, :] = (base_x + cell_x).astype(f32) + 0.5
     cells_ref[36:37, :] = (base_y + cell_y).astype(f32) + 0.5
     cells_ref[37:38, :] = cell_z.astype(f32) + 0.5
-    cells_ref[38:40, :] = jnp.zeros((2, LEAVES), f32)
+    cells_ref[38:39, :] = counts_row[...].astype(f32)
+    cells_ref[39:40, :] = jnp.zeros((1, LEAVES), f32)
 
     moments = {alpha: cells_ref[n : n + 1, :] for n, alpha in enumerate(ALPHAS)}
     moved = shift_moments(moments, parent_offsets())
@@ -210,11 +240,11 @@
         pay = pays[q]
 
         def copy_leaf(k, _, pay=pay, q=q):
-            pay[k] = own_ref[send_ref[q * SLOTS + k]]
+            pay[k] = own_ref[send_ref[0, q * SLOTS + k]]
             return 0
 
         lax.fori_loop(0, SLOTS, copy_leaf, 0, unroll=8)
-        ids = ids_ref[q : q + 1, :]
+        ids = id_row(sent_leaves, sent_parents, q)
         leaf_hot = onehot_rows(LEAVES, jnp.where(lane128 < SLOTS, ids, -1))
         parent_hot = onehot_rows(128, jnp.where(lane128 >= SLOTS, ids, -1))
         block = pick(cells_ref[...], leaf_hot) + pick(pcells, parent_hot)
@@ -236,6 +266,7 @@
 VM = pl.BlockSpec(memory_space=pltpu.VMEM)
 SM = pl.BlockSpec(memory_space=pltpu.SMEM)
 HB = pl.BlockSpec(memory_space=pl.ANY)
+HBM = pl.BlockSpec(memory_space=pltpu.MemorySpace.HBM)
 PARAMS = dict(vmem_limit_bytes=48 * 1024 * 1024)
 
 
@@ -243,21 +274,29 @@
     return jax.ShapeDtypeStruct(shape, f32)
 
 
-def front(at, counts, send, ids, positions, masses):
+def front(at, counts, send_leaves, send_parents, positions, masses):
     return pl.pallas_call(
         front_kernel,
         name="front",
         out_shape=[
             shaped(LEAVES, 4, LEAF), shaped(40, LEAVES), shaped(40, 128),
         ] + [shaped(PAY, 4, LEAF)] * 4,
-        in_specs=[SM, SM, SM, VM, VM, VM],
+        in_specs=[SM, VM, VM, VM, HBM, HBM, HBM, HBM],
         out_specs=[VM] * 7,
         scratch_shapes=[
             pltpu.VMEM((LEAVES * 16, 128), f32),
             pltpu.VMEM((4, LEAF, LEAVES), f32),
+            pltpu.VMEM((3, LEAVES * LEAF), f32),
+            pltpu.VMEM((LEAVES * 2, 128), f32),
+            pltpu.SMEM((LEAVES,), jnp.int32),
+            pltpu.SMEM((1, 4 * SLOTS), jnp.int32),
+            pltpu.SemaphoreType.DMA((4,)),
         ],
         compiler_params=pltpu.CompilerParams(**PARAMS),
-    )(at, counts, send, ids, positions, masses)
+    )(
+        at, counts.reshape(1, LEAVES), send_leaves, send_parents, counts, send_leaves, positions,
+        masses.reshape(-1, 128),
+    )
 
 
 def slab8(slab):
@@ -307,10 +346,11 @@
 def finish(total, points):
     row = iota(points.shape, 0)
     mass = total[0:1]
-    square = b_form(points)[4:5]
-    along = jnp.sum(jnp.where((row >= 1) & (row <= 3), points * total, 0.0), 0, keepdims=True)
-    potential = total[4:5] + (square + SOFT) * mass - 2.0 * along
-    return jnp.where(row == 0, -potential, total - points * mass)[0:4]
+    pushed = points * mass
+    terms = jnp.where(row == 0, SOFT * total, points * (pushed - 2.0 * total))
+    terms = jnp.where(row == 4, total, terms)
+    potential = jnp.sum(terms, 0, keepdims=True)
+    return jnp.where(row == 0, -potential, total - pushed)[0:4]
 
 
 def load_points(slab):
@@ -358,8 +398,8 @@
 
 
 def near_kernel(
-    pairs_ref, moved_ref, own_ref, in0, in1, in2, in3, backs_ref,
-    out_ref, pay0, pay1, pay2, pay3, table, total, sem,
+    list_ref, own_ref, in0, in1, in2, in3, backs_ref,
+    out_ref, pay0, pay1, pay2, pay3, table, total, shifts, sem, *held,
 ):
     pays = (pay0, pay1, pay2, pay3)
     copies = [pltpu.make_async_copy(own_ref, table.at[pl.ds(0, LEAVES)], sem.at[0])]
@@ -378,50 +418,71 @@
         total[c] = jnp.zeros((8, LEAF), f32)
         return 0
 
-    lax.fori_loop(0, 2 * LEAVES, clear, 0, unroll=8)
+    lax.fori_loop(0, 2 * LEAVES + 8, clear, 0, unroll=8)
+    row = iota((8, 128), 0)
+    for code in range(27):
+        step = (code % 3 - 1, code // 3 % 3 - 1, code // 9 - 1)
+        value = jnp.zeros((8, 128), f32)
+        for k in range(3):
+            value = jnp.where(row == k + 1, float(step[k]), value)
+        shifts[code] = value
     for copy in copies:
         copy.wait()
 
-    row = iota((8, LEAF), 0)
-
-    def some_pairs(step, _):
-        first = step * WIDTH
-        ends, loaded = [], []
-        for k in range(WIDTH):
-            p = first + k
-            a = pairs_ref[0, p]
-            listed = pairs_ref[1, p]
-            b = jnp.maximum(listed, 0)
-            used = jnp.where(listed >= 0, 1.0, 0.0)
-            points_a, weight_a = load_points(table[a])
-            points_b, weight_b = load_points(table[b])
-            shift = jnp.where(
-                row == 1,
-                moved_ref[0, p],
-                jnp.where(row == 2, moved_ref[1, p], jnp.where(row == 3, moved_ref[2, p], 0.0)),
-            )
-            ends.append((a, b))
-            loaded.append((points_a + shift, weight_a * used, points_b, weight_b * used, shift))
-        spaced = [squares(from_b, points_b) for from_b, _, points_b, _, _ in loaded]
-        high = []
-        for value in spaced:
-            inverse = lax.rsqrt(value)
-            high.append((inverse * inverse * inverse).astype(bf16))
-        done = []
-        for (from_b, weight_a, points_b, weight_b, shift), cube in zip(loaded, high):
-            to_b = fold(dot_nn(sources(from_b, weight_a), cube))
-            to_a = fold(dot_nt(sources(points_b - shift, weight_b), cube))
-            done.append((to_a, to_b))
-        for (a, b), (to_a, to_b) in zip(ends, done):
-            total[a] = total[a] + to_a
-            total[b] = total[b] + to_b
-        return 0
-
-    def count_used(p, n):
-        return n + jnp.where(pairs_ref[1, p] >= 0, 1, 0)
-
-    used_pairs = lax.fori_loop(0, NEAR, count_used, 0)
-    lax.fori_loop(0, (used_pairs + WIDTH - 1) // WIDTH, some_pairs, 0)
+    def decode(group, k):
+        code = list_ref[0, group * WIDTH + k]
+        value = jnp.maximum(code - 1, 0)
+        return value & 511, (value >> 9) & 511, value >> 18, code > 0
+
+    def shift_of(code):
+        half = shifts[code]
+        return jnp.concatenate([half, half], 1)
+
+    def spaced(group, k, rows):
+        r, c, code, _ = decode(group, k)
+        points_r, _ = load_points(table[r])
+        points_c, _ = load_points(table[c])
+        return squares((points_r + shift_of(code))[:, :rows], points_c)
+
+    def keep(k, rows, value):
+        inverse = lax.rsqrt(value)
+        held[k][0:rows, :] = (inverse * inverse * inverse).astype(bf16)
+
+    def products(group, k, rows):
+        r, c, code, live = decode(group, k)
+        points_r, weight_r = load_points(table[r])
+        points_c, weight_c = load_points(table[c])
+        shift = shift_of(code)
+        cube = held[k][0:rows, :]
+        side_r = sources((points_r + shift)[:, :rows], weight_r[:, :rows])
+        to_c = fold(dot_nn(side_r, cube))
+        to_r = fold(dot_nt(sources(points_c - shift, weight_c), cube))
+        return jnp.where(live, r, 2 * LEAVES), jnp.where(live, c, 2 * LEAVES), to_r, to_c
+
+    def settle(done, rows):
+        for r, c, to_r, to_c in done:
+            total[r, :, 0:rows] = total[r, :, 0:rows] + to_r
+            total[c] = total[c] + to_c
+
+    for n, rows in enumerate(CLASSES):
+        first = list_ref[1, n]
+        end = list_ref[1, n + 1]
+
+        @pl.when(end > first)
+        def _(first=first, end=end, rows=rows):
+            for k in range(WIDTH):
+                keep(k, rows, spaced(first, k, rows))
+
+            def advance(group, _):
+                done = []
+                for k in range(WIDTH):
+                    done.append(products(group, k, rows))
+                    keep(k, rows, spaced(group + 1, k, rows))
+                settle(done, rows)
+                return 0
+
+            lax.fori_loop(first, end - 1, advance, 0)
+            settle([products(end - 1, k, rows) for k in range(WIDTH)], rows)
 
     def finish_own(c, _):
         points, _ = load_points(table[c])
@@ -440,23 +501,44 @@
         put_block(pays[q], backs_ref[q])
 
 
-def near_part(pairs, moved, own, incoming, backs):
+def near_part(ordered, own, incoming, backs):
     return pl.pallas_call(
         near_kernel,
         name="near_part",
         out_shape=[shaped(LEAVES, 4, LEAF)] + [shaped(PAY, 4, LEAF)] * 4,
-        in_specs=[SM, SM, HB, HB, HB, HB, HB, VM],
+        in_specs=[SM, HB, HB, HB, HB, HB, VM],
         out_specs=[VM] * 5,
         scratch_shapes=[
             pltpu.VMEM((2 * LEAVES, 4, LEAF), f32),
-            pltpu.VMEM((2 * LEAVES, 8, LEAF), f32),
+            pltpu.VMEM((2 * LEAVES + 8, 8, LEAF), f32),
+            pltpu.VMEM((27, 8, 128), f32),
             pltpu.SemaphoreType.DMA((5,)),
-        ],
+        ] + [pltpu.VMEM((LEAF, LEAF), bf16)] * WIDTH,
         cost_estimate=pl.CostEstimate(
             flops=NEAR * 80_000_000, bytes_accessed=4_000_000, transcendentals=0
         ),
         compiler_params=pltpu.CompilerParams(**PARAMS),
-    )(pairs, moved, own, *incoming, backs)
+    )(ordered, own, *incoming, backs)
+
+
+def sort_lists(code, group, out_ref):
+    count = code.shape[1]
+    hot = jnp.where(iota((8, count), 0) == group, 1.0, 0.0)
+    earlier = jnp.where(iota((count, count), 0) < iota((count, count), 1), 1.0, 0.0).astype(bf16)
+    before = dot_nn(hot.astype(bf16), earlier)
+    members = jnp.sum(hot, 1, keepdims=True)
+    lane = iota((1, SORTED), 1)
+    place = jnp.zeros((1, count), f32)
+    groups = jnp.zeros((1, 1), f32)
+    ends = jnp.zeros((1, SORTED), f32)
+    for n in range(len(CLASSES)):
+        place = place + hot[n : n + 1] * (before[n : n + 1] + groups * WIDTH)
+        groups = groups + jnp.floor((members[n : n + 1] + (WIDTH - 1)) * (1.0 / WIDTH))
+        ends = jnp.where(lane == n + 1, groups, ends)
+    place = jnp.where(group >= 0, place, -1.0).astype(jnp.int32)
+    ordered = pick(jnp.broadcast_to(code, (8, count)), onehot_rows(SORTED, place), True)
+    out_ref[0:1, :] = ordered[0:1].astype(jnp.int32)
+    out_ref[1:2, :] = ends.astype(jnp.int32)
 
 
 def derivatives(x, y, z):
@@ -514,7 +596,7 @@
 
 def far_kernel(
     image_ref, far_ref, parent_ref, near_ref, cells_ref, pcells_ref, in0, in1, in2, in3,
-    leaf_ref, par_ref, backs_ref, moved_ref, tails, table, left, right, to_a, to_b, total, sem,
+    leaf_ref, par_ref, backs_ref, ordered_ref, tails, table, left, right, to_a, to_b, total, sem,
 ):
     copies = []
     for q, part in enumerate((in0, in1, in2, in3)):
@@ -585,22 +667,39 @@
 
     for g in range(FAR // 128):
         lanes = slice(g * 128, g * 128 + 128)
-        load(far_ref[0:1, lanes], far_ref[1:2, lanes], far_ref[2:3, lanes], g, False)
+        load(far_ref[0, :, lanes], far_ref[1, :, lanes], far_ref[2, :, lanes], g, False)
     mutual(left, right, to_a, to_b)
     for g in range(FAR // 128):
         lanes = slice(g * 128, g * 128 + 128)
-        store(far_ref[0:1, lanes], far_ref[1:2, lanes], g, False)
-    load(parent_ref[0:1, :], parent_ref[1:2, :], parent_ref[2:3, :], 0, True)
+        store(far_ref[0, :, lanes], far_ref[1, :, lanes], g, False)
+    ids_a, ids_b, lifts = [
+        jnp.concatenate([parent_ref[k], jnp.full((1, 128 - PFAR), -(k == 1), jnp.int32)], 1)
+        for k in range(3)
+    ]
+    load(ids_a, ids_b, lifts, 0, True)
     mutual(left, right, to_a, to_b)
-    store(parent_ref[0:1, :], parent_ref[1:2, :], 0, True)
-
-    for g in range(NEAR // 128):
-        lanes = slice(g * 128, g * 128 + 128)
-        hot_a, _, _, hot_b, _, _ = hots(near_ref[0:1, lanes], near_ref[1:2, lanes], False)
-        apart = gathered(hot_a, 0, LEAVES) - gathered(hot_b, 0, 768)
-        apart = jnp.where(row == 37, apart - near_ref[2:3, lanes].astype(f32) * float(CZ), apart)
-        for k in range(3):
-            moved_ref[k : k + 1, lanes] = apart[35 + k : 36 + k, :]
+    store(ids_a, ids_b, 0, True)
+
+    ids_a, ids_b, lifts = near_ref[0], near_ref[1], near_ref[2]
+    hot_a, _, _, hot_b, _, _ = hots(ids_a, ids_b, False)
+    from_a = gathered(hot_a, 0, LEAVES)[35:39]
+    from_b = gathered(hot_b, 0, 768)[35:39]
+    count_a, count_b = from_a[3:4], from_b[3:4]
+    fewer = jnp.minimum(count_a, count_b)
+    swap = count_b < count_a
+    group = jnp.where(fewer <= 128.0, 0, jnp.where(fewer <= 192.0, 1, 2))
+    group = jnp.where(ids_b >= 0, group, -1)
+    moved = jnp.zeros((1, NEAR), f32)
+    for k in range(3):
+        apart = from_a[k : k + 1] - from_b[k : k + 1]
+        if k == 2:
+            apart = apart - lifts.astype(f32) * float(CZ)
+        apart = jnp.where(swap, -apart, apart)
+        moved = moved + (apart + 1.0) * float(3**k)
+    rows = jnp.where(swap, ids_b, ids_a)
+    columns = jnp.where(swap, ids_a, ids_b)
+    code = 1.0 + rows.astype(f32) + columns.astype(f32) * 512.0 + moved * 262144.0
+    sort_lists(jnp.where(ids_b >= 0, code, 0.0), group, ordered_ref)
 
     leaf_ref[...] = total[:, 0:LEAVES]
     par_ref[...] = total[:, LEAVES + 512 :]
@@ -613,7 +712,8 @@
         far_kernel,
         name="far_part",
         out_shape=[
-            shaped(40, LEAVES), shaped(40, 128), shaped(4, 40, 128), shaped(3, NEAR),
+            shaped(40, LEAVES), shaped(40, 128), shaped(4, 40, 128),
+            jax.ShapeDtypeStruct((2, SORTED), jnp.int32),
         ],
         in_specs=[SM, VM, VM, VM, VM, VM, HB, HB, HB, HB],
         out_specs=[VM] * 4,
@@ -625,7 +725,10 @@
             pltpu.SemaphoreType.DMA((4,)),
         ],
         compiler_params=pltpu.CompilerParams(**PARAMS),
-    )(image, far, parent, near, cells, pcells, *incoming)
+    )(
+        image, far.transpose(1, 0, 2), parent.transpose(1, 0, 2), near.transpose(1, 0, 2),
+        cells, pcells, *incoming,
+    )
 
 
 def shift_terms(terms, offsets):
@@ -659,7 +762,7 @@
 
 
 def last_kernel(
-    counts_ref, send_ref, ids_ref, own_ref, near_ref, self0_ref, self1_ref, leaf_ref, par_ref,
+    counts_ref, send_ref, sent_leaves, sent_parents, own_ref, near_ref, self0_ref, self1_ref, leaf_ref, par_ref,
     in0, in1, in2, in3, out_ref, slab_ref, turned_ref, terms_ref, field_ref, near_sum,
 ):
     incoming = (in0, in1, in2, in3)
@@ -682,14 +785,14 @@
     par = par_ref[...]
     for q in range(4):
         block = get_block(lambda s, q=q: incoming[q][SLOTS + s])
-        ids = ids_ref[q : q + 1, :]
+        ids = id_row(sent_leaves, sent_parents, q)
         leaf_hot = onehot_rows(LEAVES, jnp.where(lane128 < SLOTS, ids, -1))
         parent_hot = onehot_rows(128, jnp.where(lane128 >= SLOTS, ids, -1))
         leaf = leaf + pick(block, leaf_hot, True)
         par = par + pick(block, parent_hot, True)
 
         def arrive(k, _, q=q):
-            c = send_ref[q * SLOTS + k]
+            c = send_ref[0, q * SLOTS + k]
             near_sum[c] = near_sum[c] + incoming[q][k]
             return 0
 
@@ -760,12 +863,12 @@
     lax.fori_loop(0, LEAVES, write, 0, unroll=8)
 
 
-def last(counts, send, ids, own, near, self0, self1, leaf, par, arrived):
+def last(counts, send_leaves, send_parents, own, near, self0, self1, leaf, par, arrived):
     return pl.pallas_call(
         last_kernel,
         name="last",
         out_shape=shaped(4, LEAVES * LEAF),
-        in_specs=[SM, SM] + [VM] * 11,
+        in_specs=[SM, SM] + [VM] * 12,
         out_specs=VM,
         scratch_shapes=[
             pltpu.VMEM((LEAVES * 16, 128), f32),
@@ -775,7 +878,9 @@
             pltpu.VMEM((LEAVES, 4, LEAF), f32),
         ],
         compiler_params=pltpu.CompilerParams(**PARAMS),
-    )(counts, send, ids, own, near, self0, self1, leaf, par, *arrived)
+    )(
+        counts, send_leaves, send_leaves, send_parents, own, near, self0, self1, leaf, par, *arrived
+    )
 
 
 def image_shift(slab_at, sub_at, slab_count, sub_count):
@@ -798,24 +903,6 @@
     return lax.ppermute(value, ("slab", "sub"), pairs)
 
 
-def id_table(send_leaves, send_parents):
-    return jnp.concatenate(
-        [
-            send_leaves.reshape(4, SLOTS),
-            send_parents.reshape(4, PSLOTS),
-            jnp.full((4, 128 - SLOTS - PSLOTS), -1, jnp.int32),
-        ],
-        1,
-    )
-
-
-def pad_pairs(pairs):
-    filler = jnp.broadcast_to(
-        jnp.array([[0], [-1], [0]], jnp.int32), (3, 128 - pairs.shape[1])
-    )
-    return jnp.concatenate([pairs, filler], 1)
-
-
 def on_device(
     positions, masses, leaf_counts, send_leaves, send_parents, near_pairs, far_pairs, parent_pairs
 ):
@@ -824,10 +911,8 @@
     slab_at = lax.axis_index("slab")
     sub_at = lax.axis_index("sub")
     at = jnp.stack([slab_at, sub_at]).astype(jnp.int32)
-    send = send_leaves[0]
-    ids = id_table(send, send_parents[0])
     own, cells, pcells, *outgoing = front(
-        at, leaf_counts, send, ids, positions, masses.reshape(-1, 128)
+        at, leaf_counts, send_leaves, send_parents, positions, masses
     )
     incoming = [
         moved_by(outgoing[q], -slab_steps[q], -sub_steps[q], slab_count, sub_count)
@@ -835,16 +920,16 @@
     ]
     image = image_shift(slab_at, sub_at, slab_count, sub_count)
     self0 = self_part(own, 0, LEAVES // 2)
-    leaf, par, backs, moved = far_part(
-        image, far_pairs[0], pad_pairs(parent_pairs[0]), near_pairs[0], cells, pcells, incoming
-    )
-    near, *returning = near_part(near_pairs[0], moved, own, incoming, backs)
+    leaf, par, backs, ordered = far_part(
+        image, far_pairs, parent_pairs, near_pairs, cells, pcells, incoming
+    )
+    near, *returning = near_part(ordered, own, incoming, backs)
     arrived = [
         moved_by(returning[q], slab_steps[q], sub_steps[q], slab_count, sub_count)
         for q in range(4)
     ]
     self1 = self_part(own, LEAVES // 2, LEAVES // 2)
-    return last(leaf_counts, send, ids, own, near, self0, self1, leaf, par, arrived)
+    return last(leaf_counts, send_leaves, send_parents, own, near, self0, self1, leaf, par, arrived)
 
 
 def solution(mesh):

time: 107 us -> 90.2 us (0.84)
  Pallas kernels: 75.3 us -> 66.8 us
  starting transfers between devices: 23.1 us -> 19.2 us
  local copies, waits for them, and re-layouts: 6.46 us -> 3.55 us
  other arithmetic: 1.72 us -> 0.24 us
    pallas_call x1, Pallas kernels: 30.2 us -> 20.6 us  [near_part(): pl.pallas_call(near_kernel, name='near_part', out_shape=[shaped(LEAVES, 4...]
    ppermute x8, starting transfers between devices: 23.1 us -> 19.2 us  [moved_by(): return lax.ppermute(value, ('slab', 'sub'), pairs)]
    unnamed x22 -> x16, local copies, waits for them, and re-layouts: 6.14 us -> 3.55 us
    unnamed x2 -> x0, other arithmetic: 1.33 us -> none
  transfers between devices with their start and end apart: 8 -> 8, of which waited for: 0 -> 0; matrix products, arithmetic and copies ran while one was open for 0% -> 0% of each run, Pallas kernels for 26% -> 31%
where the time goes in v3:
time: 90.2 us; the launch traced here: 89.9 us
  Pallas kernels  66.8 us (74%)
  starting transfers between devices  19.2 us (21%)
  local copies, waits for them, and re-layouts  3.55 us (4%)
    pallas_call x2, Pallas kernels, self_part(): pl.pallas_call(self_kernel, name='self_part', grid=(count // block,), out...  27.5 us
    pallas_call x1, Pallas kernels, near_part(): pl.pallas_call(near_kernel, name='near_part', out_shape=[shaped(LEAVES, 4...  20.6 us
    ppermute x8, starting transfers between devices, moved_by(): return lax.ppermute(value, ('slab', 'sub'), pairs)  19.2 us
    pallas_call x1, Pallas kernels, front(): pl.pallas_call(front_kernel, name='front', out_shape=[shaped(LEAVES, 4, L...  8.44 us
    pallas_call x1, Pallas kernels, last(): pl.pallas_call(last_kernel, name='last', out_shape=shaped(4, LEAVES * LEA...  7.03 us
    unnamed x16, local copies, waits for them, and re-layouts  3.55 us
    pallas_call x1, Pallas kernels, far_part(): pl.pallas_call(far_kernel, name='far_part', out_shape=[shaped(40, LEAVES)...  3.27 us
  transfers between devices with their start and end apart: 8, of which 0 were waited for; matrix products, arithmetic and copies ran while one was open for 0% of the time, Pallas kernels for 31%

profile of v3, /device:TPU:1, one launch (start us, length us, event | category | flops | bytes accessed | tf_op | source)
XLA Modules:
  0.0 89.9 jit_solution(6466141572965429201)
XLA Ops:
  0.0 0.1 pad_add_fusion.at_ref
  0.1 0.0 copy-start.4
  0.1 0.0 copy-start.2
  0.1 0.0 copy-start.6
  0.1 0.7 copy-done.4
  0.8 0.0 copy-done.2
  0.8 0.0 copy-done.6
  0.8 0.0 copy-start
  0.8 1.2 %copy-done = f32[3,65536]{1,0:T(4,128)S(1)} copy-done((f32[3,65536]{1,0:T(4,128)S(1)}, f32[3,65536]{1,0:T(4,128)}, u32[]{:S(2)}) %copy-start) | copy-done | bytes 786456
  2.0 0.0 copy-start.1
  2.0 0.9 %copy-done.1 = f32[65536]{0:T(1024)S(1)} copy-done((f32[65536]{0:T(1024)S(1)}, f32[65536]{0:T(1024)}, u32[]{:S(2)}) %copy-start.1) | copy-done | bytes 262168
  3.0 8.4 %front.1 = (f32[256,4,256]{2,1,0:T(4,128)S(1)}, f32[40,256]{1,0:T(8,128)S(1)}, f32[40,128]{1,0:T(8,128)S(1)}, f32[69,4,256]{2,1,0:T(4,128)S(1)}, f32[69,4,256]{2...) custom-call(s32[2]{0:T(128)S(1)} %pad_add_fusion.at_ref, s32[1,256]{1,0:T(1,128)S(1)} %bitcast.22, ...), custom_call_target="tpu_custom_call" | custom-call | tf_op jit(solution)/shard_map/front/pallas_call | solution.py:278
  11.4 1.4 %collective-permute-start = (f32[69,4,256]{2,1,0:T(4,128)S(1)}, f32[69,4,256]{2,1,0:T(4,128)S(1)}, u32[]{:S(2)}, u32[]{:S(2)}) collective-permute-start(f32[69,4,256]{2,1,0:T(4,128)S(1)} %get-tuple-element.24), channel_id=1, source_target_pairs={{0,112},{1,113},{2,114},{3,115},{4,116},{5,117},{6,118},{7,119},{8... | collective-permute-start | bytes 847880 | tf_op jit(solution)/shard_map/ppermute | solution.py:903
  12.8 6.0 %collective-permute-start.1 = (f32[69,4,256]{2,1,0:T(4,128)S(1)}, f32[69,4,256]{2,1,0:T(4,128)S(1)}, u32[]{:S(2)}, u32[]{:S(2)}) collective-permute-start(f32[69,4,256]{2,1,0:T(4,128)S(1)} %get-tuple-element.25), channel_id=1, source_target_pairs={{0,15},{1,0},{2,1},{3,2},{4,3},{5,4},{6,5},{7,6},{8,7},{9,8},{10,9... | collective-permute-start | bytes 847880 | tf_op jit(solution)/shard_map/ppermute | solution.py:903
  18.9 3.2 %collective-permute-start.2 = (f32[69,4,256]{2,1,0:T(4,128)S(1)}, f32[69,4,256]{2,1,0:T(4,128)S(1)}, u32[]{:S(2)}, u32[]{:S(2)}) collective-permute-start(f32[69,4,256]{2,1,0:T(4,128)S(1)} %get-tuple-element.26), channel_id=1, source_target_pairs={{0,127},{1,112},{2,113},{3,114},{4,115},{5,116},{6,117},{7,118},{8... | collective-permute-start | bytes 847880 | tf_op jit(solution)/shard_map/ppermute | solution.py:903
  22.0 1.0 %collective-permute-start.3 = (f32[69,4,256]{2,1,0:T(4,128)S(1)}, f32[69,4,256]{2,1,0:T(4,128)S(1)}, u32[]{:S(2)}, u32[]{:S(2)}) collective-permute-start(f32[69,4,256]{2,1,0:T(4,128)S(1)} %get-tuple-element.27), channel_id=1, source_target_pairs={{0,113},{1,114},{2,115},{3,116},{4,117},{5,118},{6,119},{7,120},{8... | collective-permute-start | bytes 847880 | tf_op jit(solution)/shard_map/ppermute | solution.py:903
  23.1 13.7 %self_part.2.self0_ref = f32[128,4,256]{2,1,0:T(4,128)S(1)} custom-call(f32[256,4,256]{2,1,0:T(4,128)S(1)} %get-tuple-element.21.own_ref), custom_call_target="tpu_custom_call" | custom-call | flops 5120000000 | bytes 1048576 | tf_op jit(solution)/shard_map/self_part/pallas_call | solution.py:386
  36.8 0.1 add_bitcast_fusion
  36.9 0.0 copy-start.3
  36.9 0.1 add_bitcast_fusion.1
  37.0 0.0 collective-permute-done.in0
  37.0 0.0 collective-permute-done.1.in1
  37.0 0.0 collective-permute-done.2.in2
  37.0 0.0 collective-permute-done.3.in3
  37.0 0.0 copy-start.5
  37.0 0.0 copy-start.7
  37.0 0.5 copy-done.3
  37.6 0.1 copy-done.5
  37.7 0.0 copy-done.7
  37.7 3.3 %far_part.1 = (f32[40,256]{1,0:T(8,128)S(1)}, f32[40,128]{1,0:T(8,128)S(1)}, f32[4,40,128]{2,1,0:T(8,128)S(1)}, s32[2,384]{1,0:T(2,128)S(1)}) custom-call(f32[4,2]{1,0:T(4,128)S(1)} %add_convert_fusion.image_ref, s32[3,1,1024]{2,1,0:T(1,128)S(1)} %bitcast.21, s32[3,1,64]{2,1,0:T(1,128)S(1)} %bitcast.24, s32[3,1,256]{2,1,0:T(1,128)S(1)} %bitcast.23, ...), custom_call_target="tpu_custom_call" | custom-call | tf_op jit(solution)/shard_map/far_part/pallas_call | solution.py:711
  41.0 20.6 %near_part.1 = (f32[256,4,256]{2,1,0:T(4,128)S(1)}, f32[69,4,256]{2,1,0:T(4,128)S(1)}, f32[69,4,256]{2,1,0:T(4,128)S(1)}, f32[69,4,256]{2,1,0:T(4,128)S(1)}, f32[69,4,256]{2,1,0:T(4,128)S(1)}) custom-call(s32[2,384]{1,0:T(2,128)S(1)} %get-tuple-element.28.list_ref, f32[256,4,256]{2,1,0:T(4,128)S(1)} %get-tuple-element.21.own_ref, ...), custom_call_target="tpu_custom_call" | custom-call | flops 20480000000 | bytes 4000000 | tf_op jit(solution)/shard_map/near_part/pallas_call | solution.py:505
  61.6 0.0 collective-permute-start.4
  61.6 0.2 collective-permute-start.5
  61.8 0.0 collective-permute-start.6
  61.8 7.3 %collective-permute-start.7 = (f32[69,4,256]{2,1,0:T(4,128)S(1)}, f32[69,4,256]{2,1,0:T(4,128)S(1)}, u32[]{:S(2)}, u32[]{:S(2)}) collective-permute-start(f32[69,4,256]{2,1,0:T(4,128)S(1)} %get-tuple-element.36), channel_id=1, source_target_pairs={{0,31},{1,16},{2,17},{3,18},{4,19},{5,20},{6,21},{7,22},{8,23},{9,... | collective-permute-start | bytes 847880 | tf_op jit(solution)/shard_map/ppermute | solution.py:903
  69.1 13.7 %self_part.3.self1_ref = f32[128,4,256]{2,1,0:T(4,128)S(1)} custom-call(f32[256,4,256]{2,1,0:T(4,128)S(1)} %get-tuple-element.21.own_ref), custom_call_target="tpu_custom_call" | custom-call | flops 5120000000 | bytes 1048576 | tf_op jit(solution)/shard_map/self_part/pallas_call | solution.py:386
  82.9 0.0 collective-permute-done.4.in0
  82.9 0.0 collective-permute-done.5.in1
  82.9 0.0 collective-permute-done.6.in2
  82.9 0.0 collective-permute-done.7.in3
  82.9 7.0 %last.1 = f32[4,65536]{1,0:T(4,128)} custom-call(s32[256]{0:T(256)S(1)} %copy-done.4, s32[1,256]{1,0:T(1,128)S(1)} %copy-done.2, s32[1,256]{1,0:T(1,128)S(1)} %copy-done.2, s32[1,64]{1,0:T(1,128)S(1)} %copy-done.6, f32[256,4,256]{2,1,0:T(4,128)S(1)} %get-tuple-element.21.own_ref, f32[256,4,256]{2,1,0:T(4,128)S(1)} %get-tuple-element.30.near_ref, ...), custom_call_target="tpu_custom_call" | custom-call | tf_op jit(solution)/shard_map/last/pallas_call | solution.py:867
  (1 shorter events, 0.0 us)
Async XLA Ops:
  0.1 0.7 copy-start.4
  0.1 0.7 copy-start.2
  0.1 0.7 copy-start.6
  0.8 1.2 %copy-start = (f32[3,65536]{1,0:T(4,128)S(1)}, f32[3,65536]{1,0:T(4,128)}, u32[]{:S(2)}) copy-start(f32[3,65536]{1,0:T(4,128)} %pos_hbm.1) | copy-start | bytes 2359300
  2.0 0.9 %copy-start.1 = (f32[65536]{0:T(1024)S(1)}, f32[65536]{0:T(1024)}, u32[]{:S(2)}) copy-start(f32[65536]{0:T(1024)} %param.9) | copy-start | bytes 786436
  11.4 25.6 %collective-permute-start = (f32[69,4,256]{2,1,0:T(4,128)S(1)}, f32[69,4,256]{2,1,0:T(4,128)S(1)}, u32[]{:S(2)}, u32[]{:S(2)}) collective-permute-start(f32[69,4,256]{2,1,0:T(4,128)S(1)} %get-tuple-element.24), channel_id=1, source_target_pairs={{0,112},{1,113},{2,114},{3,115},{4,116},{5,117},{6,118},{7,119},{8... | collective-permute-start | bytes 847880 | tf_op jit(solution)/shard_map/ppermute | solution.py:903
  12.8 24.2 %collective-permute-start.1 = (f32[69,4,256]{2,1,0:T(4,128)S(1)}, f32[69,4,256]{2,1,0:T(4,128)S(1)}, u32[]{:S(2)}, u32[]{:S(2)}) collective-permute-start(f32[69,4,256]{2,1,0:T(4,128)S(1)} %get-tuple-element.25), channel_id=1, source_target_pairs={{0,15},{1,0},{2,1},{3,2},{4,3},{5,4},{6,5},{7,6},{8,7},{9,8},{10,9... | collective-permute-start | bytes 847880 | tf_op jit(solution)/shard_map/ppermute | solution.py:903
  18.9 18.1 %collective-permute-start.2 = (f32[69,4,256]{2,1,0:T(4,128)S(1)}, f32[69,4,256]{2,1,0:T(4,128)S(1)}, u32[]{:S(2)}, u32[]{:S(2)}) collective-permute-start(f32[69,4,256]{2,1,0:T(4,128)S(1)} %get-tuple-element.26), channel_id=1, source_target_pairs={{0,127},{1,112},{2,113},{3,114},{4,115},{5,116},{6,117},{7,118},{8... | collective-permute-start | bytes 847880 | tf_op jit(solution)/shard_map/ppermute | solution.py:903
  22.0 15.0 %collective-permute-start.3 = (f32[69,4,256]{2,1,0:T(4,128)S(1)}, f32[69,4,256]{2,1,0:T(4,128)S(1)}, u32[]{:S(2)}, u32[]{:S(2)}) collective-permute-start(f32[69,4,256]{2,1,0:T(4,128)S(1)} %get-tuple-element.27), channel_id=1, source_target_pairs={{0,113},{1,114},{2,115},{3,116},{4,117},{5,118},{6,119},{7,120},{8... | collective-permute-start | bytes 847880 | tf_op jit(solution)/shard_map/ppermute | solution.py:903
  36.9 0.7 copy-start.3
  37.0 0.7 copy-start.5
  37.0 0.7 copy-start.7
  61.6 21.3 %collective-permute-start.4 = (f32[69,4,256]{2,1,0:T(4,128)S(1)}, f32[69,4,256]{2,1,0:T(4,128)S(1)}, u32[]{:S(2)}, u32[]{:S(2)}) collective-permute-start(f32[69,4,256]{2,1,0:T(4,128)S(1)} %get-tuple-element.33), channel_id=1, source_target_pairs={{0,16},{1,17},{2,18},{3,19},{4,20},{5,21},{6,22},{7,23},{8,24},{9,... | collective-permute-start | bytes 847880 | tf_op jit(solution)/shard_map/ppermute | solution.py:903
  61.6 21.2 %collective-permute-start.5 = (f32[69,4,256]{2,1,0:T(4,128)S(1)}, f32[69,4,256]{2,1,0:T(4,128)S(1)}, u32[]{:S(2)}, u32[]{:S(2)}) collective-permute-start(f32[69,4,256]{2,1,0:T(4,128)S(1)} %get-tuple-element.34), channel_id=1, source_target_pairs={{0,1},{1,2},{2,3},{3,4},{4,5},{5,6},{6,7},{7,8},{8,9},{9,10},{10,1... | collective-permute-start | bytes 847880 | tf_op jit(solution)/shard_map/ppermute | solution.py:903
  61.8 21.1 %collective-permute-start.6 = (f32[69,4,256]{2,1,0:T(4,128)S(1)}, f32[69,4,256]{2,1,0:T(4,128)S(1)}, u32[]{:S(2)}, u32[]{:S(2)}) collective-permute-start(f32[69,4,256]{2,1,0:T(4,128)S(1)} %get-tuple-element.35), channel_id=1, source_target_pairs={{0,17},{1,18},{2,19},{3,20},{4,21},{5,22},{6,23},{7,24},{8,25},{9,... | collective-permute-start | bytes 847880 | tf_op jit(solution)/shard_map/ppermute | solution.py:903
  61.8 21.1 %collective-permute-start.7 = (f32[69,4,256]{2,1,0:T(4,128)S(1)}, f32[69,4,256]{2,1,0:T(4,128)S(1)}, u32[]{:S(2)}, u32[]{:S(2)}) collective-permute-start(f32[69,4,256]{2,1,0:T(4,128)S(1)} %get-tuple-element.36), channel_id=1, source_target_pairs={{0,31},{1,16},{2,17},{3,18},{4,19},{5,20},{6,21},{7,22},{8,23},{9,... | collective-permute-start | bytes 847880 | tf_op jit(solution)/shard_map/ppermute | solution.py:903

commit v4 on v3

--- a/solution.py
+++ b/solution.py
@@ -159,8 +159,8 @@
 
 def front_kernel(
     at_ref, counts_row, sent_leaves, sent_parents, counts_hbm, send_hbm, pos_hbm, mass_hbm,
-    own_ref, cells_ref, pcells_ref, pay0, pay1, pay2, pay3,
-    slab_ref, turned_ref, pos_ref, mass_ref, counts_ref, send_ref, sem,
+    own_ref, cells_ref, pcells_ref, pay0, pay1, pay2, pay3, turned_ref,
+    slab_ref, pos_ref, mass_ref, counts_ref, send_ref, sem,
 ):
     pays = (pay0, pay1, pay2, pay3)
     fetch_all(
@@ -171,25 +171,33 @@
     base_y = at_ref[1] * CY
     row4 = iota((4, LEAF), 0)
     lane = iota((1, LEAF), 1)
-
-    def one_leaf(c, _):
-        start = pl.multiple_of(c * LEAF, LEAF)
-        place = pos_ref[:, pl.ds(start, LEAF)]
-        mass = jnp.concatenate(
-            [mass_ref[pl.ds(2 * c, 1), :], mass_ref[pl.ds(2 * c + 1, 1), :]], 1
-        )
-        weight = jnp.where(lane < counts_ref[c], mass, 0.0)
-        centre_x = (base_x + c // (CY * CZ)).astype(f32) + 0.5
-        centre_y = (base_y + c // CZ % CY).astype(f32) + 0.5
-        centre_z = (c % CZ).astype(f32) + 0.5
-        centre = jnp.where(row4 == 1, centre_x, jnp.where(row4 == 2, centre_y, centre_z))
-        centre = jnp.where(row4 == 0, 0.0, centre)
-        slab = jnp.concatenate([weight, place], 0) - centre
-        own_ref[c] = slab
-        put_slab(slab_ref, c, slab)
-        return 0
-
-    lax.fori_loop(0, LEAVES, one_leaf, 0, unroll=8)
+    batch = 8
+
+    for x in range(CX):
+        for y in range(CY):
+            centre = jnp.where(row4 == 1, (base_x + x).astype(f32) + 0.5, 0.0)
+            centre = jnp.where(row4 == 2, (base_y + y).astype(f32) + 0.5, centre)
+
+            def some_leaves(step, _, x=x, y=y, centre=centre):
+                low = step * batch
+                first = (x * CY + y) * CZ + low
+                from_z = jnp.where(row4 == 3, low.astype(f32) + 0.5, centre)
+                for k in range(batch):
+                    c = first + k
+                    start = pl.multiple_of(c * LEAF, LEAF)
+                    place = pos_ref[:, pl.ds(start, LEAF)]
+                    mass = jnp.concatenate(
+                        [mass_ref[pl.ds(2 * c, 1), :], mass_ref[pl.ds(2 * c + 1, 1), :]], 1
+                    )
+                    weight = jnp.where(lane < counts_ref[c], mass, 0.0)
+                    slab = jnp.concatenate([weight, place], 0) - (
+                        from_z + jnp.where(row4 == 3, float(k), 0.0)
+                    )
+                    own_ref[c] = slab
+                    put_slab(slab_ref, c, slab)
+                return 0
+
+            lax.fori_loop(0, CZ // batch, some_leaves, 0)
 
     for comp in range(4):
         turned_ref[comp] = get_rows(slab_ref, comp).T
@@ -280,19 +288,18 @@
         name="front",
         out_shape=[
             shaped(LEAVES, 4, LEAF), shaped(40, LEAVES), shaped(40, 128),
-        ] + [shaped(PAY, 4, LEAF)] * 4,
+        ] + [shaped(PAY, 4, LEAF)] * 4 + [shaped(4, LEAF, LEAVES)],
         in_specs=[SM, VM, VM, VM, HBM, HBM, HBM, HBM],
-        out_specs=[VM] * 7,
+        out_specs=[VM] * 8,
         scratch_shapes=[
             pltpu.VMEM((LEAVES * 16, 128), f32),
-            pltpu.VMEM((4, LEAF, LEAVES), f32),
             pltpu.VMEM((3, LEAVES * LEAF), f32),
             pltpu.VMEM((LEAVES * 2, 128), f32),
             pltpu.SMEM((LEAVES,), jnp.int32),
             pltpu.SMEM((1, 4 * SLOTS), jnp.int32),
             pltpu.SemaphoreType.DMA((4,)),
         ],
-        compiler_params=pltpu.CompilerParams(**PARAMS),
+        compiler_params=pltpu.CompilerParams(vmem_limit_bytes=63 * 1024 * 1024),
     )(
         at, counts.reshape(1, LEAVES), send_leaves, send_parents, counts, send_leaves, positions,
         masses.reshape(-1, 128),
@@ -359,7 +366,8 @@
     return jnp.where(row == 0, 1.0, wide), slab[0:1]
 
 
-def self_kernel(own_ref, out_ref):
+def self_kernel(own_ref, *refs):
+    out_ref = refs[-1]
     apart = jnp.where(iota((LEAF, LEAF), 0) == iota((LEAF, LEAF), 1), 0.0, 1.0)
 
     def some_leaves(step, _):
@@ -375,30 +383,32 @@
             low = (cubes[k] - high[k].astype(f32)).astype(bf16)
             side = sources(points, weight)
             total = fold(dot_nn(side, high[k])) + fold(dot_nn(side[0:16], low))
-            out_ref[first + k] = finish(total, points)
+            value = finish(total, points)
+            out_ref[first + k] = value + refs[0][first + k] if len(refs) > 1 else value
         return 0
 
     lax.fori_loop(0, own_ref.shape[0] // WIDTH, some_leaves, 0)
 
 
-def self_part(own, first, count):
+def self_part(own, first, count, others=()):
     block = 32
+    spec = pl.BlockSpec((block, 4, LEAF), lambda i: (i + first // block, 0, 0))
     return pl.pallas_call(
         self_kernel,
         name="self_part",
         grid=(count // block,),
         out_shape=shaped(count, 4, LEAF),
-        in_specs=[pl.BlockSpec((block, 4, LEAF), lambda i: (i + first // block, 0, 0))],
+        in_specs=[spec] * (1 + len(others)),
         out_specs=pl.BlockSpec((block, 4, LEAF), lambda i: (i, 0, 0)),
         cost_estimate=pl.CostEstimate(
             flops=count * 40_000_000, bytes_accessed=count * 8192, transcendentals=0
         ),
         compiler_params=pltpu.CompilerParams(**PARAMS),
-    )(own)
+    )(own, *others)
 
 
 def near_kernel(
-    list_ref, own_ref, in0, in1, in2, in3, backs_ref,
+    list_ref, own_ref, in0, in1, in2, in3, backs_ref, self_ref,
     out_ref, pay0, pay1, pay2, pay3, table, total, shifts, sem, *held,
 ):
     pays = (pay0, pay1, pay2, pay3)
@@ -489,7 +499,13 @@
         out_ref[c] = finish(total[c], points)
         return 0
 
-    lax.fori_loop(0, LEAVES, finish_own, 0, unroll=8)
+    def finish_both(c, _):
+        points, _ = load_points(table[c])
+        out_ref[c] = finish(total[c], points) + self_ref[c]
+        return 0
+
+    lax.fori_loop(0, LEAVES // 2, finish_both, 0, unroll=8)
+    lax.fori_loop(LEAVES // 2, LEAVES, finish_own, 0, unroll=8)
     for q in range(4):
 
         def finish_other(k, _, q=q):
@@ -501,12 +517,12 @@
         put_block(pays[q], backs_ref[q])
 
 
-def near_part(ordered, own, incoming, backs):
+def near_part(ordered, own, incoming, backs, self0):
     return pl.pallas_call(
         near_kernel,
         name="near_part",
         out_shape=[shaped(LEAVES, 4, LEAF)] + [shaped(PAY, 4, LEAF)] * 4,
-        in_specs=[SM, HB, HB, HB, HB, HB, VM],
+        in_specs=[SM, HB, HB, HB, HB, HB, VM, VM],
         out_specs=[VM] * 5,
         scratch_shapes=[
             pltpu.VMEM((2 * LEAVES, 4, LEAF), f32),
@@ -518,7 +534,7 @@
             flops=NEAR * 80_000_000, bytes_accessed=4_000_000, transcendentals=0
         ),
         compiler_params=pltpu.CompilerParams(**PARAMS),
-    )(ordered, own, *incoming, backs)
+    )(ordered, own, *incoming, backs, self0)
 
 
 def sort_lists(code, group, out_ref):
@@ -762,25 +778,19 @@
 
 
 def last_kernel(
-    counts_ref, send_ref, sent_leaves, sent_parents, own_ref, near_ref, self0_ref, self1_ref, leaf_ref, par_ref,
-    in0, in1, in2, in3, out_ref, slab_ref, turned_ref, terms_ref, field_ref, near_sum,
+    counts_ref, send_ref, sent_leaves, sent_parents, turned_ref, near_hbm, self_hbm, leaf_ref,
+    par_ref, in0, in1, in2, in3, out_ref, slab_ref, terms_ref, field_ref, near_sum, sem,
 ):
     incoming = (in0, in1, in2, in3)
     lane128 = iota((1, 128), 1)
-
-    def copy_leaf(c, _):
-        put_slab(slab_ref, c, own_ref[c])
-        return 0
-
-    lax.fori_loop(0, LEAVES, copy_leaf, 0, unroll=8)
-
-    def both(c, _):
-        near_sum[c] = near_ref[c] + self0_ref[c]
-        near_sum[c + LEAVES // 2] = near_ref[c + LEAVES // 2] + self1_ref[c]
-        return 0
-
-    lax.fori_loop(0, LEAVES // 2, both, 0, unroll=8)
-
+    half = LEAVES // 2
+    fetch_all(
+        (
+            (near_hbm.at[pl.ds(0, half)], near_sum.at[pl.ds(0, half)]),
+            (self_hbm, near_sum.at[pl.ds(half, half)]),
+        ),
+        sem,
+    )
     leaf = leaf_ref[...]
     par = par_ref[...]
     for q in range(4):
@@ -791,12 +801,15 @@
         leaf = leaf + pick(block, leaf_hot, True)
         par = par + pick(block, parent_hot, True)
 
-        def arrive(k, _, q=q):
-            c = send_ref[0, q * SLOTS + k]
-            near_sum[c] = near_sum[c] + incoming[q][k]
+        def arrive(step, _, q=q):
+            first = step * 8
+            places = [send_ref[0, q * SLOTS + first + k] for k in range(8)]
+            values = [near_sum[c] + incoming[q][first + k] for k, c in enumerate(places)]
+            for c, value in zip(places, values):
+                near_sum[c] = value
             return 0
 
-        lax.fori_loop(0, SLOTS, arrive, 0, unroll=4)
+        lax.fori_loop(0, SLOTS // 8, arrive, 0)
     lane_parent = (iota((128, LEAVES), 1) // CZ % CY // 2) * (CZ // 2) + iota(
         (128, LEAVES), 1
     ) % CZ // 2
@@ -805,9 +818,6 @@
     terms = shift_terms(terms, parent_offsets())
     for n, alpha in enumerate(ALPHAS):
         terms_ref[n : n + 1, :] = leaf[n : n + 1, :] + terms[alpha]
-
-    for comp in range(1, 4):
-        turned_ref[comp] = get_rows(slab_ref, comp).T
 
     for half in range(2):
         lanes = slice(half * 128, half * 128 + 128)
@@ -863,23 +873,23 @@
     lax.fori_loop(0, LEAVES, write, 0, unroll=8)
 
 
-def last(counts, send_leaves, send_parents, own, near, self0, self1, leaf, par, arrived):
+def last(counts, send_leaves, send_parents, turned, near, self1, leaf, par, arrived):
     return pl.pallas_call(
         last_kernel,
         name="last",
         out_shape=shaped(4, LEAVES * LEAF),
-        in_specs=[SM, SM] + [VM] * 12,
+        in_specs=[SM, SM, VM, VM, VM, HB, HB] + [VM] * 6,
         out_specs=VM,
         scratch_shapes=[
             pltpu.VMEM((LEAVES * 16, 128), f32),
-            pltpu.VMEM((4, LEAF, LEAVES), f32),
             pltpu.VMEM((40, LEAVES), f32),
             pltpu.VMEM((4, LEAF, LEAVES), f32),
             pltpu.VMEM((LEAVES, 4, LEAF), f32),
+            pltpu.SemaphoreType.DMA((2,)),
         ],
         compiler_params=pltpu.CompilerParams(**PARAMS),
     )(
-        counts, send_leaves, send_leaves, send_parents, own, near, self0, self1, leaf, par, *arrived
+        counts, send_leaves, send_leaves, send_parents, turned, near, self1, leaf, par, *arrived
     )
 
 
@@ -911,7 +921,7 @@
     slab_at = lax.axis_index("slab")
     sub_at = lax.axis_index("sub")
     at = jnp.stack([slab_at, sub_at]).astype(jnp.int32)
-    own, cells, pcells, *outgoing = front(
+    own, cells, pcells, *outgoing, turned = front(
         at, leaf_counts, send_leaves, send_parents, positions, masses
     )
     incoming = [
@@ -923,13 +933,15 @@
     leaf, par, backs, ordered = far_part(
         image, far_pairs, parent_pairs, near_pairs, cells, pcells, incoming
     )
-    near, *returning = near_part(ordered, own, incoming, backs)
+    near, *returning = near_part(ordered, own, incoming, backs, self0)
     arrived = [
         moved_by(returning[q], slab_steps[q], sub_steps[q], slab_count, sub_count)
         for q in range(4)
     ]
-    self1 = self_part(own, LEAVES // 2, LEAVES // 2)
-    return last(leaf_counts, send_leaves, send_parents, own, near, self0, self1, leaf, par, arrived)
+    self1 = self_part(own, LEAVES // 2, LEAVES // 2, (near,))
+    return last(
+        leaf_counts, send_leaves, send_parents, turned, near, self1, leaf, par, arrived
+    )
 
 
 def solution(mesh):

time: 90.2 us -> 88.6 us (0.982)
  starting transfers between devices: 19.2 us -> 17.9 us
  local copies, waits for them, and re-layouts: 3.55 us -> 2.56 us
    pallas_call x1, Pallas kernels: 20.6 us -> 22 us  [near_part(): pl.pallas_call(near_kernel, name='near_part', out_shape=[shaped(LEAVES, 4...]
    ppermute x8, starting transfers between devices: 19.2 us -> 17.9 us  [moved_by(): return lax.ppermute(value, ('slab', 'sub'), pairs)]
    unnamed x16 -> x22, local copies, waits for them, and re-layouts: 3.55 us -> 2.56 us
    pallas_call x1, Pallas kernels: 7.03 us -> 6.12 us  [last(): pl.pallas_call(last_kernel, name='last', out_shape=shaped(4, LEAVES * LEA...]
where the time goes in v4:
time: 88.6 us; the launch traced here: 88.3 us
  Pallas kernels  66.8 us (75%)
  starting transfers between devices  17.9 us (20%)
  local copies, waits for them, and re-layouts  2.56 us (3%)
    pallas_call x2, Pallas kernels, self_part(): pl.pallas_call(self_kernel, name='self_part', grid=(count // block,), out...  27.5 us
    pallas_call x1, Pallas kernels, near_part(): pl.pallas_call(near_kernel, name='near_part', out_shape=[shaped(LEAVES, 4...  22 us
    ppermute x8, starting transfers between devices, moved_by(): return lax.ppermute(value, ('slab', 'sub'), pairs)  17.9 us
    pallas_call x1, Pallas kernels, front(): pl.pallas_call(front_kernel, name='front', out_shape=[shaped(LEAVES, 4, L...  7.9 us
    pallas_call x1, Pallas kernels, last(): pl.pallas_call(last_kernel, name='last', out_shape=shaped(4, LEAVES * LEA...  6.12 us
    pallas_call x1, Pallas kernels, far_part(): pl.pallas_call(far_kernel, name='far_part', out_shape=[shaped(40, LEAVES)...  3.27 us
    unnamed x22, local copies, waits for them, and re-layouts  2.56 us
  transfers between devices with their start and end apart: 8, of which 0 were waited for; matrix products, arithmetic and copies ran while one was open for 0% of the time, Pallas kernels for 31%

profile of v4, /device:TPU:1, one launch (start us, length us, event | category | flops | bytes accessed | tf_op | source)
XLA Modules:
  0.0 88.3 jit_solution(811306856635225914)
XLA Ops:
  0.0 0.7 pad_add_fusion.at_ref
  0.7 7.9 %front.1 = (f32[256,4,256]{2,1,0:T(4,128)}, f32[40,256]{1,0:T(8,128)}, f32[40,128]{1,0:T(8,128)}, f32[69,4,256]{2,1,0:T(4,128)}, f32[69,4,256]{2,1,0:T(4,128)}, ...) custom-call(s32[2]{0:T(128)} %pad_add_fusion.at_ref, s32[1,256]{1,0:T(1,128)} %bitcast.21, ...), custom_call_target="tpu_custom_call" | custom-call | tf_op jit(solution)/shard_map/front/pallas_call | solution.py:286
  8.6 1.4 %collective-permute-start = (f32[69,4,256]{2,1,0:T(4,128)}, f32[69,4,256]{2,1,0:T(4,128)S(1)}, u32[]{:S(2)}, u32[]{:S(2)}) collective-permute-start(f32[69,4,256]{2,1,0:T(4,128)} %get-tuple-element.25), channel_id=1, source_target_pairs={{0,112},{1,113},{2,114},{3,115},{4,116},{5,117},{6,118},{7,119},{8... | collective-permute-start | bytes 847880 | tf_op jit(solution)/shard_map/ppermute | solution.py:913
  10.0 6.0 %collective-permute-start.1 = (f32[69,4,256]{2,1,0:T(4,128)}, f32[69,4,256]{2,1,0:T(4,128)S(1)}, u32[]{:S(2)}, u32[]{:S(2)}) collective-permute-start(f32[69,4,256]{2,1,0:T(4,128)} %get-tuple-element.26), channel_id=1, source_target_pairs={{0,15},{1,0},{2,1},{3,2},{4,3},{5,4},{6,5},{7,6},{8,7},{9,8},{10,9... | collective-permute-start | bytes 847880 | tf_op jit(solution)/shard_map/ppermute | solution.py:913
  16.0 3.2 %collective-permute-start.2 = (f32[69,4,256]{2,1,0:T(4,128)}, f32[69,4,256]{2,1,0:T(4,128)S(1)}, u32[]{:S(2)}, u32[]{:S(2)}) collective-permute-start(f32[69,4,256]{2,1,0:T(4,128)} %get-tuple-element.27), channel_id=1, source_target_pairs={{0,127},{1,112},{2,113},{3,114},{4,115},{5,116},{6,117},{7,118},{8... | collective-permute-start | bytes 847880 | tf_op jit(solution)/shard_map/ppermute | solution.py:913
  19.2 1.0 %collective-permute-start.3 = (f32[69,4,256]{2,1,0:T(4,128)}, f32[69,4,256]{2,1,0:T(4,128)S(1)}, u32[]{:S(2)}, u32[]{:S(2)}) collective-permute-start(f32[69,4,256]{2,1,0:T(4,128)} %get-tuple-element.28), channel_id=1, source_target_pairs={{0,113},{1,114},{2,115},{3,116},{4,117},{5,118},{6,119},{7,120},{8... | collective-permute-start | bytes 847880 | tf_op jit(solution)/shard_map/ppermute | solution.py:913
  20.2 0.0 copy-start.9
  20.2 1.2 %copy-done.9 = f32[256,4,256]{2,1,0:T(4,128)S(1)} copy-done((f32[256,4,256]{2,1,0:T(4,128)S(1)}, f32[256,4,256]{2,1,0:T(4,128)}, u32[]{:S(2)}) %copy-start.9) | copy-done | bytes 1048600
  21.5 0.0 copy-start.1
  21.5 0.0 copy-start.8
  21.5 0.0 copy-start.10
  21.5 13.7 %self_part.2.self_ref = f32[128,4,256]{2,1,0:T(4,128)S(1)} custom-call(f32[256,4,256]{2,1,0:T(4,128)S(1)} %copy-done.9), custom_call_target="tpu_custom_call" | custom-call | flops 5120000000 | bytes 1048576 | tf_op jit(solution)/shard_map/self_part/pallas_call | solution.py:396
  35.2 0.0 copy-start.2
  35.2 0.1 add_bitcast_fusion
  35.3 0.0 copy-start.4
  35.3 0.1 add_bitcast_fusion.1
  35.4 0.0 collective-permute-done.in0
  35.4 0.0 collective-permute-done.1.in1
  35.4 0.0 collective-permute-done.2.in2
  35.4 0.0 collective-permute-done.3.in3
  35.4 0.0 copy-start.6
  35.5 0.0 copy-done.1
  35.5 0.0 copy-done.8
  35.5 0.5 copy-done.2
  35.9 0.1 copy-done.4
  36.0 0.1 copy-done.6
  36.1 3.3 %far_part.1 = (f32[40,256]{1,0:T(8,128)S(1)}, f32[40,128]{1,0:T(8,128)S(1)}, f32[4,40,128]{2,1,0:T(8,128)S(1)}, s32[2,384]{1,0:T(2,128)S(1)}) custom-call(f32[4,2]{1,0:T(4,128)S(1)} %add_convert_fusion.image_ref, s32[3,1,1024]{2,1,0:T(1,128)S(1)} %bitcast.20, s32[3,1,64]{2,1,0:T(1,128)S(1)} %bitcast.23, s32[3,1,256]{2,1,0:T(1,128)S(1)} %bitcast.22, ...), custom_call_target="tpu_custom_call" | custom-call | tf_op jit(solution)/shard_map/far_part/pallas_call | solution.py:727
  39.4 0.0 copy-done.10
  39.4 22.0 %near_part.1 = (f32[256,4,256]{2,1,0:T(4,128)S(1)}, f32[69,4,256]{2,1,0:T(4,128)S(1)}, f32[69,4,256]{2,1,0:T(4,128)S(1)}, f32[69,4,256]{2,1,0:T(4,128)S(1)}, f32[69,4,256]{2,1,0:T(4,128)S(1)}) custom-call(s32[2,384]{1,0:T(2,128)S(1)} %get-tuple-element.29.list_ref, f32[256,4,256]{2,1,0:T(4,128)S(1)} %copy-done.10, ...), custom_call_target="tpu_custom_call" | custom-call | flops 20480000000 | bytes 4000000 | tf_op jit(solution)/shard_map/near_part/pallas_call | solution.py:521
  61.4 1.4 %collective-permute-start.4 = (f32[69,4,256]{2,1,0:T(4,128)S(1)}, f32[69,4,256]{2,1,0:T(4,128)S(1)}, u32[]{:S(2)}, u32[]{:S(2)}) collective-permute-start(f32[69,4,256]{2,1,0:T(4,128)S(1)} %get-tuple-element.35), channel_id=1, source_target_pairs={{0,16},{1,17},{2,18},{3,19},{4,20},{5,21},{6,22},{7,23},{8,24},{9,... | collective-permute-start | bytes 847880 | tf_op jit(solution)/shard_map/ppermute | solution.py:913
  62.8 0.0 collective-permute-start.5
  62.8 0.0 collective-permute-start.6
  62.8 4.9 %collective-permute-start.7 = (f32[69,4,256]{2,1,0:T(4,128)S(1)}, f32[69,4,256]{2,1,0:T(4,128)S(1)}, u32[]{:S(2)}, u32[]{:S(2)}) collective-permute-start(f32[69,4,256]{2,1,0:T(4,128)S(1)} %get-tuple-element.38), channel_id=1, source_target_pairs={{0,31},{1,16},{2,17},{3,18},{4,19},{5,20},{6,21},{7,22},{8,23},{9,... | collective-permute-start | bytes 847880 | tf_op jit(solution)/shard_map/ppermute | solution.py:913
  67.7 0.0 copy-start
  67.7 0.0 copy-start.5
  67.7 13.8 %self_part.3.self_hbm = f32[128,4,256]{2,1,0:T(4,128)S(1)} custom-call(f32[256,4,256]{2,1,0:T(4,128)S(1)} %copy-done.10, f32[256,4,256]{2,1,0:T(4,128)S(1)} %get-tuple-element.32.refs_0_.near_hbm), custom_call_target="tpu_custom_call" | custom-call | flops 5120000000 | bytes 1048576 | tf_op jit(solution)/shard_map/self_part/pallas_call | solution.py:396
  81.5 0.0 collective-permute-done.4.in0
  81.5 0.0 collective-permute-done.5.in1
  81.5 0.0 collective-permute-done.6.in2
  81.5 0.0 collective-permute-done.7.in3
  81.5 0.0 copy-start.3
  81.6 0.0 copy-start.7
  81.6 0.0 copy-done
  81.6 0.0 copy-done.5
  81.6 0.6 copy-done.3
  82.2 0.0 copy-done.7
  82.2 6.1 %last.1 = f32[4,65536]{1,0:T(4,128)} custom-call(s32[256]{0:T(256)S(1)} %copy-done.5, s32[1,256]{1,0:T(1,128)S(1)} %copy-done.3, s32[1,256]{1,0:T(1,128)S(1)} %copy-done.3, s32[1,64]{1,0:T(1,128)S(1)} %copy-done.7, f32[4,256,256]{2,1,0:T(8,128)S(1)} %copy-done, f32[256,4,256]{2,1,0:T(4,128)S(1)} %get-tuple-element.32.refs_0_.near_hbm, ...), custom_call_target="tpu_custom_call" | custom-call | tf_op jit(solution)/shard_map/last/pallas_call | solution.py:877
  (1 shorter events, 0.0 us)
Async XLA Ops:
  8.6 26.8 %collective-permute-start = (f32[69,4,256]{2,1,0:T(4,128)}, f32[69,4,256]{2,1,0:T(4,128)S(1)}, u32[]{:S(2)}, u32[]{:S(2)}) collective-permute-start(f32[69,4,256]{2,1,0:T(4,128)} %get-tuple-element.25), channel_id=1, source_target_pairs={{0,112},{1,113},{2,114},{3,115},{4,116},{5,117},{6,118},{7,119},{8... | collective-permute-start | bytes 847880 | tf_op jit(solution)/shard_map/ppermute | solution.py:913
  10.0 25.4 %collective-permute-start.1 = (f32[69,4,256]{2,1,0:T(4,128)}, f32[69,4,256]{2,1,0:T(4,128)S(1)}, u32[]{:S(2)}, u32[]{:S(2)}) collective-permute-start(f32[69,4,256]{2,1,0:T(4,128)} %get-tuple-element.26), channel_id=1, source_target_pairs={{0,15},{1,0},{2,1},{3,2},{4,3},{5,4},{6,5},{7,6},{8,7},{9,8},{10,9... | collective-permute-start | bytes 847880 | tf_op jit(solution)/shard_map/ppermute | solution.py:913
  16.0 19.4 %collective-permute-start.2 = (f32[69,4,256]{2,1,0:T(4,128)}, f32[69,4,256]{2,1,0:T(4,128)S(1)}, u32[]{:S(2)}, u32[]{:S(2)}) collective-permute-start(f32[69,4,256]{2,1,0:T(4,128)} %get-tuple-element.27), channel_id=1, source_target_pairs={{0,127},{1,112},{2,113},{3,114},{4,115},{5,116},{6,117},{7,118},{8... | collective-permute-start | bytes 847880 | tf_op jit(solution)/shard_map/ppermute | solution.py:913
  19.2 16.2 %collective-permute-start.3 = (f32[69,4,256]{2,1,0:T(4,128)}, f32[69,4,256]{2,1,0:T(4,128)S(1)}, u32[]{:S(2)}, u32[]{:S(2)}) collective-permute-start(f32[69,4,256]{2,1,0:T(4,128)} %get-tuple-element.28), channel_id=1, source_target_pairs={{0,113},{1,114},{2,115},{3,116},{4,117},{5,118},{6,119},{7,120},{8... | collective-permute-start | bytes 847880 | tf_op jit(solution)/shard_map/ppermute | solution.py:913
  20.2 1.2 %copy-start.9 = (f32[256,4,256]{2,1,0:T(4,128)S(1)}, f32[256,4,256]{2,1,0:T(4,128)}, u32[]{:S(2)}) copy-start(f32[256,4,256]{2,1,0:T(4,128)} %get-tuple-element.30.own_ref) | copy-start | bytes 3145732
  21.5 14.0 %copy-start.1 = (f32[40,256]{1,0:T(8,128)S(1)}, f32[40,256]{1,0:T(8,128)}, u32[]{:S(2)}) copy-start(f32[40,256]{1,0:T(8,128)} %get-tuple-element.23.cells_ref) | copy-start | bytes 122884
  21.5 14.0 %copy-start.8 = (s32[1,3,64]{2,0,1:T(1,128)S(1)}, s32[1,3,64]{2,0,1:T(1,128)}, u32[]{:S(2)}) copy-start(s32[1,3,64]{2,0,1:T(1,128)} %param.15) | copy-start | bytes 2308
  21.5 17.9 %copy-start.10 = (f32[256,4,256]{2,1,0:T(4,128)S(1)}, f32[256,4,256]{2,1,0:T(4,128)}, u32[]{:S(2)}) copy-start(f32[256,4,256]{2,1,0:T(4,128)} %get-tuple-element.30.own_ref) | copy-start | bytes 3145732
  35.2 0.7 copy-start.2
  35.3 0.7 copy-start.4
  35.4 0.7 copy-start.6
  61.4 20.1 %collective-permute-start.4 = (f32[69,4,256]{2,1,0:T(4,128)S(1)}, f32[69,4,256]{2,1,0:T(4,128)S(1)}, u32[]{:S(2)}, u32[]{:S(2)}) collective-permute-start(f32[69,4,256]{2,1,0:T(4,128)S(1)} %get-tuple-element.35), channel_id=1, source_target_pairs={{0,16},{1,17},{2,18},{3,19},{4,20},{5,21},{6,22},{7,23},{8,24},{9,... | collective-permute-start | bytes 847880 | tf_op jit(solution)/shard_map/ppermute | solution.py:913
  62.8 18.7 %collective-permute-start.5 = (f32[69,4,256]{2,1,0:T(4,128)S(1)}, f32[69,4,256]{2,1,0:T(4,128)S(1)}, u32[]{:S(2)}, u32[]{:S(2)}) collective-permute-start(f32[69,4,256]{2,1,0:T(4,128)S(1)} %get-tuple-element.36), channel_id=1, source_target_pairs={{0,1},{1,2},{2,3},{3,4},{4,5},{5,6},{6,7},{7,8},{8,9},{9,10},{10,1... | collective-permute-start | bytes 847880 | tf_op jit(solution)/shard_map/ppermute | solution.py:913
  62.8 18.7 %collective-permute-start.6 = (f32[69,4,256]{2,1,0:T(4,128)S(1)}, f32[69,4,256]{2,1,0:T(4,128)S(1)}, u32[]{:S(2)}, u32[]{:S(2)}) collective-permute-start(f32[69,4,256]{2,1,0:T(4,128)S(1)} %get-tuple-element.37), channel_id=1, source_target_pairs={{0,17},{1,18},{2,19},{3,20},{4,21},{5,22},{6,23},{7,24},{8,25},{9,... | collective-permute-start | bytes 847880 | tf_op jit(solution)/shard_map/ppermute | solution.py:913
  62.8 18.7 %collective-permute-start.7 = (f32[69,4,256]{2,1,0:T(4,128)S(1)}, f32[69,4,256]{2,1,0:T(4,128)S(1)}, u32[]{:S(2)}, u32[]{:S(2)}) collective-permute-start(f32[69,4,256]{2,1,0:T(4,128)S(1)} %get-tuple-element.38), channel_id=1, source_target_pairs={{0,31},{1,16},{2,17},{3,18},{4,19},{5,20},{6,21},{7,22},{8,23},{9,... | collective-permute-start | bytes 847880 | tf_op jit(solution)/shard_map/ppermute | solution.py:913
  67.7 13.9 %copy-start = (f32[4,256,256]{2,1,0:T(8,128)S(1)}, f32[4,256,256]{2,1,0:T(8,128)}, u32[]{:S(2)}) copy-start(f32[4,256,256]{2,1,0:T(8,128)} %get-tuple-element.22.turned_ref) | copy-start | bytes 3145732
  67.7 13.9 %copy-start.5 = (s32[256]{0:T(256)S(1)}, s32[256]{0:T(256)}, u32[]{:S(2)}) copy-start(s32[256]{0:T(256)} %counts_ref.1) | copy-start | bytes 3076
  81.5 0.7 copy-start.3
  81.6 0.7 copy-start.7

commit v5 on v4

--- a/solution.py
+++ b/solution.py
@@ -1,3 +1,5 @@
+import functools
+
 import jax
 import jax.numpy as jnp
 from jax import lax
@@ -19,6 +21,7 @@
 PAY = SLOTS + 5
 SOFT = 0.0025
 WIDTH = 8
+SELF_WIDTH = 16
 CLASSES = (128, 192, 256)
 SORTED = 384
 slab_steps = (1, 0, 1, 1)
@@ -159,7 +162,7 @@
 
 def front_kernel(
     at_ref, counts_row, sent_leaves, sent_parents, counts_hbm, send_hbm, pos_hbm, mass_hbm,
-    own_ref, cells_ref, pcells_ref, pay0, pay1, pay2, pay3, turned_ref,
+    own_ref, cells_ref, pcells_ref, pay0, pay1, pay2, pay3, turned_ref, ordered_ref,
     slab_ref, pos_ref, mass_ref, counts_ref, send_ref, sem,
 ):
     pays = (pay0, pay1, pay2, pay3)
@@ -258,6 +261,10 @@
         block = pick(cells_ref[...], leaf_hot) + pick(pcells, parent_hot)
         put_block(pay, block)
 
+    counts = counts_row[...]
+    group = jnp.where(counts <= 128, 0, jnp.where(counts <= 192, 1, 2))
+    sort_lists(iota((1, LEAVES), 1).astype(f32) + 1.0, group, SELF_WIDTH, ordered_ref)
+
 
 def put_block(pay, block):
     for s in range(5):
@@ -288,9 +295,11 @@
         name="front",
         out_shape=[
             shaped(LEAVES, 4, LEAF), shaped(40, LEAVES), shaped(40, 128),
-        ] + [shaped(PAY, 4, LEAF)] * 4 + [shaped(4, LEAF, LEAVES)],
+        ] + [shaped(PAY, 4, LEAF)] * 4 + [
+            shaped(4, LEAF, LEAVES), jax.ShapeDtypeStruct((2, SORTED), jnp.int32),
+        ],
         in_specs=[SM, VM, VM, VM, HBM, HBM, HBM, HBM],
-        out_specs=[VM] * 8,
+        out_specs=[VM] * 9,
         scratch_shapes=[
             pltpu.VMEM((LEAVES * 16, 128), f32),
             pltpu.VMEM((3, LEAVES * LEAF), f32),
@@ -366,45 +375,71 @@
     return jnp.where(row == 0, 1.0, wide), slab[0:1]
 
 
-def self_kernel(own_ref, *refs):
-    out_ref = refs[-1]
-    apart = jnp.where(iota((LEAF, LEAF), 0) == iota((LEAF, LEAF), 1), 0.0, 1.0)
-
-    def some_leaves(step, _):
-        first = step * WIDTH
-        loaded = [load_points(own_ref[first + k]) for k in range(WIDTH)]
-        spaced = [squares(points, points) for points, _ in loaded]
+def self_kernel(part, list_ref, own_hbm, *refs):
+    before_ref = refs[0] if part else None
+    out_ref, own_ref, sem = refs[-3:]
+    copy = pltpu.make_async_copy(own_hbm, own_ref, sem.at[0])
+    copy.start()
+
+    def begin(c, _):
+        out_ref[c] = before_ref[c] if part else jnp.zeros((4, LEAF), f32)
+        return 0
+
+    lax.fori_loop(0, LEAVES, begin, 0, unroll=8)
+    copy.wait()
+
+    def some_leaves(step, rows, lanes):
+        places, loaded = [], []
+        for k in range(SELF_WIDTH):
+            code = list_ref[0, step * SELF_WIDTH + k]
+            leaf = jnp.maximum(code - 1, 0)
+            points, weight = load_points(own_ref[leaf])
+            places.append((leaf, jnp.where(code > 0, leaf, LEAVES)))
+            loaded.append((points[:, :rows], weight[:, :rows], points[:, :lanes]))
+        spaced = [squares(left, right) for left, _, right in loaded]
+        apart = jnp.where(iota((rows, lanes), 0) == iota((rows, lanes), 1), 0.0, 1.0)
         cubes = []
         for value in spaced:
             inverse = lax.rsqrt(value) * apart
             cubes.append(inverse * inverse * inverse)
         high = [cube.astype(bf16) for cube in cubes]
-        for k, (points, weight) in enumerate(loaded):
-            low = (cubes[k] - high[k].astype(f32)).astype(bf16)
-            side = sources(points, weight)
-            total = fold(dot_nn(side, high[k])) + fold(dot_nn(side[0:16], low))
-            value = finish(total, points)
-            out_ref[first + k] = value + refs[0][first + k] if len(refs) > 1 else value
-        return 0
-
-    lax.fori_loop(0, own_ref.shape[0] // WIDTH, some_leaves, 0)
-
-
-def self_part(own, first, count, others=()):
-    block = 32
-    spec = pl.BlockSpec((block, 4, LEAF), lambda i: (i + first // block, 0, 0))
+        done = []
+        for cube, top, (left, weight, right) in zip(cubes, high, loaded):
+            low = (cube - top.astype(f32)).astype(bf16)
+            side = sources(left, weight)
+            total = fold(dot_nn(side, top)) + fold(dot_nn(side[0:16], low))
+            done.append(finish(total, right))
+        for (leaf, place), value in zip(places, done):
+            if part:
+                value = value + before_ref[leaf, :, 0:lanes]
+            out_ref[place, :, 0:lanes] = value
+
+    for n, rows in enumerate(CLASSES):
+        first = list_ref[1, n]
+        end = list_ref[1, n + 1]
+        middle = (first + end + n % 2) >> 1
+        lanes = 128 if rows == 128 else LEAF
+
+        def body(step, _, rows=rows, lanes=lanes):
+            some_leaves(step, rows, lanes)
+            return 0
+
+        lax.fori_loop(middle if part else first, end if part else middle, body, 0)
+
+
+def self_part(part, ordered, own, before=()):
     return pl.pallas_call(
-        self_kernel,
+        functools.partial(self_kernel, part),
         name="self_part",
-        grid=(count // block,),
-        out_shape=shaped(count, 4, LEAF),
-        in_specs=[spec] * (1 + len(others)),
-        out_specs=pl.BlockSpec((block, 4, LEAF), lambda i: (i, 0, 0)),
+        out_shape=shaped(LEAVES + 8, 4, LEAF),
+        in_specs=[SM, HBM] + [VM] * len(before),
+        out_specs=VM,
+        scratch_shapes=[pltpu.VMEM((LEAVES, 4, LEAF), f32), pltpu.SemaphoreType.DMA((1,))],
         cost_estimate=pl.CostEstimate(
-            flops=count * 40_000_000, bytes_accessed=count * 8192, transcendentals=0
+            flops=LEAVES * 20_000_000, bytes_accessed=LEAVES * 8192, transcendentals=0
         ),
         compiler_params=pltpu.CompilerParams(**PARAMS),
-    )(own, *others)
+    )(ordered, own, *before)
 
 
 def near_kernel(
@@ -496,16 +531,10 @@
 
     def finish_own(c, _):
         points, _ = load_points(table[c])
-        out_ref[c] = finish(total[c], points)
-        return 0
-
-    def finish_both(c, _):
-        points, _ = load_points(table[c])
         out_ref[c] = finish(total[c], points) + self_ref[c]
         return 0
 
-    lax.fori_loop(0, LEAVES // 2, finish_both, 0, unroll=8)
-    lax.fori_loop(LEAVES // 2, LEAVES, finish_own, 0, unroll=8)
+    lax.fori_loop(0, LEAVES, finish_own, 0, unroll=8)
     for q in range(4):
 
         def finish_other(k, _, q=q):
@@ -537,7 +566,7 @@
     )(ordered, own, *incoming, backs, self0)
 
 
-def sort_lists(code, group, out_ref):
+def sort_lists(code, group, width, out_ref):
     count = code.shape[1]
     hot = jnp.where(iota((8, count), 0) == group, 1.0, 0.0)
     earlier = jnp.where(iota((count, count), 0) < iota((count, count), 1), 1.0, 0.0).astype(bf16)
@@ -548,8 +577,8 @@
     groups = jnp.zeros((1, 1), f32)
     ends = jnp.zeros((1, SORTED), f32)
     for n in range(len(CLASSES)):
-        place = place + hot[n : n + 1] * (before[n : n + 1] + groups * WIDTH)
-        groups = groups + jnp.floor((members[n : n + 1] + (WIDTH - 1)) * (1.0 / WIDTH))
+        place = place + hot[n : n + 1] * (before[n : n + 1] + groups * width)
+        groups = groups + jnp.floor((members[n : n + 1] + (width - 1)) * (1.0 / width))
         ends = jnp.where(lane == n + 1, groups, ends)
     place = jnp.where(group >= 0, place, -1.0).astype(jnp.int32)
     ordered = pick(jnp.broadcast_to(code, (8, count)), onehot_rows(SORTED, place), True)
@@ -715,7 +744,7 @@
     rows = jnp.where(swap, ids_b, ids_a)
     columns = jnp.where(swap, ids_a, ids_b)
     code = 1.0 + rows.astype(f32) + columns.astype(f32) * 512.0 + moved * 262144.0
-    sort_lists(jnp.where(ids_b >= 0, code, 0.0), group, ordered_ref)
+    sort_lists(jnp.where(ids_b >= 0, code, 0.0), group, WIDTH, ordered_ref)
 
     leaf_ref[...] = total[:, 0:LEAVES]
     par_ref[...] = total[:, LEAVES + 512 :]
@@ -778,19 +807,12 @@
 
 
 def last_kernel(
-    counts_ref, send_ref, sent_leaves, sent_parents, turned_ref, near_hbm, self_hbm, leaf_ref,
+    counts_ref, send_ref, sent_leaves, sent_parents, turned_ref, self_hbm, leaf_ref,
     par_ref, in0, in1, in2, in3, out_ref, slab_ref, terms_ref, field_ref, near_sum, sem,
 ):
     incoming = (in0, in1, in2, in3)
     lane128 = iota((1, 128), 1)
-    half = LEAVES // 2
-    fetch_all(
-        (
-            (near_hbm.at[pl.ds(0, half)], near_sum.at[pl.ds(0, half)]),
-            (self_hbm, near_sum.at[pl.ds(half, half)]),
-        ),
-        sem,
-    )
+    fetch_all(((self_hbm.at[pl.ds(0, LEAVES)], near_sum),), sem)
     leaf = leaf_ref[...]
     par = par_ref[...]
     for q in range(4):
@@ -873,23 +895,23 @@
     lax.fori_loop(0, LEAVES, write, 0, unroll=8)
 
 
-def last(counts, send_leaves, send_parents, turned, near, self1, leaf, par, arrived):
+def last(counts, send_leaves, send_parents, turned, near, leaf, par, arrived):
     return pl.pallas_call(
         last_kernel,
         name="last",
         out_shape=shaped(4, LEAVES * LEAF),
-        in_specs=[SM, SM, VM, VM, VM, HB, HB] + [VM] * 6,
+        in_specs=[SM, SM, VM, VM, VM, HB] + [VM] * 6,
         out_specs=VM,
         scratch_shapes=[
             pltpu.VMEM((LEAVES * 16, 128), f32),
             pltpu.VMEM((40, LEAVES), f32),
             pltpu.VMEM((4, LEAF, LEAVES), f32),
             pltpu.VMEM((LEAVES, 4, LEAF), f32),
-            pltpu.SemaphoreType.DMA((2,)),
+            pltpu.SemaphoreType.DMA((1,)),
         ],
         compiler_params=pltpu.CompilerParams(**PARAMS),
     )(
-        counts, send_leaves, send_leaves, send_parents, turned, near, self1, leaf, par, *arrived
+        counts, send_leaves, send_leaves, send_parents, turned, near, leaf, par, *arrived
     )
 
 
@@ -921,7 +943,7 @@
     slab_at = lax.axis_index("slab")
     sub_at = lax.axis_index("sub")
     at = jnp.stack([slab_at, sub_at]).astype(jnp.int32)
-    own, cells, pcells, *outgoing, turned = front(
+    own, cells, pcells, *outgoing, turned, leaf_order = front(
         at, leaf_counts, send_leaves, send_parents, positions, masses
     )
     incoming = [
@@ -929,7 +951,7 @@
         for q in range(4)
     ]
     image = image_shift(slab_at, sub_at, slab_count, sub_count)
-    self0 = self_part(own, 0, LEAVES // 2)
+    self0 = self_part(0, leaf_order, own)
     leaf, par, backs, ordered = far_part(
         image, far_pairs, parent_pairs, near_pairs, cells, pcells, incoming
     )
@@ -938,9 +960,9 @@
         moved_by(returning[q], slab_steps[q], sub_steps[q], slab_count, sub_count)
         for q in range(4)
     ]
-    self1 = self_part(own, LEAVES // 2, LEAVES // 2, (near,))
+    near = self_part(1, leaf_order, own, (near,))
     return last(
-        leaf_counts, send_leaves, send_parents, turned, near, self1, leaf, par, arrived
+        leaf_counts, send_leaves, send_parents, turned, near, leaf, par, arrived
     )
 
 

time: 88.6 us -> 83.3 us (0.940)
  Pallas kernels: 66.8 us -> 58.7 us
  starting transfers between devices: 17.9 us -> 19.7 us
    pallas_call x2, Pallas kernels: 27.5 us -> 21.1 us  [self_part(): pl.pallas_call(functools.partial(self_kernel, part), name='self_part', ou...]
    ppermute x8, starting transfers between devices: 17.9 us -> 19.7 us  [moved_by(): return lax.ppermute(value, ('slab', 'sub'), pairs)]
    pallas_call x1, Pallas kernels: 22 us -> 20.4 us  [near_part(): pl.pallas_call(near_kernel, name='near_part', out_shape=[shaped(LEAVES, 4...]
    unnamed x22 -> x24, local copies, waits for them, and re-layouts: 2.56 us -> 1.95 us
  transfers between devices with their start and end apart: 8 -> 8, of which waited for: 0 -> 1; matrix products, arithmetic and copies ran while one was open for 0% -> 0% of each run, Pallas kernels for 31% -> 26%
where the time goes in v5:
time: 83.3 us; the launch traced here: 82.3 us
  Pallas kernels  58.7 us (70%)
  starting transfers between devices  19.7 us (24%)
  local copies, waits for them, and re-layouts  1.95 us (2%)
  waiting for transfers between devices  0.86 us (1%)
    pallas_call x2, Pallas kernels, self_part(): pl.pallas_call(functools.partial(self_kernel, part), name='self_part', ou...  21.1 us
    pallas_call x1, Pallas kernels, near_part(): pl.pallas_call(near_kernel, name='near_part', out_shape=[shaped(LEAVES, 4...  20.4 us
    ppermute x8, starting transfers between devices, moved_by(): return lax.ppermute(value, ('slab', 'sub'), pairs)  19.7 us
    pallas_call x1, Pallas kernels, front(): pl.pallas_call(front_kernel, name='front', out_shape=[shaped(LEAVES, 4, L...  7.9 us
    pallas_call x1, Pallas kernels, last(): pl.pallas_call(last_kernel, name='last', out_shape=shaped(4, LEAVES * LEA...  6.11 us
    pallas_call x1, Pallas kernels, far_part(): pl.pallas_call(far_kernel, name='far_part', out_shape=[shaped(40, LEAVES)...  3.27 us
    unnamed x24, local copies, waits for them, and re-layouts  1.95 us
  transfers between devices with their start and end apart: 8, of which 1 were waited for; matrix products, arithmetic and copies ran while one was open for 0% of the time, Pallas kernels for 26%

profile of v5, /device:TPU:1, one launch (start us, length us, event | category | flops | bytes accessed | tf_op | source)
XLA Modules:
  0.0 82.3 jit_solution(17631775860358346448)
XLA Ops:
  0.0 0.6 pad_add_fusion.at_ref
  0.6 7.9 %front.1 = (f32[256,4,256]{2,1,0:T(4,128)}, f32[40,256]{1,0:T(8,128)}, f32[40,128]{1,0:T(8,128)}, f32[69,4,256]{2,1,0:T(4,128)}, f32[69,4,256]{2,1,0:T(4,128)}, ...) custom-call(s32[2]{0:T(128)} %pad_add_fusion.at_ref, ...), custom_call_target="tpu_custom_call" | custom-call | tf_op jit(solution)/shard_map/front/pallas_call | solution.py:293
  8.5 1.4 %collective-permute-start = (f32[69,4,256]{2,1,0:T(4,128)}, f32[69,4,256]{2,1,0:T(4,128)S(1)}, u32[]{:S(2)}, u32[]{:S(2)}) collective-permute-start(f32[69,4,256]{2,1,0:T(4,128)} %get-tuple-element.28), channel_id=1, source_target_pairs={{0,112},{1,113},{2,114},{3,115},{4,116},{5,117},{6,118},{7,119},{8... | collective-permute-start | bytes 847880 | tf_op jit(solution)/shard_map/ppermute | solution.py:935
  9.9 6.0 %collective-permute-start.1 = (f32[69,4,256]{2,1,0:T(4,128)}, f32[69,4,256]{2,1,0:T(4,128)S(1)}, u32[]{:S(2)}, u32[]{:S(2)}) collective-permute-start(f32[69,4,256]{2,1,0:T(4,128)} %get-tuple-element.29), channel_id=1, source_target_pairs={{0,15},{1,0},{2,1},{3,2},{4,3},{5,4},{6,5},{7,6},{8,7},{9,8},{10,9... | collective-permute-start | bytes 847880 | tf_op jit(solution)/shard_map/ppermute | solution.py:935
  16.0 3.2 %collective-permute-start.2 = (f32[69,4,256]{2,1,0:T(4,128)}, f32[69,4,256]{2,1,0:T(4,128)S(1)}, u32[]{:S(2)}, u32[]{:S(2)}) collective-permute-start(f32[69,4,256]{2,1,0:T(4,128)} %get-tuple-element.30), channel_id=1, source_target_pairs={{0,127},{1,112},{2,113},{3,114},{4,115},{5,116},{6,117},{7,118},{8... | collective-permute-start | bytes 847880 | tf_op jit(solution)/shard_map/ppermute | solution.py:935
  19.1 1.0 %collective-permute-start.3 = (f32[69,4,256]{2,1,0:T(4,128)}, f32[69,4,256]{2,1,0:T(4,128)S(1)}, u32[]{:S(2)}, u32[]{:S(2)}) collective-permute-start(f32[69,4,256]{2,1,0:T(4,128)} %get-tuple-element.31), channel_id=1, source_target_pairs={{0,113},{1,114},{2,115},{3,116},{4,117},{5,118},{6,119},{7,120},{8... | collective-permute-start | bytes 847880 | tf_op jit(solution)/shard_map/ppermute | solution.py:935
  20.2 0.0 copy-start.9
  20.2 1.2 %copy-done.9 = f32[256,4,256]{2,1,0:T(4,128)S(1)} copy-done((f32[256,4,256]{2,1,0:T(4,128)S(1)}, f32[256,4,256]{2,1,0:T(4,128)}, u32[]{:S(2)}) %copy-start.9) | copy-done | bytes 1048600
  21.4 0.0 copy-start.11
  21.4 0.7 copy-done.11
  22.1 0.0 copy-start.1
  22.1 0.0 copy-start.2
  22.1 0.0 copy-start.4
  22.1 0.0 copy-start.6
  22.1 0.0 copy-start.8
  22.1 11.2 %self_part.2.self_ref = f32[264,4,256]{2,1,0:T(4,128)S(1)} custom-call(s32[2,384]{1,0:T(2,128)S(1)} %copy-done.11, f32[256,4,256]{2,1,0:T(4,128)S(1)} %copy-done.9), custom_call_target="tpu_custom_call" | custom-call | flops 5120000000 | bytes 2097152 | tf_op jit(solution)/shard_map/self_part/pallas_call | solution.py:431
  33.3 0.0 copy-start.10
  33.3 0.1 add_bitcast_fusion
  33.4 0.1 add_bitcast_fusion.1
  33.5 0.0 collective-permute-done.in0
  33.5 0.0 collective-permute-done.1.in1
  33.5 0.0 collective-permute-done.2.in2
  33.5 0.0 collective-permute-done.3.in3
  33.5 0.0 copy-done.1
  33.5 0.0 copy-done.2
  33.5 0.0 copy-done.4
  33.5 0.0 copy-done.6
  33.5 0.0 copy-done.8
  33.5 3.3 %far_part.1 = (f32[40,256]{1,0:T(8,128)S(1)}, f32[40,128]{1,0:T(8,128)S(1)}, f32[4,40,128]{2,1,0:T(8,128)S(1)}, s32[2,384]{1,0:T(2,128)S(1)}) custom-call(f32[4,2]{1,0:T(4,128)S(1)} %add_convert_fusion.image_ref, s32[3,1,1024]{2,1,0:T(1,128)S(1)} %bitcast.20, s32[3,1,64]{2,1,0:T(1,128)S(1)} %bitcast.23, s32[3,1,256]{2,1,0:T(1,128)S(1)} %bitcast.22, ...), custom_call_target="tpu_custom_call" | custom-call | tf_op jit(solution)/shard_map/far_part/pallas_call | solution.py:756
  36.8 0.0 copy-done.10
  36.8 20.4 %near_part.1 = (f32[256,4,256]{2,1,0:T(4,128)S(1)}, f32[69,4,256]{2,1,0:T(4,128)S(1)}, f32[69,4,256]{2,1,0:T(4,128)S(1)}, f32[69,4,256]{2,1,0:T(4,128)S(1)}, f32[69,4,256]{2,1,0:T(4,128)S(1)}) custom-call(s32[2,384]{1,0:T(2,128)S(1)} %get-tuple-element.32.list_ref, f32[256,4,256]{2,1,0:T(4,128)S(1)} %copy-done.10, ...), custom_call_target="tpu_custom_call" | custom-call | flops 20480000000 | bytes 4000000 | tf_op jit(solution)/shard_map/near_part/pallas_call | solution.py:550
  57.2 3.2 %collective-permute-start.4 = (f32[69,4,256]{2,1,0:T(4,128)S(1)}, f32[69,4,256]{2,1,0:T(4,128)S(1)}, u32[]{:S(2)}, u32[]{:S(2)}) collective-permute-start(f32[69,4,256]{2,1,0:T(4,128)S(1)} %get-tuple-element.37), channel_id=1, source_target_pairs={{0,16},{1,17},{2,18},{3,19},{4,20},{5,21},{6,22},{7,23},{8,24},{9,... | collective-permute-start | bytes 847880 | tf_op jit(solution)/shard_map/ppermute | solution.py:935
  60.4 0.0 collective-permute-start.5
  60.4 0.0 collective-permute-start.6
  60.4 4.9 %collective-permute-start.7 = (f32[69,4,256]{2,1,0:T(4,128)S(1)}, f32[69,4,256]{2,1,0:T(4,128)S(1)}, u32[]{:S(2)}, u32[]{:S(2)}) collective-permute-start(f32[69,4,256]{2,1,0:T(4,128)S(1)} %get-tuple-element.40), channel_id=1, source_target_pairs={{0,31},{1,16},{2,17},{3,18},{4,19},{5,20},{6,21},{7,22},{8,23},{9,... | collective-permute-start | bytes 847880 | tf_op jit(solution)/shard_map/ppermute | solution.py:935
  65.2 0.0 copy-start
  65.2 0.0 copy-start.3
  65.2 0.0 copy-start.5
  65.2 9.9 %self_part.3.self_hbm = f32[264,4,256]{2,1,0:T(4,128)S(1)} custom-call(s32[2,384]{1,0:T(2,128)S(1)} %copy-done.11, f32[256,4,256]{2,1,0:T(4,128)S(1)} %copy-done.10, f32[256,4,256]{2,1,0:T(4,128)S(1)} %get-tuple-element.34.refs_0_), custom_call_target="tpu_custom_call" | custom-call | flops 5120000000 | bytes 2097152 | tf_op jit(solution)/shard_map/self_part/pallas_call | solution.py:431
  75.2 0.0 collective-permute-done.4.in0
  75.2 0.1 collective-permute-done.5.in1
  75.2 0.8 collective-permute-done.6.in2
  76.0 0.0 collective-permute-done.7.in3
  76.0 0.0 copy-done
  76.0 0.0 copy-done.3
  76.1 0.0 copy-done.5
  76.1 0.0 copy-done.7
  76.1 6.1 %last.1 = f32[4,65536]{1,0:T(4,128)} custom-call(s32[256]{0:T(256)S(1)} %copy-done.5, s32[1,256]{1,0:T(1,128)S(1)} %copy-done.3, s32[1,256]{1,0:T(1,128)S(1)} %copy-done.3, s32[1,64]{1,0:T(1,128)S(1)} %copy-done.7, f32[4,256,256]{2,1,0:T(8,128)S(1)} %copy-done, f32[264,4,256]{2,1,0:T(4,128)S(1)} %self_part.3.self_hbm, ...), custom_call_target="tpu_custom_call" | custom-call | tf_op jit(solution)/shard_map/last/pallas_call | solution.py:899
  (2 shorter events, 0.0 us)
Async XLA Ops:
  8.5 25.0 %collective-permute-start = (f32[69,4,256]{2,1,0:T(4,128)}, f32[69,4,256]{2,1,0:T(4,128)S(1)}, u32[]{:S(2)}, u32[]{:S(2)}) collective-permute-start(f32[69,4,256]{2,1,0:T(4,128)} %get-tuple-element.28), channel_id=1, source_target_pairs={{0,112},{1,113},{2,114},{3,115},{4,116},{5,117},{6,118},{7,119},{8... | collective-permute-start | bytes 847880 | tf_op jit(solution)/shard_map/ppermute | solution.py:935
  9.9 23.5 %collective-permute-start.1 = (f32[69,4,256]{2,1,0:T(4,128)}, f32[69,4,256]{2,1,0:T(4,128)S(1)}, u32[]{:S(2)}, u32[]{:S(2)}) collective-permute-start(f32[69,4,256]{2,1,0:T(4,128)} %get-tuple-element.29), channel_id=1, source_target_pairs={{0,15},{1,0},{2,1},{3,2},{4,3},{5,4},{6,5},{7,6},{8,7},{9,8},{10,9... | collective-permute-start | bytes 847880 | tf_op jit(solution)/shard_map/ppermute | solution.py:935
  16.0 17.5 %collective-permute-start.2 = (f32[69,4,256]{2,1,0:T(4,128)}, f32[69,4,256]{2,1,0:T(4,128)S(1)}, u32[]{:S(2)}, u32[]{:S(2)}) collective-permute-start(f32[69,4,256]{2,1,0:T(4,128)} %get-tuple-element.30), channel_id=1, source_target_pairs={{0,127},{1,112},{2,113},{3,114},{4,115},{5,116},{6,117},{7,118},{8... | collective-permute-start | bytes 847880 | tf_op jit(solution)/shard_map/ppermute | solution.py:935
  19.1 14.4 %collective-permute-start.3 = (f32[69,4,256]{2,1,0:T(4,128)}, f32[69,4,256]{2,1,0:T(4,128)S(1)}, u32[]{:S(2)}, u32[]{:S(2)}) collective-permute-start(f32[69,4,256]{2,1,0:T(4,128)} %get-tuple-element.31), channel_id=1, source_target_pairs={{0,113},{1,114},{2,115},{3,116},{4,117},{5,118},{6,119},{7,120},{8... | collective-permute-start | bytes 847880 | tf_op jit(solution)/shard_map/ppermute | solution.py:935
  20.2 1.2 %copy-start.9 = (f32[256,4,256]{2,1,0:T(4,128)S(1)}, f32[256,4,256]{2,1,0:T(4,128)}, u32[]{:S(2)}) copy-start(f32[256,4,256]{2,1,0:T(4,128)} %get-tuple-element.25.own_hbm.own_ref) | copy-start | bytes 3145732
  21.4 0.7 copy-start.11
  22.1 11.4 %copy-start.1 = (f32[40,256]{1,0:T(8,128)S(1)}, f32[40,256]{1,0:T(8,128)}, u32[]{:S(2)}) copy-start(f32[40,256]{1,0:T(8,128)} %get-tuple-element.26.cells_ref) | copy-start | bytes 122884
  22.1 11.4 %copy-start.2 = (f32[40,128]{1,0:T(8,128)S(1)}, f32[40,128]{1,0:T(8,128)}, u32[]{:S(2)}) copy-start(f32[40,128]{1,0:T(8,128)} %get-tuple-element.27.pcells_ref) | copy-start | bytes 61444
  22.1 11.4 %copy-start.4 = (s32[1,3,1024]{2,0,1:T(1,128)S(1)}, s32[1,3,1024]{2,0,1:T(1,128)}, u32[]{:S(2)}) copy-start(s32[1,3,1024]{2,0,1:T(1,128)} %param.14) | copy-start | bytes 36868
  22.1 11.4 %copy-start.6 = (s32[1,3,256]{2,0,1:T(1,128)S(1)}, s32[1,3,256]{2,0,1:T(1,128)}, u32[]{:S(2)}) copy-start(s32[1,3,256]{2,0,1:T(1,128)} %param.13) | copy-start | bytes 9220
  22.1 11.4 %copy-start.8 = (s32[1,3,64]{2,0,1:T(1,128)S(1)}, s32[1,3,64]{2,0,1:T(1,128)}, u32[]{:S(2)}) copy-start(s32[1,3,64]{2,0,1:T(1,128)} %param.15) | copy-start | bytes 2308
  33.3 3.6 %copy-start.10 = (f32[256,4,256]{2,1,0:T(4,128)S(1)}, f32[256,4,256]{2,1,0:T(4,128)}, u32[]{:S(2)}) copy-start(f32[256,4,256]{2,1,0:T(4,128)} %get-tuple-element.25.own_hbm.own_ref) | copy-start | bytes 3145732
  57.2 18.0 %collective-permute-start.4 = (f32[69,4,256]{2,1,0:T(4,128)S(1)}, f32[69,4,256]{2,1,0:T(4,128)S(1)}, u32[]{:S(2)}, u32[]{:S(2)}) collective-permute-start(f32[69,4,256]{2,1,0:T(4,128)S(1)} %get-tuple-element.37), channel_id=1, source_target_pairs={{0,16},{1,17},{2,18},{3,19},{4,20},{5,21},{6,22},{7,23},{8,24},{9,... | collective-permute-start | bytes 847880 | tf_op jit(solution)/shard_map/ppermute | solution.py:935
  60.4 14.9 %collective-permute-start.5 = (f32[69,4,256]{2,1,0:T(4,128)S(1)}, f32[69,4,256]{2,1,0:T(4,128)S(1)}, u32[]{:S(2)}, u32[]{:S(2)}) collective-permute-start(f32[69,4,256]{2,1,0:T(4,128)S(1)} %get-tuple-element.38), channel_id=1, source_target_pairs={{0,1},{1,2},{2,3},{3,4},{4,5},{5,6},{6,7},{7,8},{8,9},{9,10},{10,1... | collective-permute-start | bytes 847880 | tf_op jit(solution)/shard_map/ppermute | solution.py:935
  60.4 15.7 %collective-permute-start.6 = (f32[69,4,256]{2,1,0:T(4,128)S(1)}, f32[69,4,256]{2,1,0:T(4,128)S(1)}, u32[]{:S(2)}, u32[]{:S(2)}) collective-permute-start(f32[69,4,256]{2,1,0:T(4,128)S(1)} %get-tuple-element.39), channel_id=1, source_target_pairs={{0,17},{1,18},{2,19},{3,20},{4,21},{5,22},{6,23},{7,24},{8,25},{9,... | collective-permute-start | bytes 847880 | tf_op jit(solution)/shard_map/ppermute | solution.py:935
  60.4 15.7 %collective-permute-start.7 = (f32[69,4,256]{2,1,0:T(4,128)S(1)}, f32[69,4,256]{2,1,0:T(4,128)S(1)}, u32[]{:S(2)}, u32[]{:S(2)}) collective-permute-start(f32[69,4,256]{2,1,0:T(4,128)S(1)} %get-tuple-element.40), channel_id=1, source_target_pairs={{0,31},{1,16},{2,17},{3,18},{4,19},{5,20},{6,21},{7,22},{8,23},{9,... | collective-permute-start | bytes 847880 | tf_op jit(solution)/shard_map/ppermute | solution.py:935
  65.2 10.8 %copy-start = (f32[4,256,256]{2,1,0:T(8,128)S(1)}, f32[4,256,256]{2,1,0:T(8,128)}, u32[]{:S(2)}) copy-start(f32[4,256,256]{2,1,0:T(8,128)} %get-tuple-element.23.turned_ref) | copy-start | bytes 3145732
  65.2 10.8 %copy-start.3 = (s32[1,256]{1,0:T(1,128)S(1)}, s32[1,256]{1,0:T(1,128)}, u32[]{:S(2)}) copy-start(s32[1,256]{1,0:T(1,128)} %sent_leaves.3) | copy-start | bytes 3076
  65.2 10.8 %copy-start.5 = (s32[256]{0:T(256)S(1)}, s32[256]{0:T(256)}, u32[]{:S(2)}) copy-start(s32[256]{0:T(256)} %counts_ref.1) | copy-start | bytes 3076
  65.2 10.8 %copy-start.7 = (s32[1,64]{1,0:T(1,128)S(1)}, s32[1,64]{1,0:T(1,128)}, u32[]{:S(2)}) copy-start(s32[1,64]{1,0:T(1,128)} %sent_parents.3) | copy-start | bytes 772

commit v6 on v5

--- a/solution.py
+++ b/solution.py
@@ -161,15 +161,33 @@
 
 
 def front_kernel(
-    at_ref, counts_row, sent_leaves, sent_parents, counts_hbm, send_hbm, pos_hbm, mass_hbm,
+    at_ref, counts_hbm, row_hbm, send_hbm, parents_hbm, pos_hbm, mass_hbm,
     own_ref, cells_ref, pcells_ref, pay0, pay1, pay2, pay3, turned_ref, ordered_ref,
-    slab_ref, pos_ref, mass_ref, counts_ref, send_ref, sem,
+    slab_ref, pos_ref, mass_ref, counts_ref, send_ref, counts_row, sent_leaves, sent_parents, sem,
 ):
     pays = (pay0, pay1, pay2, pay3)
-    fetch_all(
-        ((counts_hbm, counts_ref), (send_hbm, send_ref), (pos_hbm, pos_ref), (mass_hbm, mass_ref)),
-        sem,
-    )
+    pieces = CX * CY
+    bodies = LEAVES * LEAF // pieces
+    places = [
+        pltpu.make_async_copy(
+            pos_hbm.at[:, pl.ds(n * bodies, bodies)], pos_ref.at[:, pl.ds(n * bodies, bodies)],
+            sem.at[6 + n],
+        )
+        for n in range(pieces)
+    ]
+    smaller = [
+        pltpu.make_async_copy(source, target, sem.at[n])
+        for n, (source, target) in enumerate(
+            (
+                (counts_hbm, counts_ref), (mass_hbm, mass_ref), (send_hbm, send_ref),
+                (row_hbm, counts_row), (send_hbm, sent_leaves), (parents_hbm, sent_parents),
+            )
+        )
+    ]
+    for copy in smaller[:2] + places + smaller[2:]:
+        copy.start()
+    for copy in smaller:
+        copy.wait()
     base_x = at_ref[0] * CX
     base_y = at_ref[1] * CY
     row4 = iota((4, LEAF), 0)
@@ -180,6 +198,7 @@
         for y in range(CY):
             centre = jnp.where(row4 == 1, (base_x + x).astype(f32) + 0.5, 0.0)
             centre = jnp.where(row4 == 2, (base_y + y).astype(f32) + 0.5, centre)
+            places[x * CY + y].wait()
 
             def some_leaves(step, _, x=x, y=y, centre=centre):
                 low = step * batch
@@ -282,7 +301,11 @@
 SM = pl.BlockSpec(memory_space=pltpu.SMEM)
 HB = pl.BlockSpec(memory_space=pl.ANY)
 HBM = pl.BlockSpec(memory_space=pltpu.MemorySpace.HBM)
-PARAMS = dict(vmem_limit_bytes=48 * 1024 * 1024)
+PARAMS = dict(vmem_limit_bytes=24 * 1024 * 1024)
+
+
+def in_hbm(value):
+    return pltpu.with_memory_space_constraint(value, pltpu.MemorySpace.HBM)
 
 
 def shaped(*shape):
@@ -298,7 +321,7 @@
         ] + [shaped(PAY, 4, LEAF)] * 4 + [
             shaped(4, LEAF, LEAVES), jax.ShapeDtypeStruct((2, SORTED), jnp.int32),
         ],
-        in_specs=[SM, VM, VM, VM, HBM, HBM, HBM, HBM],
+        in_specs=[SM] + [HBM] * 6,
         out_specs=[VM] * 9,
         scratch_shapes=[
             pltpu.VMEM((LEAVES * 16, 128), f32),
@@ -306,12 +329,21 @@
             pltpu.VMEM((LEAVES * 2, 128), f32),
             pltpu.SMEM((LEAVES,), jnp.int32),
             pltpu.SMEM((1, 4 * SLOTS), jnp.int32),
-            pltpu.SemaphoreType.DMA((4,)),
+            pltpu.VMEM((1, LEAVES), jnp.int32),
+            pltpu.VMEM((1, 4 * SLOTS), jnp.int32),
+            pltpu.VMEM((1, 4 * PSLOTS), jnp.int32),
+            pltpu.SemaphoreType.DMA((6 + CX * CY,)),
         ],
-        compiler_params=pltpu.CompilerParams(vmem_limit_bytes=63 * 1024 * 1024),
+        compiler_params=pltpu.CompilerParams(**PARAMS),
     )(
-        at, counts.reshape(1, LEAVES), send_leaves, send_parents, counts, send_leaves, positions,
-        masses.reshape(-1, 128),
+        at,
+        *map(
+            in_hbm,
+            (
+                counts, counts.reshape(1, LEAVES), send_leaves, send_parents, positions,
+                masses.reshape(-1, 128),
+            ),
+        ),
     )
 
 
@@ -361,12 +393,10 @@
 
 def finish(total, points):
     row = iota(points.shape, 0)
-    mass = total[0:1]
-    pushed = points * mass
-    terms = jnp.where(row == 0, SOFT * total, points * (pushed - 2.0 * total))
-    terms = jnp.where(row == 4, total, terms)
-    potential = jnp.sum(terms, 0, keepdims=True)
-    return jnp.where(row == 0, -potential, total - pushed)[0:4]
+    field = total - points * total[0:1]
+    sign = jnp.where(row == 0, -SOFT, jnp.where(row == 4, -1.0, 1.0))
+    terms = jnp.where(row == 4, total, points * (field + total)) * sign
+    return jnp.where(row == 0, jnp.sum(terms, 0, keepdims=True), field)[0:4]
 
 
 def load_points(slab):
@@ -376,25 +406,38 @@
 
 
 def self_kernel(part, list_ref, own_hbm, *refs):
-    before_ref = refs[0] if part else None
-    out_ref, own_ref, sem = refs[-3:]
-    copy = pltpu.make_async_copy(own_hbm, own_ref, sem.at[0])
-    copy.start()
-
-    def begin(c, _):
-        out_ref[c] = before_ref[c] if part else jnp.zeros((4, LEAF), f32)
-        return 0
-
-    lax.fori_loop(0, LEAVES, begin, 0, unroll=8)
-    copy.wait()
+    if part:
+        before_hbm, out_ref, own_ref, before_ref, sem = refs
+        moves = ((own_hbm, own_ref), (before_hbm, before_ref))
+    else:
+        out_ref, own_ref, sem = refs
+        moves = ((own_hbm, own_ref),)
+    copies = [
+        pltpu.make_async_copy(source, target, sem.at[n])
+        for n, (source, target) in enumerate(moves)
+    ]
+    for copy in copies:
+        copy.start()
+    if not part:
+
+        def begin(c, _):
+            out_ref[c] = jnp.zeros((8, LEAF), f32)
+            return 0
+
+        lax.fori_loop(0, LEAVES, begin, 0, unroll=8)
+    for copy in copies:
+        copy.wait()
+
+    def place_of(step, k):
+        code = list_ref[0, step * SELF_WIDTH + k]
+        leaf = jnp.maximum(code - 1, 0)
+        return leaf, jnp.where(code > 0, leaf, LEAVES)
 
     def some_leaves(step, rows, lanes):
-        places, loaded = [], []
-        for k in range(SELF_WIDTH):
-            code = list_ref[0, step * SELF_WIDTH + k]
-            leaf = jnp.maximum(code - 1, 0)
+        places = [place_of(step, k) for k in range(SELF_WIDTH)]
+        loaded = []
+        for leaf, _ in places:
             points, weight = load_points(own_ref[leaf])
-            places.append((leaf, jnp.where(code > 0, leaf, LEAVES)))
             loaded.append((points[:, :rows], weight[:, :rows], points[:, :lanes]))
         spaced = [squares(left, right) for left, _, right in loaded]
         apart = jnp.where(iota((rows, lanes), 0) == iota((rows, lanes), 1), 0.0, 1.0)
@@ -404,15 +447,21 @@
             cubes.append(inverse * inverse * inverse)
         high = [cube.astype(bf16) for cube in cubes]
         done = []
-        for cube, top, (left, weight, right) in zip(cubes, high, loaded):
+        for cube, top, (left, weight, right), (leaf, _) in zip(cubes, high, loaded, places):
             low = (cube - top.astype(f32)).astype(bf16)
             side = sources(left, weight)
-            total = fold(dot_nn(side, top)) + fold(dot_nn(side[0:16], low))
-            done.append(finish(total, right))
-        for (leaf, place), value in zip(places, done):
+            value = fold(dot_nn(side, top)) + fold(dot_nn(side[0:16], low))
             if part:
-                value = value + before_ref[leaf, :, 0:lanes]
+                value = finish(value + before_ref[leaf, :, 0:lanes], right)
+            done.append(value)
+        for (_, place), value in zip(places, done):
             out_ref[place, :, 0:lanes] = value
+
+    def finish_some(step):
+        places = [place_of(step, k) for k in range(SELF_WIDTH)]
+        done = [finish(before_ref[leaf], load_points(own_ref[leaf])[0]) for leaf, _ in places]
+        for (_, place), value in zip(places, done):
+            out_ref[place] = value
 
     for n, rows in enumerate(CLASSES):
         first = list_ref[1, n]
@@ -425,16 +474,25 @@
             return 0
 
         lax.fori_loop(middle if part else first, end if part else middle, body, 0)
-
-
-def self_part(part, ordered, own, before=()):
+        if part:
+
+            def rest(step, _):
+                finish_some(step)
+                return 0
+
+            lax.fori_loop(first, middle, rest, 0)
+
+
+def self_part(part, ordered, own, *before):
     return pl.pallas_call(
         functools.partial(self_kernel, part),
         name="self_part",
-        out_shape=shaped(LEAVES + 8, 4, LEAF),
-        in_specs=[SM, HBM] + [VM] * len(before),
+        out_shape=shaped(LEAVES + 8, 4 if part else 8, LEAF),
+        in_specs=[SM, HB] + [HB] * part,
         out_specs=VM,
-        scratch_shapes=[pltpu.VMEM((LEAVES, 4, LEAF), f32), pltpu.SemaphoreType.DMA((1,))],
+        scratch_shapes=[pltpu.VMEM((LEAVES, 4, LEAF), f32)]
+        + [pltpu.VMEM((LEAVES, 8, LEAF), f32)] * part
+        + [pltpu.SemaphoreType.DMA((2,))],
         cost_estimate=pl.CostEstimate(
             flops=LEAVES * 20_000_000, bytes_accessed=LEAVES * 8192, transcendentals=0
         ),
@@ -447,7 +505,10 @@
     out_ref, pay0, pay1, pay2, pay3, table, total, shifts, sem, *held,
 ):
     pays = (pay0, pay1, pay2, pay3)
-    copies = [pltpu.make_async_copy(own_ref, table.at[pl.ds(0, LEAVES)], sem.at[0])]
+    copies = [
+        pltpu.make_async_copy(own_ref, table.at[pl.ds(0, LEAVES)], sem.at[0]),
+        pltpu.make_async_copy(self_ref.at[pl.ds(0, LEAVES)], total.at[pl.ds(0, LEAVES)], sem.at[5]),
+    ]
     for q, part in enumerate((in0, in1, in2, in3)):
         copies.append(
             pltpu.make_async_copy(
@@ -463,7 +524,7 @@
         total[c] = jnp.zeros((8, LEAF), f32)
         return 0
 
-    lax.fori_loop(0, 2 * LEAVES + 8, clear, 0, unroll=8)
+    lax.fori_loop(LEAVES, 2 * LEAVES + 8, clear, 0, unroll=8)
     row = iota((8, 128), 0)
     for code in range(27):
         step = (code % 3 - 1, code // 3 % 3 - 1, code // 9 - 1)
@@ -529,12 +590,8 @@
             lax.fori_loop(first, end - 1, advance, 0)
             settle([products(end - 1, k, rows) for k in range(WIDTH)], rows)
 
-    def finish_own(c, _):
-        points, _ = load_points(table[c])
-        out_ref[c] = finish(total[c], points) + self_ref[c]
-        return 0
-
-    lax.fori_loop(0, LEAVES, finish_own, 0, unroll=8)
+    store = pltpu.make_async_copy(total.at[pl.ds(0, LEAVES)], out_ref, sem.at[6])
+    store.start()
     for q in range(4):
 
         def finish_other(k, _, q=q):
@@ -544,20 +601,21 @@
 
         lax.fori_loop(0, SLOTS, finish_other, 0, unroll=8)
         put_block(pays[q], backs_ref[q])
+    store.wait()
 
 
 def near_part(ordered, own, incoming, backs, self0):
     return pl.pallas_call(
         near_kernel,
         name="near_part",
-        out_shape=[shaped(LEAVES, 4, LEAF)] + [shaped(PAY, 4, LEAF)] * 4,
-        in_specs=[SM, HB, HB, HB, HB, HB, VM, VM],
-        out_specs=[VM] * 5,
+        out_shape=[shaped(LEAVES, 8, LEAF)] + [shaped(PAY, 4, LEAF)] * 4,
+        in_specs=[SM, HB, HB, HB, HB, HB, VM, HB],
+        out_specs=[HB] + [VM] * 4,
         scratch_shapes=[
             pltpu.VMEM((2 * LEAVES, 4, LEAF), f32),
             pltpu.VMEM((2 * LEAVES + 8, 8, LEAF), f32),
             pltpu.VMEM((27, 8, 128), f32),
-            pltpu.SemaphoreType.DMA((5,)),
+            pltpu.SemaphoreType.DMA((7,)),
         ] + [pltpu.VMEM((LEAF, LEAF), bf16)] * WIDTH,
         cost_estimate=pl.CostEstimate(
             flops=NEAR * 80_000_000, bytes_accessed=4_000_000, transcendentals=0
@@ -960,7 +1018,7 @@
         moved_by(returning[q], slab_steps[q], sub_steps[q], slab_count, sub_count)
         for q in range(4)
     ]
-    near = self_part(1, leaf_order, own, (near,))
+    near = self_part(1, leaf_order, own, near)
     return last(
         leaf_counts, send_leaves, send_parents, turned, near, leaf, par, arrived
     )

time: 83.3 us -> 78.1 us (0.938)
  Pallas kernels: 58.7 us -> 54.6 us
  local copies, waits for them, and re-layouts: 1.95 us -> 0.02 us
  starting transfers between devices: 19.7 us -> 20.8 us
  waiting for transfers between devices: 0.86 us -> 1.96 us
    pallas_call x1, Pallas kernels: 20.4 us -> 17.1 us  [near_part(): pl.pallas_call(near_kernel, name='near_part', out_shape=[shaped(LEAVES, 8...]
    unnamed x24 -> x12, local copies, waits for them, and re-layouts: 1.95 us -> 0.02 us
    ppermute x8, starting transfers between devices: 19.7 us -> 20.8 us  [moved_by(): return lax.ppermute(value, ('slab', 'sub'), pairs)]
    ppermute x8, waiting for transfers between devices: 0.86 us -> 1.96 us  [moved_by(): return lax.ppermute(value, ('slab', 'sub'), pairs)]
    pallas_call x1, Pallas kernels: 7.9 us -> 6.89 us  [front(): pl.pallas_call(front_kernel, name='front', out_shape=[shaped(LEAVES, 4, L...]
  transfers between devices with their start and end apart: 8 -> 8, of which waited for: 1 -> 1; matrix products, arithmetic and copies ran while one was open for 0% -> 0% of each run, Pallas kernels for 26% -> 27%
where the time goes in v6:
time: 78.1 us; the launch traced here: 77.9 us
  Pallas kernels  54.6 us (70%)
  starting transfers between devices  20.8 us (27%)
  waiting for transfers between devices  1.96 us (3%)
    pallas_call x2, Pallas kernels, self_part(): pl.pallas_call(functools.partial(self_kernel, part), name='self_part', ou...  21.2 us
    ppermute x8, starting transfers between devices, moved_by(): return lax.ppermute(value, ('slab', 'sub'), pairs)  20.8 us
    pallas_call x1, Pallas kernels, near_part(): pl.pallas_call(near_kernel, name='near_part', out_shape=[shaped(LEAVES, 8...  17.1 us
    pallas_call x1, Pallas kernels, front(): pl.pallas_call(front_kernel, name='front', out_shape=[shaped(LEAVES, 4, L...  6.89 us
    pallas_call x1, Pallas kernels, last(): pl.pallas_call(last_kernel, name='last', out_shape=shaped(4, LEAVES * LEA...  6.09 us
    pallas_call x1, Pallas kernels, far_part(): pl.pallas_call(far_kernel, name='far_part', out_shape=[shaped(40, LEAVES)...  3.27 us
    ppermute x8, waiting for transfers between devices, moved_by(): return lax.ppermute(value, ('slab', 'sub'), pairs)  1.96 us
  transfers between devices with their start and end apart: 8, of which 1 were waited for; matrix products, arithmetic and copies ran while one was open for 0% of the time, Pallas kernels for 27%

profile of v6, /device:TPU:1, one launch (start us, length us, event | category | flops | bytes accessed | tf_op | source)
XLA Modules:
  0.0 77.9 jit_solution(17320997655475813158)
XLA Ops:
  0.0 0.1 pad_add_fusion.at_ref
  0.1 6.9 %front.1 = (f32[256,4,256]{2,1,0:T(4,128)S(1)}, f32[40,256]{1,0:T(8,128)S(1)}, f32[40,128]{1,0:T(8,128)S(1)}, f32[69,4,256]{2,1,0:T(4,128)}, f32[69,4,256]{2,1,0...) custom-call(s32[2]{0:T(128)S(1)} %pad_add_fusion.at_ref, ...), custom_call_target="tpu_custom_call" | custom-call | tf_op jit(solution)/shard_map/front/pallas_call | solution.py:316
  7.0 1.4 %collective-permute-start = (f32[69,4,256]{2,1,0:T(4,128)}, f32[69,4,256]{2,1,0:T(4,128)S(1)}, u32[]{:S(2)}, u32[]{:S(2)}) collective-permute-start(f32[69,4,256]{2,1,0:T(4,128)} %get-tuple-element.28), channel_id=1, source_target_pairs={{0,112},{1,113},{2,114},{3,115},{4,116},{5,117},{6,118},{7,119},{8... | collective-permute-start | bytes 847880 | tf_op jit(solution)/shard_map/ppermute | solution.py:993
  8.4 6.0 %collective-permute-start.1 = (f32[69,4,256]{2,1,0:T(4,128)}, f32[69,4,256]{2,1,0:T(4,128)S(1)}, u32[]{:S(2)}, u32[]{:S(2)}) collective-permute-start(f32[69,4,256]{2,1,0:T(4,128)} %get-tuple-element.29), channel_id=1, source_target_pairs={{0,15},{1,0},{2,1},{3,2},{4,3},{5,4},{6,5},{7,6},{8,7},{9,8},{10,9... | collective-permute-start | bytes 847880 | tf_op jit(solution)/shard_map/ppermute | solution.py:993
  14.5 3.2 %collective-permute-start.2 = (f32[69,4,256]{2,1,0:T(4,128)}, f32[69,4,256]{2,1,0:T(4,128)S(1)}, u32[]{:S(2)}, u32[]{:S(2)}) collective-permute-start(f32[69,4,256]{2,1,0:T(4,128)} %get-tuple-element.30), channel_id=1, source_target_pairs={{0,127},{1,112},{2,113},{3,114},{4,115},{5,116},{6,117},{7,118},{8... | collective-permute-start | bytes 847880 | tf_op jit(solution)/shard_map/ppermute | solution.py:993
  17.6 1.0 %collective-permute-start.3 = (f32[69,4,256]{2,1,0:T(4,128)}, f32[69,4,256]{2,1,0:T(4,128)S(1)}, u32[]{:S(2)}, u32[]{:S(2)}) collective-permute-start(f32[69,4,256]{2,1,0:T(4,128)} %get-tuple-element.31), channel_id=1, source_target_pairs={{0,113},{1,114},{2,115},{3,116},{4,117},{5,118},{6,119},{7,120},{8... | collective-permute-start | bytes 847880 | tf_op jit(solution)/shard_map/ppermute | solution.py:993
  18.6 0.0 copy-start
  18.6 0.0 copy-start.3
  18.6 0.0 copy-start.5
  18.6 9.3 %self_part.2.self_ref = f32[264,8,256]{2,1,0:T(8,128)S(1)} custom-call(s32[2,384]{1,0:T(2,128)S(1)} %get-tuple-element.24.list_ref, f32[256,4,256]{2,1,0:T(4,128)S(1)} %get-tuple-element.25.own_hbm.own_ref), custom_call_target="tpu_custom_call" | custom-call | flops 5120000000 | bytes 2097152 | tf_op jit(solution)/shard_map/self_part/pallas_call | solution.py:487
  28.0 0.1 add_bitcast_fusion
  28.1 0.1 add_bitcast_fusion.1
  28.1 0.0 collective-permute-done.in0
  28.2 0.0 collective-permute-done.1.in1
  28.2 0.0 collective-permute-done.2.in2
  28.2 1.9 %collective-permute-done.3.in3 = f32[69,4,256]{2,1,0:T(4,128)S(1)} collective-permute-done((f32[69,4,256]{2,1,0:T(4,128)}, f32[69,4,256]{2,1,0:T(4,128)S(1)}, u32[]{:S(2)}, u32[]{:S(2)}) %collective-permute-start.3) | collective-permute-done | bytes 282656 | tf_op jit(solution)/shard_map/ppermute | solution.py:993
  30.1 0.0 copy-done
  30.1 0.0 copy-done.3
  30.1 0.0 copy-done.5
  30.1 3.3 %far_part.1 = (f32[40,256]{1,0:T(8,128)S(1)}, f32[40,128]{1,0:T(8,128)S(1)}, f32[4,40,128]{2,1,0:T(8,128)S(1)}, s32[2,384]{1,0:T(2,128)S(1)}) custom-call(f32[4,2]{1,0:T(4,128)S(1)} %add_convert_fusion.image_ref, s32[3,1,1024]{2,1,0:T(1,128)S(1)} %bitcast.20, s32[3,1,64]{2,1,0:T(1,128)S(1)} %bitcast.23, s32[3,1,256]{2,1,0:T(1,128)S(1)} %bitcast.22, ...), custom_call_target="tpu_custom_call" | custom-call | tf_op jit(solution)/shard_map/far_part/pallas_call | solution.py:814
  33.4 17.1 %near_part.1 = (f32[256,8,256]{2,1,0:T(8,128)S(1)}, f32[69,4,256]{2,1,0:T(4,128)S(1)}, f32[69,4,256]{2,1,0:T(4,128)S(1)}, f32[69,4,256]{2,1,0:T(4,128)S(1)}, f32[69,4,256]{2,1,0:T(4,128)S(1)}) custom-call(s32[2,384]{1,0:T(2,128)S(1)} %get-tuple-element.32.list_ref, f32[256,4,256]{2,1,0:T(4,128)S(1)} %get-tuple-element.25.own_hbm.own_ref, ...), custom_call_target="tpu_custom_call" | custom-call | flops 20480000000 | bytes 4000000 | tf_op jit(solution)/shard_map/near_part/pallas_call | solution.py:608
  50.5 0.0 collective-permute-start.4
  50.5 0.1 collective-permute-start.5
  50.6 2.0 %collective-permute-start.6 = (f32[69,4,256]{2,1,0:T(4,128)S(1)}, f32[69,4,256]{2,1,0:T(4,128)S(1)}, u32[]{:S(2)}, u32[]{:S(2)}) collective-permute-start(f32[69,4,256]{2,1,0:T(4,128)S(1)} %get-tuple-element.39), channel_id=1, source_target_pairs={{0,17},{1,18},{2,19},{3,20},{4,21},{5,22},{6,23},{7,24},{8,25},{9,... | collective-permute-start | bytes 847880 | tf_op jit(solution)/shard_map/ppermute | solution.py:993
  52.6 7.1 %collective-permute-start.7 = (f32[69,4,256]{2,1,0:T(4,128)S(1)}, f32[69,4,256]{2,1,0:T(4,128)S(1)}, u32[]{:S(2)}, u32[]{:S(2)}) collective-permute-start(f32[69,4,256]{2,1,0:T(4,128)S(1)} %get-tuple-element.40), channel_id=1, source_target_pairs={{0,31},{1,16},{2,17},{3,18},{4,19},{5,20},{6,21},{7,22},{8,23},{9,... | collective-permute-start | bytes 847880 | tf_op jit(solution)/shard_map/ppermute | solution.py:993
  59.7 0.0 copy-start.1
  59.7 0.0 copy-start.2
  59.7 0.0 copy-start.4
  59.7 11.9 %self_part.3.self_hbm = f32[264,4,256]{2,1,0:T(4,128)S(1)} custom-call(s32[2,384]{1,0:T(2,128)S(1)} %get-tuple-element.24.list_ref, f32[256,4,256]{2,1,0:T(4,128)S(1)} %get-tuple-element.25.own_hbm.own_ref, f32[256,8,256]{2,1,0:T(8,128)S(1)} %get-tuple-element.34.refs_0_), custom_call_target="tpu_custom_call" | custom-call | flops 5120000000 | bytes 2097152 | tf_op jit(solution)/shard_map/self_part/pallas_call | solution.py:487
  71.6 0.0 collective-permute-done.4.in0
  71.6 0.0 collective-permute-done.5.in1
  71.6 0.0 collective-permute-done.6.in2
  71.6 0.0 collective-permute-done.7.in3
  71.7 0.0 copy-done.1
  71.7 0.0 copy-done.2
  71.7 0.0 copy-done.4
  71.7 6.1 %last.1 = f32[4,65536]{1,0:T(4,128)} custom-call(s32[256]{0:T(256)S(1)} %copy-done.1, s32[1,256]{1,0:T(1,128)S(1)} %copy-done.2, s32[1,256]{1,0:T(1,128)S(1)} %copy-done.2, s32[1,64]{1,0:T(1,128)S(1)} %copy-done.4, f32[4,256,256]{2,1,0:T(8,128)S(1)} %get-tuple-element.23.turned_ref, f32[264,4,256]{2,1,0:T(4,128)S(1)} %self_part.3.self_hbm, ...), custom_call_target="tpu_custom_call" | custom-call | tf_op jit(solution)/shard_map/last/pallas_call | solution.py:957
  (1 shorter events, 0.0 us)
Async XLA Ops:
  7.0 21.2 %collective-permute-start = (f32[69,4,256]{2,1,0:T(4,128)}, f32[69,4,256]{2,1,0:T(4,128)S(1)}, u32[]{:S(2)}, u32[]{:S(2)}) collective-permute-start(f32[69,4,256]{2,1,0:T(4,128)} %get-tuple-element.28), channel_id=1, source_target_pairs={{0,112},{1,113},{2,114},{3,115},{4,116},{5,117},{6,118},{7,119},{8... | collective-permute-start | bytes 847880 | tf_op jit(solution)/shard_map/ppermute | solution.py:993
  8.4 19.7 %collective-permute-start.1 = (f32[69,4,256]{2,1,0:T(4,128)}, f32[69,4,256]{2,1,0:T(4,128)S(1)}, u32[]{:S(2)}, u32[]{:S(2)}) collective-permute-start(f32[69,4,256]{2,1,0:T(4,128)} %get-tuple-element.29), channel_id=1, source_target_pairs={{0,15},{1,0},{2,1},{3,2},{4,3},{5,4},{6,5},{7,6},{8,7},{9,8},{10,9... | collective-permute-start | bytes 847880 | tf_op jit(solution)/shard_map/ppermute | solution.py:993
  14.5 13.7 %collective-permute-start.2 = (f32[69,4,256]{2,1,0:T(4,128)}, f32[69,4,256]{2,1,0:T(4,128)S(1)}, u32[]{:S(2)}, u32[]{:S(2)}) collective-permute-start(f32[69,4,256]{2,1,0:T(4,128)} %get-tuple-element.30), channel_id=1, source_target_pairs={{0,127},{1,112},{2,113},{3,114},{4,115},{5,116},{6,117},{7,118},{8... | collective-permute-start | bytes 847880 | tf_op jit(solution)/shard_map/ppermute | solution.py:993
  17.6 12.5 %collective-permute-start.3 = (f32[69,4,256]{2,1,0:T(4,128)}, f32[69,4,256]{2,1,0:T(4,128)S(1)}, u32[]{:S(2)}, u32[]{:S(2)}) collective-permute-start(f32[69,4,256]{2,1,0:T(4,128)} %get-tuple-element.31), channel_id=1, source_target_pairs={{0,113},{1,114},{2,115},{3,116},{4,117},{5,118},{6,119},{7,120},{8... | collective-permute-start | bytes 847880 | tf_op jit(solution)/shard_map/ppermute | solution.py:993
  18.6 11.5 %copy-start = (s32[1,3,1024]{2,0,1:T(1,128)S(1)}, s32[1,3,1024]{2,0,1:T(1,128)}, u32[]{:S(2)}) copy-start(s32[1,3,1024]{2,0,1:T(1,128)} %param.14) | copy-start | bytes 36868
  18.6 11.5 %copy-start.3 = (s32[1,3,256]{2,0,1:T(1,128)S(1)}, s32[1,3,256]{2,0,1:T(1,128)}, u32[]{:S(2)}) copy-start(s32[1,3,256]{2,0,1:T(1,128)} %param.13) | copy-start | bytes 9220
  18.6 11.5 %copy-start.5 = (s32[1,3,64]{2,0,1:T(1,128)S(1)}, s32[1,3,64]{2,0,1:T(1,128)}, u32[]{:S(2)}) copy-start(s32[1,3,64]{2,0,1:T(1,128)} %param.15) | copy-start | bytes 2308
  50.5 21.1 %collective-permute-start.4 = (f32[69,4,256]{2,1,0:T(4,128)S(1)}, f32[69,4,256]{2,1,0:T(4,128)S(1)}, u32[]{:S(2)}, u32[]{:S(2)}) collective-permute-start(f32[69,4,256]{2,1,0:T(4,128)S(1)} %get-tuple-element.37), channel_id=1, source_target_pairs={{0,16},{1,17},{2,18},{3,19},{4,20},{5,21},{6,22},{7,23},{8,24},{9,... | collective-permute-start | bytes 847880 | tf_op jit(solution)/shard_map/ppermute | solution.py:993
  50.5 21.1 %collective-permute-start.5 = (f32[69,4,256]{2,1,0:T(4,128)S(1)}, f32[69,4,256]{2,1,0:T(4,128)S(1)}, u32[]{:S(2)}, u32[]{:S(2)}) collective-permute-start(f32[69,4,256]{2,1,0:T(4,128)S(1)} %get-tuple-element.38), channel_id=1, source_target_pairs={{0,1},{1,2},{2,3},{3,4},{4,5},{5,6},{6,7},{7,8},{8,9},{9,10},{10,1... | collective-permute-start | bytes 847880 | tf_op jit(solution)/shard_map/ppermute | solution.py:993
  50.6 21.0 %collective-permute-start.6 = (f32[69,4,256]{2,1,0:T(4,128)S(1)}, f32[69,4,256]{2,1,0:T(4,128)S(1)}, u32[]{:S(2)}, u32[]{:S(2)}) collective-permute-start(f32[69,4,256]{2,1,0:T(4,128)S(1)} %get-tuple-element.39), channel_id=1, source_target_pairs={{0,17},{1,18},{2,19},{3,20},{4,21},{5,22},{6,23},{7,24},{8,25},{9,... | collective-permute-start | bytes 847880 | tf_op jit(solution)/shard_map/ppermute | solution.py:993
  52.6 19.0 %collective-permute-start.7 = (f32[69,4,256]{2,1,0:T(4,128)S(1)}, f32[69,4,256]{2,1,0:T(4,128)S(1)}, u32[]{:S(2)}, u32[]{:S(2)}) collective-permute-start(f32[69,4,256]{2,1,0:T(4,128)S(1)} %get-tuple-element.40), channel_id=1, source_target_pairs={{0,31},{1,16},{2,17},{3,18},{4,19},{5,20},{6,21},{7,22},{8,23},{9,... | collective-permute-start | bytes 847880 | tf_op jit(solution)/shard_map/ppermute | solution.py:993
  59.7 12.0 %copy-start.1 = (s32[256]{0:T(256)S(1)}, s32[256]{0:T(256)}, u32[]{:S(2)}) copy-start(s32[256]{0:T(256)} %counts_ref.1) | copy-start | bytes 3076
  59.7 12.0 %copy-start.2 = (s32[1,256]{1,0:T(1,128)S(1)}, s32[1,256]{1,0:T(1,128)}, u32[]{:S(2)}) copy-start(s32[1,256]{1,0:T(1,128)} %sent_leaves.1) | copy-start | bytes 3076
  59.7 12.0 %copy-start.4 = (s32[1,64]{1,0:T(1,128)S(1)}, s32[1,64]{1,0:T(1,128)}, u32[]{:S(2)}) copy-start(s32[1,64]{1,0:T(1,128)} %sent_parents.1) | copy-start | bytes 772
